TPU v7x, 512 devices: a whole 4x8x8 slice. The times are simulated.
512 devices in a mesh: segment: 8 (over z), owner: 64 (over y, x, core).
Axes of the slice: x: 4, y: 8, z: 8, core: 2. Of those that a mesh axis runs over, the one named last changes fastest.
Arguments:
- layer_input_rows: bfloat16 [8, 8192, 4096], P('segment', 'owner'), may hold values from -6 to 6
- output_gradient: bfloat16 [8, 8192, 1024], P('segment', 'owner'), may hold values from -6 to 6
- tenant: int32 [8192, 1], P('owner'), may hold values from 0 to 63; in each aligned block of 128 rows (0 to 127, 128 to 255, ...) at most 4 rows name the same one
- adapter_owner_index: int32 [64], replicated, may hold values from 0 to 63, each once
- adapter_down_weight: bfloat16 [8, 64, 4096, 64], P('segment', 'owner'), may hold values from -0.09375 to 0.09375
- adapter_up_weight: bfloat16 [8, 64, 64, 1024], P('segment', 'owner'), may hold values from -0.1875 to 0.1875
Outputs:
- passed_grad: bfloat16 [8, 8192, 4096], P('segment', 'owner')
- grad_down: float32 [8, 64, 4096, 64], P('segment', 'owner')
- grad_up: float32 [8, 64, 64, 1024], P('segment', 'owner')
Inputs may be any that keep to these rules, and one draw needn't show every extreme that they name: `tenant`: within the rows of one device no adapter is named by more than 4 rows, and in every draw some device names some adapter exactly 4 times. `adapter_owner_index`: each owner index appears once.
All inputs are finite; a program needn't handle non-finite values.
Results may differ from a plain program's by a relative error of at most 0.014.
Values may be sent and summed in bfloat16 or wider, within the bound.
No kernel may reach another device: no remote copies, remote signals or barrier semaphores. Data moves between devices by JAX's collectives and lax.ppermute only.
A program may use at most 128 MiB of HBM per device.

v0:
```python
import jax
import jax.numpy as jnp
from jax import lax
from jax.sharding import PartitionSpec as P

adapter_scale = 2.0


def prefix(x, axis, join, neutral):
    count = lax.axis_size(axis)
    place = lax.axis_index(axis)
    ahead = count - 1 - place
    gathered = lax.all_gather(x.astype(jnp.bfloat16), axis)
    state = jnp.zeros_like(x) + jnp.asarray(neutral, x.dtype)

    def one(step, state):
        source = count - 1 - step
        return join(state, lax.dynamic_index_in_dim(gathered, source, 0, False).astype(x.dtype))

    return lax.fori_loop(0, ahead, one, state)


def local(
    layer_input_rows,
    output_gradient,
    tenant,
    adapter_owner_index,
    adapter_down_weight,
    adapter_up_weight,
):
    inputs = layer_input_rows[0]
    gradient_list = output_gradient[0]
    tok_rows = inputs.shape[0]
    width = inputs.shape[1]
    out_width = gradient_list.shape[1]
    owners = lax.axis_size("owner")
    capacity = 2 * tok_rows // owners
    highest_precision = lax.Precision.HIGHEST
    ids = tenant[:, 0]
    adapter_count = adapter_owner_index.shape[0]
    matched = ids[:, None] == jnp.arange(adapter_count, dtype=jnp.int32)[None, :]
    dest = jnp.sum(jnp.where(matched, adapter_owner_index[None, :], 0), axis=1)
    onehot = (dest[:, None] == jnp.arange(owners, dtype=jnp.int32)[None, :]).astype(jnp.int32)
    rank = jnp.sum((jnp.cumsum(onehot, axis=0) - 1) * onehot, axis=1)
    target = dest * capacity + rank
    placing = (jnp.arange(owners * capacity, dtype=jnp.int32)[:, None] == target[None, :]).astype(
        jnp.bfloat16
    )
    send_inputs = jnp.dot(placing, inputs, preferred_element_type=jnp.float32).astype(jnp.bfloat16)
    send_grads = jnp.dot(placing, gradient_list, preferred_element_type=jnp.float32).astype(
        jnp.bfloat16
    )
    send_inputs = send_inputs.reshape(owners, capacity, width)
    send_grads = send_grads.reshape(owners, capacity, out_width)
    down_factor = adapter_down_weight[0, 0]
    up_factor = adapter_up_weight[0, 0]
    recv_inputs, recv_grads = (
        lax.all_to_all(send_inputs, "owner", split_axis=0, concat_axis=0, tiled=True),
        lax.all_to_all(send_grads, "owner", split_axis=0, concat_axis=0, tiled=True),
    )
    rows_in = recv_inputs.reshape(owners * capacity, width)
    rows_grad = recv_grads.reshape(owners * capacity, out_width)
    scale_weight = adapter_scale * jnp.einsum(
        "rm,km->rk", rows_grad, up_factor, preferred_element_type=jnp.float32
    )
    partial_terms = jnp.einsum(
        "rk,dk->rd",
        scale_weight,
        down_factor,
        precision=highest_precision,
        preferred_element_type=jnp.float32,
    )
    partial_terms = partial_terms.astype(jnp.bfloat16).reshape(owners, capacity, width)
    returned = lax.all_to_all(partial_terms, "owner", split_axis=0, concat_axis=0, tiled=True)
    projected_rows = jnp.dot(rows_in, down_factor, preferred_element_type=jnp.float32)
    grad_down = jnp.einsum(
        "rd,rk->dk",
        rows_in,
        scale_weight,
        precision=highest_precision,
        preferred_element_type=jnp.float32,
    )
    grad_up = jnp.einsum(
        "rk,rm->km",
        projected_rows,
        rows_grad,
        precision=highest_precision,
        preferred_element_type=jnp.float32,
    )
    own_term = jnp.einsum(
        "sr,sd->rd",
        placing,
        returned.reshape(owners * capacity, width),
        preferred_element_type=jnp.float32,
    )

    def combine(earlier, later):
        return earlier + later

    above = prefix(own_term, "segment", combine, jnp.zeros_like(own_term))
    passed = (above + own_term).astype(jnp.bfloat16)
    return (passed[None], grad_down[None, None], grad_up[None, None])


def solution(mesh):
    return jax.shard_map(
        local,
        mesh=mesh,
        in_specs=(
            P("segment", "owner", None),
            P("segment", "owner", None),
            P("owner", None),
            P(),
            P("segment", "owner", None, None),
            P("segment", "owner", None, None),
        ),
        out_specs=(
            P("segment", "owner", None),
            P("segment", "owner", None, None),
            P("segment", "owner", None, None),
        ),
        check_vma=False,
    )
```

profile of v0, /device:TPU:1, one launch (start us, length us, event | category | flops | bytes accessed | tf_op | source)
XLA Modules:
  0.0 226.6 jit_solution(12534766949074843805)
XLA Ops:
  7.2 0.9 select_reduce_fusion.1
  8.3 0.2 reduce_window_sum.11
  8.4 0.2 select_reduce_fusion
  8.6 1.2 convolution_convert_fusion.2
  9.9 0.2 reshape.34
  10.1 29.1 %all_to_all.15 = bf16[64,4,1024]{2,1,0:T(4,128)(2,1)S(1)} all-to-all(bf16[64,4,1024]{2,1,0:T(4,128)(2,1)S(1)} %reshape.34), channel_id=1, replica_groups=mesh['segment'=8,'owner'=64] {'owner'}, dimensions={0} | all-to-all | bytes 1048576 | tf_op jit(solution)/shard_map/all_to_all | solution.py:59
  39.4 0.3 convolution_multiply_fusion
  39.6 0.5 copy-done.1
  40.1 3.2 %convolution_convert_fusion.1 = bf16[256,4096]{1,0:T(8,128)(2,1)} fusion(f32[256,64]{0,1:T(8,128)S(1)} %convolution_multiply_fusion, bf16[1,1,4096,64]{2,3,1,0:T(8,128)(2,1)S(1)} %copy-done.3), kind=kOutput, calls=%fused_computation.2 | convolution fusion | flops 806354944 | bytes 2686976 | tf_op jit(solution)/shard_map/rk,dk->rd/dot_general | solution.py:66
  43.3 2.7 %reshape.36 = bf16[64,4,4096]{2,1,0:T(4,128)(2,1)S(1)} reshape(bf16[256,4096]{1,0:T(8,128)(2,1)} %convolution_convert_fusion.1) | data formatting | bytes 4194304 | tf_op jit(solution)/shard_map/reshape | solution.py:73
  46.1 55.3 %all_to_all.16 = bf16[64,4,4096]{2,1,0:T(4,128)(2,1)} all-to-all(bf16[64,4,4096]{2,1,0:T(4,128)(2,1)S(1)} %reshape.36), channel_id=1, replica_groups=mesh['segment'=8,'owner'=64] {'owner'}, dimensions={0} | all-to-all | bytes 4194304 | tf_op jit(solution)/shard_map/all_to_all | solution.py:74
  101.4 2.5 %reshape.37 = bf16[256,4096]{1,0:T(8,128)(2,1)S(1)} reshape(bf16[64,4,4096]{2,1,0:T(4,128)(2,1)} %all_to_all.16) | data formatting | bytes 4194304 | tf_op jit(solution)/shard_map/reshape | solution.py:93
  103.9 2.2 fusion.12
  106.1 0.7 convolution_convert_fusion
  106.8 2.2 reshape.38
  109.0 7.2 %all-to-all-start.2 = ((bf16[64,4,4096]{2,1,0:T(4,128)(2,1)}), bf16[64,4,4096]{2,1,0:T(4,128)(2,1)}, u32[]{:S(2)}, u32[]{:S(2)}) async-start(bf16[64,4,4096]{2,1,0:T(4,128)(2,1)} %reshape.38), calls=%async_computation.2 | async-start | bytes 4194304 | tf_op jit(solution)/shard_map/all_to_all | solution.py:58
  116.2 49.6 %all-to-all-done.2 = bf16[64,4,4096]{2,1,0:T(4,128)(2,1)} async-done(((bf16[64,4,4096]{2,1,0:T(4,128)(2,1)}), bf16[64,4,4096]{2,1,0:T(4,128)(2,1)}, u32[]{:S(2)}, u32[]{:S(2)}) %all-to-all-start.2) | async-done | bytes 2097184 | tf_op jit(solution)/shard_map/all_to_all | solution.py:58
  165.8 2.6 %reshape.39 = bf16[256,4096]{1,0:T(8,128)(2,1)S(1)} reshape(bf16[64,4,4096]{2,1,0:T(4,128)(2,1)} %all-to-all-done.2) | data formatting | bytes 4194304 | tf_op jit(solution)/shard_map/reshape | solution.py:61
  168.4 1.8 fusion.2
  170.2 1.1 convolution_bitcast_fusion.1
  171.4 2.2 convolution_bitcast_fusion
  173.5 31.2 %all-gather.3.cloned.1.call-done = bf16[1024,4096]{1,0:T(8,128)(2,1)} async-done(((bf16[128,4096]{1,0:T(8,128)(2,1)}), bf16[1024,4096]{1,0:T(8,128)(2,1)}) %all-gather.3.cloned.1.call-update) | async-done | bytes 8388624 | tf_op jit(solution)/shard_map/all_gather | solution.py:13
  204.7 0.2 broadcast_in_dim.30
  204.9 12.1 %while.12 = (s32[]{:T(128)}, f32[128,4096]{1,0:T(8,128)S(1)}, s32[]{:T(128)}, bf16[8,128,4096]{2,1,0:T(8,128)(2,1)}, s32[]{:T(128)}, /*index=5*/s32[]{:T(128)}, s32[]{:T(128)}, s32[]{:T(128)}) while((s32[]{:T(128)}, f32[128,4096]{1,0:T(8,128)S(1)}, s32[]{:T(128)}, bf16[8,128,4096]{2,1,0:T(8,128)(2,1)}, s32[]{:T(128)}, /*index=5*/s32[]{:T(128)}, ...), condition=%wide.region_4.5_spmd, body=%wide.region_3.4_spmd.sunk | while | flops 1048582 | bytes 5243015 | solution.py:20
  204.9 1.7 convert_add_fusion.2
  206.7 1.7 convert_add_fusion.2
  208.4 1.7 convert_add_fusion.2
  210.1 1.7 convert_add_fusion.2
  211.8 1.7 convert_add_fusion.2
  213.5 1.7 convert_add_fusion.2
  215.3 1.7 convert_add_fusion.2
  217.0 2.8 %fusion = bf16[1,128,4096]{2,1,0:T(8,128)(2,1)} fusion(f32[128,4096]{1,0:T(8,128)S(1)} %get-tuple-element.59, f32[128,4096]{1,0:T(8,128)} %get-tuple-element.69), kind=kLoop, calls=%fused_computation.8 | loop fusion | flops 1048576 | bytes 5242880 | tf_op jit(solution)/shard_map/broadcast_in_dim | solution.py:102
  (14 shorter events, 0.3 us)
Async XLA Ops:
  7.2 98.9 %copy-start = (bf16[1,128,4096]{2,1,0:T(8,128)(2,1)S(1)}, bf16[1,128,4096]{2,1,0:T(8,128)(2,1)}, u32[]{:S(2)}) copy-start(bf16[1,128,4096]{2,1,0:T(8,128)(2,1)} %param.8) | copy-start | bytes 3145732
  7.2 197.5 %all-gather.3.cloned.1.call-start = ((), (), s32[]{:S(2)}) async-start(), calls=%async_computation.3 | async-start | bytes 9437184 | tf_op jit(solution)/shard_map/all_gather | solution.py:13
  8.2 31.2 %copy-start.4 = (bf16[1,1,64,1024]{3,2,1,0:T(8,128)(2,1)S(1)}, bf16[1,1,64,1024]{3,2,1,0:T(8,128)(2,1)}, u32[]{:S(2)}) copy-start(bf16[1,1,64,1024]{3,2,1,0:T(8,128)(2,1)} %param.13) | copy-start | bytes 393220
  9.9 30.3 %copy-start.3 = (bf16[1,1,4096,64]{2,3,1,0:T(8,128)(2,1)S(1)}, bf16[1,1,4096,64]{2,3,1,0:T(8,128)(2,1)}, u32[]{:S(2)}) copy-start(bf16[1,1,4096,64]{2,3,1,0:T(8,128)(2,1)} %param.12) | copy-start | bytes 1572868
  39.3 0.8 copy-start.1
  109.0 56.8 %all-to-all-start.2 = ((bf16[64,4,4096]{2,1,0:T(4,128)(2,1)}), bf16[64,4,4096]{2,1,0:T(4,128)(2,1)}, u32[]{:S(2)}, u32[]{:S(2)}) async-start(bf16[64,4,4096]{2,1,0:T(4,128)(2,1)} %reshape.38), calls=%async_computation.2 | async-start | bytes 4194304 | tf_op jit(solution)/shard_map/all_to_all | solution.py:58
  168.4 1.8 copy-start.2
Sparse Core Ops, SparseCore 0:
  106.2 98.4 all-gather.2
where the time goes:
time: 227 us
  blocking collectives  84.4 us (37%)
  waiting for transfers between devices  80.8 us (36%)
  other arithmetic  16 us (7%)
  between operations  14.2 us (6%)
  matrix products  12.7 us (6%)
  local copies, waits for them, and re-layouts  11.1 us (5%)
  starting transfers between devices  7.25 us (3%)
    all_to_all x1, blocking collectives, local(): lax.all_to_all(partial_terms, 'owner', split_axis=0, concat_axis=0, tiled...  55.3 us
    all_to_all x1, waiting for transfers between devices, local(): lax.all_to_all(send_inputs, 'owner', split_axis=0, concat_axis=0, tiled=T...  49.6 us
    all_gather x1, waiting for transfers between devices, prefix(): gathered = lax.all_gather(x.astype(jnp.bfloat16), axis)  31.2 us
    all_to_all x1, blocking collectives, local(): lax.all_to_all(send_grads, 'owner', split_axis=0, concat_axis=0, tiled=True)  29.1 us
    add x7, other arithmetic, combine(): return earlier + later  11.9 us
    all_to_all x1, starting transfers between devices, local(): lax.all_to_all(send_inputs, 'owner', split_axis=0, concat_axis=0, tiled=T...  7.21 us
  transfers between devices with their start and end apart: 2, of which 2 were waited for; matrix products, arithmetic and copies ran while one was open for 5% of the time, Pallas kernels for 0%

commit v1 on v0

v1 whole, which is shorter than its diff:
```python
import jax
import jax.numpy as jnp
from jax import lax
from jax.experimental import pallas as pl
from jax.experimental.pallas import tpu as pltpu
from jax.sharding import PartitionSpec as P

adapter_scale = 2.0
row_limit = 4
group = 2 * row_limit
f32 = jnp.float32
bf16 = jnp.bfloat16


def dot(a, b, contract):
    return lax.dot_general(a, b, (contract, ((), ())), preferred_element_type=f32)


def iota(shape, axis):
    return lax.broadcasted_iota(jnp.int32, shape, axis)


def half_of(shape):
    return (iota(shape, 0) // row_limit) % 2


def place_gradient_kernel(tenant_ref, owner_ref, grad_ref, placing_ref, send_ref):
    tok_rows = tenant_ref.shape[1]
    owners = owner_ref.shape[1]
    slots = owners * group
    named = (iota((owners, tok_rows), 0) == tenant_ref[...]).astype(bf16)
    held = (iota((owners, owners), 0) == owner_ref[...]).astype(bf16)
    goes = dot(held, named, ((1,), (0,)))
    before = (iota((tok_rows, tok_rows), 0) < iota((tok_rows, tok_rows), 1)).astype(bf16)
    rank = dot(goes.astype(bf16), before, ((1,), (0,)))
    key = (goes * (rank + 1.0)).astype(bf16)
    spread = (iota((slots, owners), 0) // group == iota((slots, owners), 1)).astype(bf16)
    wide_key = dot(spread, key, ((1,), (0,)))
    index = (iota((slots, tok_rows), 0) % row_limit + 1).astype(f32)
    placing = wide_key == index
    placing_ref[...] = placing.astype(bf16)
    half = half_of((slots, tok_rows))
    width = grad_ref.shape[1] // 2
    lower = jnp.where(placing & (half == 0), 1.0, 0.0).astype(bf16)
    upper = jnp.where(placing & (half == 1), 1.0, 0.0).astype(bf16)
    sent = dot(lower, grad_ref[:, :width], ((1,), (0,))) + dot(upper, grad_ref[:, width:], ((1,), (0,)))
    send_ref[...] = sent.astype(bf16).reshape(send_ref.shape)


def place_inputs_kernel(placing_ref, low_ref, high_ref, send_ref):
    placing = placing_ref[...]
    half = half_of(placing.shape)
    zero = jnp.zeros_like(placing)
    lower = jnp.where(half == 0, placing, zero)
    upper = jnp.where(half == 1, placing, zero)
    sent = dot(lower, low_ref[...], ((1,), (0,))) + dot(upper, high_ref[...], ((1,), (0,)))
    send_ref[...] = sent.astype(bf16).reshape(send_ref.shape)


def both_halves(x):
    blocks = x.reshape(x.shape[0] // group, group, x.shape[1])
    return (blocks + pltpu.roll(blocks, row_limit, 1)).reshape(x.shape)


def coef_kernel(grad_ref, up_ref, coef_ref):
    grads = grad_ref[...].reshape(coef_ref.shape[0], grad_ref.shape[2])
    width = grad_ref.shape[2]
    low = dot(grads, up_ref[:, :width], ((1,), (1,)))
    high = dot(grads, up_ref[:, width:], ((1,), (1,)))
    part = jnp.where(half_of(low.shape) == 0, low, high)
    coef_ref[...] = (adapter_scale * both_halves(part)).astype(bf16)


def term_kernel(place_ref, coef_ref, low_ref, high_ref, out_ref):
    place = place_ref[0]
    sections = coef_ref.shape[0]
    parts = []
    for k in range(sections):
        parts.append(jnp.where(place <= k, coef_ref[k], jnp.zeros_like(coef_ref[k])))
    coef = jnp.concatenate(parts, axis=1)
    low = dot(coef, low_ref[...], ((1,), (0,)))
    high = dot(coef, high_ref[...], ((1,), (0,)))
    out = jnp.where(half_of(low.shape) == 0, low, high)
    out_ref[...] = out.astype(bf16).reshape(out_ref.shape)


def weight_gradient_kernel(rows_ref, grads_ref, coef_ref, down_ref, grad_down_ref, grad_up_ref):
    slots = coef_ref.shape[0]
    rank = coef_ref.shape[1]
    width = rows_ref.shape[2]
    out_width = grads_ref.shape[2]
    rows = rows_ref[...].reshape(slots, width)
    grads = grads_ref[...].reshape(slots, out_width)
    half = half_of((slots, rank))
    coef = coef_ref[...]
    zero = jnp.zeros_like(coef)
    pair = jnp.concatenate([jnp.where(half == 0, coef, zero), jnp.where(half == 1, coef, zero)], axis=1)
    down = dot(pair, rows, ((0,), (0,)))
    grad_down_ref[:, :width] = down[:rank]
    grad_down_ref[:, width:] = down[rank:]
    low = dot(rows, down_ref[:, :width], ((1,), (1,)))
    high = dot(rows, down_ref[:, width:], ((1,), (1,)))
    proj = both_halves(jnp.where(half == 0, low, high)).astype(bf16)
    pair = jnp.concatenate([jnp.where(half == 0, proj, zero), jnp.where(half == 1, proj, zero)], axis=1)
    up = dot(pair, grads, ((0,), (0,)))
    grad_up_ref[:, :out_width] = up[:rank]
    grad_up_ref[:, out_width:] = up[rank:]


def unplace_kernel(placing_ref, rows_ref, out_ref):
    placing = placing_ref[...]
    mine = half_of(placing.shape) == pl.program_id(1)
    picked = jnp.where(mine, placing, jnp.zeros_like(placing))
    rows = rows_ref[...].reshape(placing.shape[0], rows_ref.shape[2])
    out_ref[...] = dot(picked, rows, ((0,), (0,))).astype(bf16)


def local(
    layer_input_rows,
    output_gradient,
    tenant,
    adapter_owner_index,
    adapter_down_weight,
    adapter_up_weight,
):
    inputs = layer_input_rows[0]
    gradient_list = output_gradient[0]
    tok_rows, width = inputs.shape
    out_width = gradient_list.shape[1]
    owners = adapter_owner_index.shape[0]
    rank = adapter_up_weight.shape[2]
    slots = owners * group
    sections = lax.axis_size("segment")
    place = lax.axis_index("segment").astype(jnp.int32).reshape(1)
    down_factor = adapter_down_weight[0, 0].T
    up_factor = adapter_up_weight[0, 0]
    half_width = width // 2
    steps = 4
    block = half_width // steps
    shape = jax.ShapeDtypeStruct

    all_down = lax.all_gather(down_factor, "segment").reshape(sections * rank, width)

    placing, send_grads = pl.pallas_call(
        place_gradient_kernel,
        out_shape=(shape((slots, tok_rows), bf16), shape((owners, group, out_width // 2), bf16)),
        name="place_gradient",
    )(tenant.reshape(1, tok_rows), adapter_owner_index.reshape(1, owners), gradient_list)
    recv_grads = lax.all_to_all(send_grads, "owner", split_axis=0, concat_axis=0, tiled=True)

    send_inputs = pl.pallas_call(
        place_inputs_kernel,
        grid=(steps,),
        in_specs=[
            pl.BlockSpec((slots, tok_rows), lambda c: (0, 0)),
            pl.BlockSpec((tok_rows, block), lambda c: (0, c)),
            pl.BlockSpec((tok_rows, block), lambda c: (0, c + steps)),
        ],
        out_specs=pl.BlockSpec((owners, group, block), lambda c: (0, 0, c)),
        out_shape=shape((owners, group, half_width), bf16),
        name="place_inputs",
    )(placing, inputs, inputs)

    coef = pl.pallas_call(
        coef_kernel,
        out_shape=shape((slots, rank), bf16),
        name="coef",
    )(recv_grads, up_factor)

    recv_inputs = lax.all_to_all(send_inputs, "owner", split_axis=0, concat_axis=0, tiled=True)
    all_coef = lax.all_gather(coef, "segment")

    terms = pl.pallas_call(
        term_kernel,
        grid=(steps,),
        in_specs=[
            pl.BlockSpec(memory_space=pltpu.SMEM),
            pl.BlockSpec((sections, slots, rank), lambda c: (0, 0, 0)),
            pl.BlockSpec((sections * rank, block), lambda c: (0, c)),
            pl.BlockSpec((sections * rank, block), lambda c: (0, c + steps)),
        ],
        out_specs=pl.BlockSpec((owners, group, block), lambda c: (0, 0, c)),
        out_shape=shape((owners, group, half_width), bf16),
        name="term",
    )(place, all_coef, all_down, all_down)
    returned = lax.all_to_all(terms, "owner", split_axis=0, concat_axis=0, tiled=True)

    grad_down, grad_up = pl.pallas_call(
        weight_gradient_kernel,
        out_shape=(shape((rank, width), f32), shape((rank, out_width), f32)),
        name="weight_gradient",
    )(recv_inputs, recv_grads, coef, down_factor)

    passed = pl.pallas_call(
        unplace_kernel,
        grid=(steps, 2),
        in_specs=[
            pl.BlockSpec((slots, tok_rows), lambda c, h: (0, 0)),
            pl.BlockSpec((owners, group, block), lambda c, h: (0, 0, c)),
        ],
        out_specs=pl.BlockSpec((tok_rows, block), lambda c, h: (0, h * steps + c)),
        out_shape=shape((tok_rows, width), bf16),
        name="unplace",
    )(placing, returned)

    return (passed[None], grad_down.T[None, None], grad_up[None, None])


def solution(mesh):
    return jax.shard_map(
        local,
        mesh=mesh,
        in_specs=(
            P("segment", "owner", None),
            P("segment", "owner", None),
            P("owner", None),
            P(),
            P("segment", "owner", None, None),
            P("segment", "owner", None, None),
        ),
        out_specs=(
            P("segment", "owner", None),
            P("segment", "owner", None, None),
            P("segment", "owner", None, None),
        ),
        check_vma=False,
    )
```

time: 227 us -> 167 us (0.74)
  blocking collectives: 84.4 us -> 34.6 us
  Pallas kernels: 0 us -> 26.8 us
  starting transfers between devices: 7.25 us -> 24.9 us
  other arithmetic: 16 us -> 0 us
  waiting for transfers between devices: 80.8 us -> 65.2 us
  matrix products: 12.7 us -> 0 us
  local copies, waits for them, and re-layouts: 11.1 us -> 0.01 us
    all_to_all x2 -> x0, blocking collectives: 84.4 us -> none  [the longest x1 55.3 us: local(): lax.all_to_all(partial_terms, 'owner', split_axis=0, concat_axis=0, tiled...]
    all_to_all x0 -> x2, waiting for transfers between devices: none -> 58.1 us  [the longest x1 45.1 us: local(): lax.all_to_all(terms, 'owner', split_axis=0, concat_axis=0, tiled=True)]
    all_to_all x1, waiting for transfers between devices: 49.6 us -> 6.48 us  [local(): lax.all_to_all(send_inputs, 'owner', split_axis=0, concat_axis=0, tiled=T...]
    all_gather x0 -> x1, blocking collectives: none -> 34.6 us  [local(): all_coef = lax.all_gather(coef, 'segment')]
    all_gather x1, waiting for transfers between devices: 31.2 us -> 0.01 us  [local(): lax.all_gather(down_factor, 'segment').reshape(sections * rank, width)]
    pallas_call x0 -> x6, Pallas kernels: none -> 26.8 us  [the longest x1 6.42 us: local(): pl.pallas_call(unplace_kernel, grid=(steps, 2), in_specs=[pl.BlockSpec((s...]
    all_to_all x0 -> x2, starting transfers between devices: none -> 19.2 us  [the longest x1 11.6 us: local(): lax.all_to_all(send_grads, 'owner', split_axis=0, concat_axis=0, tiled=True)]
    dot_general x8 -> x0, matrix products: 12.7 us -> none  [the longest x1 3.17 us: local(): jnp.einsum('rk,dk->rd', scale_weight, down_factor, precision=highest_prec...]
  transfers between devices with their start and end apart: 2 -> 4, of which waited for: 2 -> 3; matrix products, arithmetic and copies ran while one was open for 5% -> 0% of each run, Pallas kernels for 0% -> 12%
where the time goes in v1:
time: 167 us; the launch traced here: 166 us
  waiting for transfers between devices  65.2 us (39%)
  blocking collectives  34.6 us (21%)
  Pallas kernels  26.8 us (16%)
  starting transfers between devices  24.9 us (15%)
  between operations  14.1 us (8%)
    all_to_all x1, waiting for transfers between devices, local(): lax.all_to_all(terms, 'owner', split_axis=0, concat_axis=0, tiled=True)  45.1 us
    all_gather x1, blocking collectives, local(): all_coef = lax.all_gather(coef, 'segment')  34.6 us
    all_to_all x1, waiting for transfers between devices, local(): lax.all_to_all(send_grads, 'owner', split_axis=0, concat_axis=0, tiled=True)  13 us
    all_to_all x1, starting transfers between devices, local(): lax.all_to_all(send_grads, 'owner', split_axis=0, concat_axis=0, tiled=True)  11.6 us
    all_to_all x1, starting transfers between devices, local(): lax.all_to_all(terms, 'owner', split_axis=0, concat_axis=0, tiled=True)  7.55 us
    all_to_all x1, waiting for transfers between devices, local(): lax.all_to_all(send_inputs, 'owner', split_axis=0, concat_axis=0, tiled=T...  6.48 us
    pallas_call x1, Pallas kernels, local(): pl.pallas_call(unplace_kernel, grid=(steps, 2), in_specs=[pl.BlockSpec((s...  6.42 us
    pallas_call x1, Pallas kernels, local(): pl.pallas_call(term_kernel, grid=(steps,), in_specs=[pl.BlockSpec(memory_...  6.42 us
  transfers between devices with their start and end apart: 4, of which 3 were waited for; matrix products, arithmetic and copies ran while one was open for 0% of the time, Pallas kernels for 12%

profile of v1, /device:TPU:1, one launch (start us, length us, event | category | flops | bytes accessed | tf_op | source)
XLA Modules:
  0.0 165.7 jit_solution(9268006328664685779)
XLA Ops:
  7.2 0.0 all-gather.4.cloned.1.call-start
  7.2 0.7 all-gather.4.cloned.1.call-update
  7.9 2.6 %place_gradient.1 = (bf16[512,128]{1,0:T(8,128)(2,1)}, bf16[64,8,512]{2,1,0:T(8,128)(2,1)}) custom-call(s32[1,128]{1,0:T(1,128)} %bitcast.23, s32[1,64]{1,0:T(1,128)} %bitcast.24, bf16[128,1024]{1,0:T(8,128)(2,1)} %bitcast.21), custom_call_target="tpu_custom_call" | custom-call | tf_op jit(solution)/shard_map/place_gradient/pallas_call | solution.py:144
  10.5 11.6 %all-to-all-start = ((bf16[64,8,512]{2,1,0:T(8,128)(2,1)}), bf16[64,8,512]{2,1,0:T(8,128)(2,1)S(1)}, u32[]{:S(2)}, u32[]{:S(2)}) async-start(bf16[64,8,512]{2,1,0:T(8,128)(2,1)} %get-tuple-element.8), calls=%async_computation | async-start | bytes 1048576 | tf_op jit(solution)/shard_map/all_to_all | solution.py:149
  22.1 4.7 %place_inputs.1 = bf16[64,8,2048]{2,1,0:T(8,128)(2,1)} custom-call(bf16[512,128]{1,0:T(8,128)(2,1)} %get-tuple-element.7.placing_ref, bf16[128,4096]{1,0:T(8,128)(2,1)} %bitcast.16, bf16[128,4096]{1,0:T(8,128)(2,1)} %bitcast.17), custom_call_target="tpu_custom_call" | custom-call | tf_op jit(solution)/shard_map/place_inputs/pallas_call | solution.py:151
  26.8 13.0 %all-to-all-done.grad_ref.grads_ref = bf16[64,8,512]{2,1,0:T(8,128)(2,1)S(1)} async-done(((bf16[64,8,512]{2,1,0:T(8,128)(2,1)}), bf16[64,8,512]{2,1,0:T(8,128)(2,1)S(1)}, u32[]{:S(2)}, u32[]{:S(2)}) %all-to-all-start) | async-done | bytes 524320 | tf_op jit(solution)/shard_map/all_to_all | solution.py:149
  39.8 0.0 copy-start.1
  39.8 5.7 %all-to-all-start.2 = ((bf16[64,8,2048]{2,1,0:T(8,128)(2,1)}), bf16[64,8,2048]{2,1,0:T(8,128)(2,1)S(1)}, u32[]{:S(2)}, u32[]{:S(2)}) async-start(bf16[64,8,2048]{2,1,0:T(8,128)(2,1)} %place_inputs.1), calls=%async_computation.2 | async-start | bytes 4194304 | tf_op jit(solution)/shard_map/all_to_all | solution.py:170
  45.6 0.0 copy-done.1
  45.6 2.1 %coef.1.coef_ref = bf16[512,64]{1,0:T(8,128)(2,1)} custom-call(bf16[64,8,512]{2,1,0:T(8,128)(2,1)} %copy-done.1, bf16[64,1024]{1,0:T(8,128)(2,1)} %bitcast.22), custom_call_target="tpu_custom_call" | custom-call | tf_op jit(solution)/shard_map/coef/pallas_call | solution.py:164
  47.7 34.6 %all-gather = bf16[4096,64]{1,0:T(8,128)(2,1)} all-gather(bf16[512,64]{1,0:T(8,128)(2,1)} %coef.1.coef_ref), channel_id=2, replica_groups=mesh['segment'=8,'owner'=64] {'segment'}, dimensions={0}, use_global_device_ids=true | all-gather | bytes 589824 | tf_op jit(solution)/shard_map/all_gather | solution.py:171
  82.4 0.0 all-gather.4.cloned.1.call-done.low_ref.high_ref
  82.4 6.4 %term.1 = bf16[64,8,2048]{2,1,0:T(8,128)(2,1)} custom-call(s32[1]{0:T(128)} %bitcast.3.place_ref, bf16[8,512,64]{2,1,0:T(8,128)(2,1)} %bitcast.15, bf16[512,4096]{1,0:T(8,128)(2,1)} %all-gather.4.cloned.1.call-done.low_ref.high_ref, bf16[512,4096]{1,0:T(8,128)(2,1)} %all-gather.4.cloned.1.call-done.low_ref.high_ref), custom_call_target="tpu_custom_call" | custom-call | tf_op jit(solution)/shard_map/term/pallas_call | solution.py:173
  88.8 6.5 %all-to-all-done.2.rows_ref = bf16[64,8,2048]{2,1,0:T(8,128)(2,1)S(1)} async-done(((bf16[64,8,2048]{2,1,0:T(8,128)(2,1)}), bf16[64,8,2048]{2,1,0:T(8,128)(2,1)S(1)}, u32[]{:S(2)}, u32[]{:S(2)}) %all-to-all-start.2) | async-done | bytes 2097184 | tf_op jit(solution)/shard_map/all_to_all | solution.py:170
  95.3 0.0 copy-start
  95.3 7.6 %all-to-all-start.1 = ((bf16[64,8,2048]{2,1,0:T(8,128)(2,1)}), bf16[64,8,2048]{2,1,0:T(8,128)(2,1)}, u32[]{:S(2)}, u32[]{:S(2)}) async-start(bf16[64,8,2048]{2,1,0:T(8,128)(2,1)} %term.1), calls=%async_computation.1 | async-start | bytes 4194304 | tf_op jit(solution)/shard_map/all_to_all | solution.py:186
  102.8 0.0 copy-done
  102.8 4.5 %weight_gradient.1 = (f32[64,4096]{1,0:T(8,128)}, f32[64,1024]{1,0:T(8,128)}) custom-call(bf16[64,8,2048]{2,1,0:T(8,128)(2,1)} %copy-done, bf16[64,8,512]{2,1,0:T(8,128)(2,1)} %copy-done.1, bf16[512,64]{1,0:T(8,128)(2,1)} %coef.1.coef_ref, bf16[64,4096]{1,0:T(8,128)(2,1)} %bitcast.19), custom_call_target="tpu_custom_call" | custom-call | tf_op jit(solution)/shard_map/weight_gradient/pallas_call | solution.py:188
  107.4 45.1 %all-to-all-done.1.rows_ref = bf16[64,8,2048]{2,1,0:T(8,128)(2,1)} async-done(((bf16[64,8,2048]{2,1,0:T(8,128)(2,1)}), bf16[64,8,2048]{2,1,0:T(8,128)(2,1)}, u32[]{:S(2)}, u32[]{:S(2)}) %all-to-all-start.1) | async-done | bytes 2097184 | tf_op jit(solution)/shard_map/all_to_all | solution.py:186
  152.4 6.4 %unplace.1 = bf16[128,4096]{1,0:T(8,128)(2,1)} custom-call(bf16[512,128]{1,0:T(8,128)(2,1)} %get-tuple-element.7.placing_ref, bf16[64,8,2048]{2,1,0:T(8,128)(2,1)} %all-to-all-done.1.rows_ref), custom_call_target="tpu_custom_call" | custom-call | tf_op jit(solution)/shard_map/unplace/pallas_call | solution.py:194
Async XLA Ops:
  7.2 75.2 %all-gather.4.cloned.1.call-start = ((), (), s32[]{:S(2)}) async-start(), calls=%async_computation.3 | async-start | bytes 4718592 | tf_op jit(solution)/shard_map/all_gather | solution.py:142
  10.5 29.3 %all-to-all-start = ((bf16[64,8,512]{2,1,0:T(8,128)(2,1)}), bf16[64,8,512]{2,1,0:T(8,128)(2,1)S(1)}, u32[]{:S(2)}, u32[]{:S(2)}) async-start(bf16[64,8,512]{2,1,0:T(8,128)(2,1)} %get-tuple-element.8), calls=%async_computation | async-start | bytes 1048576 | tf_op jit(solution)/shard_map/all_to_all | solution.py:149
  39.8 5.7 %copy-start.1 = (bf16[64,8,512]{2,1,0:T(8,128)(2,1)}, bf16[64,8,512]{2,1,0:T(8,128)(2,1)S(1)}, u32[]{:S(2)}) copy-start(bf16[64,8,512]{2,1,0:T(8,128)(2,1)S(1)} %all-to-all-done.grad_ref.grads_ref) | copy-start | bytes 1572868
  39.8 55.4 %all-to-all-start.2 = ((bf16[64,8,2048]{2,1,0:T(8,128)(2,1)}), bf16[64,8,2048]{2,1,0:T(8,128)(2,1)S(1)}, u32[]{:S(2)}, u32[]{:S(2)}) async-start(bf16[64,8,2048]{2,1,0:T(8,128)(2,1)} %place_inputs.1), calls=%async_computation.2 | async-start | bytes 4194304 | tf_op jit(solution)/shard_map/all_to_all | solution.py:170
  95.3 7.6 %copy-start = (bf16[64,8,2048]{2,1,0:T(8,128)(2,1)}, bf16[64,8,2048]{2,1,0:T(8,128)(2,1)S(1)}, u32[]{:S(2)}) copy-start(bf16[64,8,2048]{2,1,0:T(8,128)(2,1)S(1)} %all-to-all-done.2.rows_ref) | copy-start | bytes 6291460
  95.3 57.2 %all-to-all-start.1 = ((bf16[64,8,2048]{2,1,0:T(8,128)(2,1)}), bf16[64,8,2048]{2,1,0:T(8,128)(2,1)}, u32[]{:S(2)}, u32[]{:S(2)}) async-start(bf16[64,8,2048]{2,1,0:T(8,128)(2,1)} %term.1), calls=%async_computation.1 | async-start | bytes 4194304 | tf_op jit(solution)/shard_map/all_to_all | solution.py:186
Sparse Core Ops, SparseCore 0:
  10.1 71.8 all-gather.3

commit v2 on v1

--- a/solution.py
+++ b/solution.py
@@ -28,14 +28,12 @@
     tok_rows = tenant_ref.shape[1]
     owners = owner_ref.shape[1]
     slots = owners * group
-    named = (iota((owners, tok_rows), 0) == tenant_ref[...]).astype(bf16)
-    held = (iota((owners, owners), 0) == owner_ref[...]).astype(bf16)
-    goes = dot(held, named, ((1,), (0,)))
+    named = iota((owners, tok_rows), 0) == tenant_ref[...]
     before = (iota((tok_rows, tok_rows), 0) < iota((tok_rows, tok_rows), 1)).astype(bf16)
-    rank = dot(goes.astype(bf16), before, ((1,), (0,)))
-    key = (goes * (rank + 1.0)).astype(bf16)
-    spread = (iota((slots, owners), 0) // group == iota((slots, owners), 1)).astype(bf16)
-    wide_key = dot(spread, key, ((1,), (0,)))
+    rank = dot(named.astype(bf16), before, ((1,), (0,)))
+    key = jnp.where(named, rank + 1.0, 0.0).astype(bf16)
+    held = (iota((slots, owners), 0) // group == owner_ref[...]).astype(bf16)
+    wide_key = dot(held, key, ((1,), (0,)))
     index = (iota((slots, tok_rows), 0) % row_limit + 1).astype(f32)
     placing = wide_key == index
     placing_ref[...] = placing.astype(bf16)
@@ -47,12 +45,18 @@
     send_ref[...] = sent.astype(bf16).reshape(send_ref.shape)
 
 
-def place_inputs_kernel(placing_ref, low_ref, high_ref, send_ref):
+def place_inputs_kernel(placing_ref, low_ref, high_ref, send_ref, back_ref):
     placing = placing_ref[...]
     half = half_of(placing.shape)
     zero = jnp.zeros_like(placing)
     lower = jnp.where(half == 0, placing, zero)
     upper = jnp.where(half == 1, placing, zero)
+
+    @pl.when(pl.program_id(0) == 0)
+    def _():
+        back_ref[0] = lower.astype(f32).T.astype(bf16)
+        back_ref[1] = upper.astype(f32).T.astype(bf16)
+
     sent = dot(lower, low_ref[...], ((1,), (0,))) + dot(upper, high_ref[...], ((1,), (0,)))
     send_ref[...] = sent.astype(bf16).reshape(send_ref.shape)
 
@@ -71,15 +75,17 @@
     coef_ref[...] = (adapter_scale * both_halves(part)).astype(bf16)
 
 
-def term_kernel(place_ref, coef_ref, low_ref, high_ref, out_ref):
+def term_kernel(place_ref, coef_ref, *refs):
+    sections = coef_ref.shape[0]
+    lows, highs, out_ref = refs[:sections], refs[sections:-1], refs[-1]
     place = place_ref[0]
-    sections = coef_ref.shape[0]
     parts = []
-    for k in range(sections):
-        parts.append(jnp.where(place <= k, coef_ref[k], jnp.zeros_like(coef_ref[k])))
+    for step in range(sections):
+        part = coef_ref[(place + step) % sections]
+        parts.append(jnp.where(place + step < sections, part, jnp.zeros_like(part)))
     coef = jnp.concatenate(parts, axis=1)
-    low = dot(coef, low_ref[...], ((1,), (0,)))
-    high = dot(coef, high_ref[...], ((1,), (0,)))
+    low = dot(coef, jnp.concatenate([r[...] for r in lows], axis=0), ((1,), (0,)))
+    high = dot(coef, jnp.concatenate([r[...] for r in highs], axis=0), ((1,), (0,)))
     out = jnp.where(half_of(low.shape) == 0, low, high)
     out_ref[...] = out.astype(bf16).reshape(out_ref.shape)
 
@@ -107,12 +113,21 @@
     grad_up_ref[:, out_width:] = up[rank:]
 
 
-def unplace_kernel(placing_ref, rows_ref, out_ref):
-    placing = placing_ref[...]
-    mine = half_of(placing.shape) == pl.program_id(1)
-    picked = jnp.where(mine, placing, jnp.zeros_like(placing))
-    rows = rows_ref[...].reshape(placing.shape[0], rows_ref.shape[2])
-    out_ref[...] = dot(picked, rows, ((0,), (0,))).astype(bf16)
+def unplace_kernel(back_ref, rows_ref, out_ref):
+    rows = rows_ref[...].reshape(back_ref.shape[2], rows_ref.shape[2])
+    out_ref[...] = dot(back_ref[0], rows, ((1,), (0,))).astype(bf16)
+
+
+def ring_round(blocks, axis):
+    count = lax.axis_size(axis)
+    down = [(i, (i - 1) % count) for i in range(count)]
+    up = [(i, (i + 1) % count) for i in range(count)]
+    step = (len(blocks) + 1) // 2
+    new = dict(blocks)
+    new[step] = lax.ppermute(blocks[step - 1], axis, down)
+    if step < count - step:
+        new[count - step] = lax.ppermute(blocks[(count - step + 1) % count], axis, up)
+    return new
 
 
 def local(
@@ -139,16 +154,15 @@
     block = half_width // steps
     shape = jax.ShapeDtypeStruct
 
-    all_down = lax.all_gather(down_factor, "segment").reshape(sections * rank, width)
-
     placing, send_grads = pl.pallas_call(
         place_gradient_kernel,
         out_shape=(shape((slots, tok_rows), bf16), shape((owners, group, out_width // 2), bf16)),
         name="place_gradient",
     )(tenant.reshape(1, tok_rows), adapter_owner_index.reshape(1, owners), gradient_list)
+    send_grads, ring_start = lax.optimization_barrier((send_grads, down_factor))
     recv_grads = lax.all_to_all(send_grads, "owner", split_axis=0, concat_axis=0, tiled=True)
 
-    send_inputs = pl.pallas_call(
+    send_inputs, back = pl.pallas_call(
         place_inputs_kernel,
         grid=(steps,),
         in_specs=[
@@ -156,10 +170,16 @@
             pl.BlockSpec((tok_rows, block), lambda c: (0, c)),
             pl.BlockSpec((tok_rows, block), lambda c: (0, c + steps)),
         ],
-        out_specs=pl.BlockSpec((owners, group, block), lambda c: (0, 0, c)),
-        out_shape=shape((owners, group, half_width), bf16),
+        out_specs=(
+            pl.BlockSpec((owners, group, block), lambda c: (0, 0, c)),
+            pl.BlockSpec((2, tok_rows, slots), lambda c: (0, 0, 0)),
+        ),
+        out_shape=(shape((owners, group, half_width), bf16), shape((2, tok_rows, slots), bf16)),
         name="place_inputs",
     )(placing, inputs, inputs)
+
+    blocks = ring_round({0: ring_start}, "segment")
+    send_inputs, blocks = lax.optimization_barrier((send_inputs, blocks))
 
     coef = pl.pallas_call(
         coef_kernel,
@@ -169,6 +189,9 @@
 
     recv_inputs = lax.all_to_all(send_inputs, "owner", split_axis=0, concat_axis=0, tiled=True)
     all_coef = lax.all_gather(coef, "segment")
+    while len(blocks) < sections:
+        blocks = ring_round(blocks, "segment")
+    downs = [blocks[step] for step in range(sections)]
 
     terms = pl.pallas_call(
         term_kernel,
@@ -176,13 +199,13 @@
         in_specs=[
             pl.BlockSpec(memory_space=pltpu.SMEM),
             pl.BlockSpec((sections, slots, rank), lambda c: (0, 0, 0)),
-            pl.BlockSpec((sections * rank, block), lambda c: (0, c)),
-            pl.BlockSpec((sections * rank, block), lambda c: (0, c + steps)),
-        ],
+        ]
+        + [pl.BlockSpec((rank, block), lambda c: (0, c))] * sections
+        + [pl.BlockSpec((rank, block), lambda c: (0, c + steps))] * sections,
         out_specs=pl.BlockSpec((owners, group, block), lambda c: (0, 0, c)),
         out_shape=shape((owners, group, half_width), bf16),
         name="term",
-    )(place, all_coef, all_down, all_down)
+    )(place, all_coef, *downs, *downs)
     returned = lax.all_to_all(terms, "owner", split_axis=0, concat_axis=0, tiled=True)
 
     grad_down, grad_up = pl.pallas_call(
@@ -191,17 +214,19 @@
         name="weight_gradient",
     )(recv_inputs, recv_grads, coef, down_factor)
 
+    back_steps = 2
+    back_block = half_width // back_steps
     passed = pl.pallas_call(
         unplace_kernel,
-        grid=(steps, 2),
+        grid=(back_steps, 2),
         in_specs=[
-            pl.BlockSpec((slots, tok_rows), lambda c, h: (0, 0)),
-            pl.BlockSpec((owners, group, block), lambda c, h: (0, 0, c)),
+            pl.BlockSpec((1, tok_rows, slots), lambda c, h: (h, 0, 0)),
+            pl.BlockSpec((owners, group, back_block), lambda c, h: (0, 0, c)),
         ],
-        out_specs=pl.BlockSpec((tok_rows, block), lambda c, h: (0, h * steps + c)),
+        out_specs=pl.BlockSpec((tok_rows, back_block), lambda c, h: (0, h * back_steps + c)),
         out_shape=shape((tok_rows, width), bf16),
         name="unplace",
-    )(placing, returned)
+    )(back, returned)
 
     return (passed[None], grad_down.T[None, None], grad_up[None, None])
 

time: 167 us -> 198 us (1.19)
  starting transfers between devices: 24.9 us -> 73.3 us
  between operations: 14.1 us -> 0.78 us
  blocking collectives: 34.6 us -> 27.1 us
  waiting for transfers between devices: 65.2 us -> 68.4 us
    ppermute x0 -> x7, starting transfers between devices: none -> 32.3 us  [the longest x4 24.4 us: ring_round(): new[step] = lax.ppermute(blocks[step - 1], axis, down)]
    ppermute x0 -> x7, waiting for transfers between devices: none -> 23.3 us  [the longest x4 18.1 us: ring_round(): new[step] = lax.ppermute(blocks[step - 1], axis, down)]
    all_to_all x1, waiting for transfers between devices: 13 us -> 0.01 us  [local(): lax.all_to_all(send_grads, 'owner', split_axis=0, concat_axis=0, tiled=True)]
    all_to_all x1, starting transfers between devices: 7.55 us -> 18.2 us  [local(): lax.all_to_all(terms, 'owner', split_axis=0, concat_axis=0, tiled=True)]
    all_gather x1, blocking collectives: 34.6 us -> 27.1 us  [local(): all_coef = lax.all_gather(coef, 'segment')]
    all_to_all x1, waiting for transfers between devices: 6.48 us -> 0.01 us  [local(): lax.all_to_all(send_inputs, 'owner', split_axis=0, concat_axis=0, tiled=T...]
    all_to_all x1, starting transfers between devices: 5.72 us -> 11.2 us  [local(): lax.all_to_all(send_inputs, 'owner', split_axis=0, concat_axis=0, tiled=T...]
  transfers between devices with their start and end apart: 4 -> 10, of which waited for: 3 -> 5; matrix products, arithmetic and copies ran while one was open for 0% -> 0% of each run, Pallas kernels for 12% -> 9%
where the time goes in v2:
time: 198 us; the launch traced here: 196 us
  starting transfers between devices  73.3 us (37%)
  waiting for transfers between devices  68.4 us (35%)
  blocking collectives  27.1 us (14%)
  Pallas kernels  25 us (13%)
    all_to_all x1, waiting for transfers between devices, local(): lax.all_to_all(terms, 'owner', split_axis=0, concat_axis=0, tiled=True)  45 us
    all_gather x1, blocking collectives, local(): all_coef = lax.all_gather(coef, 'segment')  27.1 us
    ppermute x4, starting transfers between devices, ring_round(): new[step] = lax.ppermute(blocks[step - 1], axis, down)  24.4 us
    all_to_all x1, starting transfers between devices, local(): lax.all_to_all(terms, 'owner', split_axis=0, concat_axis=0, tiled=True)  18.2 us
    ppermute x4, waiting for transfers between devices, ring_round(): new[step] = lax.ppermute(blocks[step - 1], axis, down)  18.1 us
    all_to_all x1, starting transfers between devices, local(): lax.all_to_all(send_grads, 'owner', split_axis=0, concat_axis=0, tiled=True)  11.6 us
    all_to_all x1, starting transfers between devices, local(): lax.all_to_all(send_inputs, 'owner', split_axis=0, concat_axis=0, tiled=T...  11.2 us
    ppermute x3, starting transfers between devices, ring_round(): lax.ppermute(blocks[(count - step + 1) % count], axis, up)  7.84 us
  transfers between devices with their start and end apart: 10, of which 5 were waited for; matrix products, arithmetic and copies ran while one was open for 0% of the time, Pallas kernels for 9%

profile of v2, /device:TPU:1, one launch (start us, length us, event | category | flops | bytes accessed | tf_op | source)
XLA Modules:
  0.0 196.3 jit_solution(15872224728829958672)
XLA Ops:
  0.6 2.5 %place_gradient.1 = (bf16[512,128]{1,0:T(8,128)(2,1)}, bf16[64,8,512]{2,1,0:T(8,128)(2,1)}) custom-call(s32[1,128]{1,0:T(1,128)} %bitcast.26, s32[1,64]{1,0:T(1,128)} %bitcast.27, bf16[128,1024]{1,0:T(8,128)(2,1)} %bitcast.24), custom_call_target="tpu_custom_call" | custom-call | tf_op jit(solution)/shard_map/place_gradient/pallas_call | solution.py:157
  3.1 11.6 %all-to-all-start = ((bf16[64,8,512]{2,1,0:T(8,128)(2,1)}), bf16[64,8,512]{2,1,0:T(8,128)(2,1)S(1)}, u32[]{:S(2)}, u32[]{:S(2)}) async-start(bf16[64,8,512]{2,1,0:T(8,128)(2,1)} %get-tuple-element.18), calls=%async_computation | async-start | bytes 1048576 | tf_op jit(solution)/shard_map/all_to_all | solution.py:163
  14.7 4.0 %collective-permute-start.1 = (bf16[64,4096]{1,0:T(8,128)(2,1)}, bf16[64,4096]{1,0:T(8,128)(2,1)S(1)}, u32[]{:S(2)}, u32[]{:S(2)}) collective-permute-start(bf16[64,4096]{1,0:T(8,128)(2,1)} %bitcast.15), channel_id=1, source_target_pairs={{0,64},{64,128},{128,192},{192,256},{256,320},{320,384},{384,448},... | collective-permute-start | bytes 1572872 | tf_op jit(solution)/shard_map/ppermute | solution.py:129
  18.7 8.6 %collective-permute-start = (bf16[64,4096]{1,0:T(8,128)(2,1)}, bf16[64,4096]{1,0:T(8,128)(2,1)S(1)}, u32[]{:S(2)}, u32[]{:S(2)}) collective-permute-start(bf16[64,4096]{1,0:T(8,128)(2,1)} %bitcast.16), channel_id=1, source_target_pairs={{0,448},{64,0},{128,64},{192,128},{256,192},{320,256},{384,320},{4... | collective-permute-start | bytes 1572872 | tf_op jit(solution)/shard_map/ppermute | solution.py:127
  27.3 5.0 %place_inputs.1 = (bf16[64,8,2048]{2,1,0:T(8,128)(2,1)}, bf16[2,128,512]{2,1,0:T(8,128)(2,1)}) custom-call(bf16[512,128]{1,0:T(8,128)(2,1)} %get-tuple-element.15.placing_ref, bf16[128,4096]{1,0:T(8,128)(2,1)} %bitcast.21, bf16[128,4096]{1,0:T(8,128)(2,1)} %bitcast.22), custom_call_target="tpu_custom_call" | custom-call | tf_op jit(solution)/shard_map/place_inputs/pallas_call | solution.py:165
  32.3 5.2 %collective-permute-done.1.refs_7_.refs_15_ = bf16[64,4096]{1,0:T(8,128)(2,1)S(1)} collective-permute-done((bf16[64,4096]{1,0:T(8,128)(2,1)}, bf16[64,4096]{1,0:T(8,128)(2,1)S(1)}, u32[]{:S(2)}, u32[]{:S(2)}) %collective-permute-start.1) | collective-permute-done | bytes 524320 | tf_op jit(solution)/shard_map/ppermute | solution.py:129
  37.5 1.0 collective-permute-done.refs_1_.refs_9_
  38.5 0.0 all-to-all-done.grad_ref.grads_ref
  38.5 0.8 copy-done.3
  39.3 0.2 copy-done.1
  39.4 11.2 %all-to-all-start.2 = ((bf16[64,8,2048]{2,1,0:T(8,128)(2,1)}), bf16[64,8,2048]{2,1,0:T(8,128)(2,1)S(1)}, u32[]{:S(2)}, u32[]{:S(2)}) async-start(bf16[64,8,2048]{2,1,0:T(8,128)(2,1)} %get-tuple-element.24), calls=%async_computation.2 | async-start | bytes 4194304 | tf_op jit(solution)/shard_map/all_to_all | solution.py:190
  50.7 5.2 %collective-permute-start.2 = (bf16[64,4096]{1,0:T(8,128)(2,1)}, bf16[64,4096]{1,0:T(8,128)(2,1)S(1)}, u32[]{:S(2)}, u32[]{:S(2)}) collective-permute-start(bf16[64,4096]{1,0:T(8,128)(2,1)} %copy-done.3), channel_id=1, source_target_pairs={{0,448},{64,0},{128,64},{192,128},{256,192},{320,256},{384,320},{4... | collective-permute-start | bytes 1572872 | tf_op jit(solution)/shard_map/ppermute | solution.py:127
  55.9 0.0 copy-done.2
  55.9 1.9 collective-permute-start.5
  57.8 9.2 %collective-permute-done.2.refs_2_.refs_10_ = bf16[64,4096]{1,0:T(8,128)(2,1)S(1)} collective-permute-done((bf16[64,4096]{1,0:T(8,128)(2,1)}, bf16[64,4096]{1,0:T(8,128)(2,1)S(1)}, u32[]{:S(2)}, u32[]{:S(2)}) %collective-permute-start.2) | collective-permute-done | bytes 524320 | tf_op jit(solution)/shard_map/ppermute | solution.py:127
  67.0 5.2 %collective-permute-start.3 = (bf16[64,4096]{1,0:T(8,128)(2,1)S(1)}, bf16[64,4096]{1,0:T(8,128)(2,1)}, u32[]{:S(2)}, u32[]{:S(2)}) collective-permute-start(bf16[64,4096]{1,0:T(8,128)(2,1)S(1)} %collective-permute-done.2.refs_2_.refs_10_), channel_id=1, source_target_pairs={{0,448},{64,0},{128,64},{192,128},{256,192},{320,256},{384,320},{4... | collective-permute-start | bytes 1572872 | tf_op jit(solution)/shard_map/ppermute | solution.py:127
  72.2 0.0 collective-permute-done.5.refs_6_.refs_14_
  72.2 1.9 collective-permute-start.6
  74.2 8.0 %collective-permute-done.3.refs_3_.refs_11_ = bf16[64,4096]{1,0:T(8,128)(2,1)} collective-permute-done((bf16[64,4096]{1,0:T(8,128)(2,1)S(1)}, bf16[64,4096]{1,0:T(8,128)(2,1)}, u32[]{:S(2)}, u32[]{:S(2)}) %collective-permute-start.3) | collective-permute-done | bytes 524320 | tf_op jit(solution)/shard_map/ppermute | solution.py:127
  82.1 5.4 %collective-permute-start.4 = (bf16[64,4096]{1,0:T(8,128)(2,1)}, bf16[64,4096]{1,0:T(8,128)(2,1)}, u32[]{:S(2)}, u32[]{:S(2)}) collective-permute-start(bf16[64,4096]{1,0:T(8,128)(2,1)} %collective-permute-done.3.refs_3_.refs_11_), channel_id=1, source_target_pairs={{0,448},{64,0},{128,64},{192,128},{256,192},{320,256},{384,320},{4... | collective-permute-start | bytes 1572872 | tf_op jit(solution)/shard_map/ppermute | solution.py:127
  87.6 2.1 %coef.1.coef_ref = bf16[512,64]{1,0:T(8,128)(2,1)} custom-call(bf16[64,8,512]{2,1,0:T(8,128)(2,1)} %copy-done.1, bf16[64,1024]{1,0:T(8,128)(2,1)} %bitcast.25), custom_call_target="tpu_custom_call" | custom-call | tf_op jit(solution)/shard_map/coef/pallas_call | solution.py:184
  89.7 27.1 %all-gather = bf16[4096,64]{1,0:T(8,128)(2,1)} all-gather(bf16[512,64]{1,0:T(8,128)(2,1)} %coef.1.coef_ref), channel_id=2, replica_groups=mesh['segment'=8,'owner'=64] {'segment'}, dimensions={0}, use_global_device_ids=true | all-gather | bytes 589824 | tf_op jit(solution)/shard_map/all_gather | solution.py:191
  116.7 0.0 collective-permute-done.6.refs_5_.refs_13_
  116.8 0.0 collective-permute-done.4.refs_4_.refs_12_
  116.8 0.0 copy-done.4
  116.8 0.8 copy-done.5
  117.6 6.4 %term.1 = bf16[64,8,2048]{2,1,0:T(8,128)(2,1)} custom-call(s32[1]{0:T(128)} %bitcast.4.place_ref, bf16[8,512,64]{2,1,0:T(8,128)(2,1)} %bitcast.20, bf16[64,4096]{1,0:T(8,128)(2,1)} %bitcast.17, bf16[64,4096]{1,0:T(8,128)(2,1)} %copy-done.3, bf16[64,4096]{1,0:T(8,128)(2,1)} %copy-done.4, bf16[64,4096]{1,0:T(8,128)(2,1)} %collective-permute-done.3.refs_3_.refs_11_, ...), custom_call_target="tpu_custom_call" | custom-call | tf_op jit(solution)/shard_map/term/pallas_call | solution.py:196
  124.0 0.0 all-to-all-done.2.rows_ref
  124.0 18.2 %all-to-all-start.1 = ((bf16[64,8,2048]{2,1,0:T(8,128)(2,1)}), bf16[64,8,2048]{2,1,0:T(8,128)(2,1)}, u32[]{:S(2)}, u32[]{:S(2)}) async-start(bf16[64,8,2048]{2,1,0:T(8,128)(2,1)} %term.1), calls=%async_computation.1 | async-start | bytes 4194304 | tf_op jit(solution)/shard_map/all_to_all | solution.py:209
  142.3 4.5 %weight_gradient.1 = (f32[64,4096]{1,0:T(8,128)}, f32[64,1024]{1,0:T(8,128)}) custom-call(bf16[64,8,2048]{2,1,0:T(8,128)(2,1)} %copy-done, bf16[64,8,512]{2,1,0:T(8,128)(2,1)} %copy-done.1, bf16[512,64]{1,0:T(8,128)(2,1)} %coef.1.coef_ref, bf16[64,4096]{1,0:T(8,128)(2,1)} %bitcast.19), custom_call_target="tpu_custom_call" | custom-call | tf_op jit(solution)/shard_map/weight_gradient/pallas_call | solution.py:211
  146.8 45.0 %all-to-all-done.1.rows_ref = bf16[64,8,2048]{2,1,0:T(8,128)(2,1)} async-done(((bf16[64,8,2048]{2,1,0:T(8,128)(2,1)}), bf16[64,8,2048]{2,1,0:T(8,128)(2,1)}, u32[]{:S(2)}, u32[]{:S(2)}) %all-to-all-start.1) | async-done | bytes 2097184 | tf_op jit(solution)/shard_map/all_to_all | solution.py:209
  191.9 4.5 %unplace.1 = bf16[128,4096]{1,0:T(8,128)(2,1)} custom-call(bf16[2,128,512]{2,1,0:T(8,128)(2,1)} %get-tuple-element.16.back_ref, bf16[64,8,2048]{2,1,0:T(8,128)(2,1)} %all-to-all-done.1.rows_ref), custom_call_target="tpu_custom_call" | custom-call | tf_op jit(solution)/shard_map/unplace/pallas_call | solution.py:219
  (7 shorter events, 0.0 us)
Async XLA Ops:
  3.1 35.4 %all-to-all-start = ((bf16[64,8,512]{2,1,0:T(8,128)(2,1)}), bf16[64,8,512]{2,1,0:T(8,128)(2,1)S(1)}, u32[]{:S(2)}, u32[]{:S(2)}) async-start(bf16[64,8,512]{2,1,0:T(8,128)(2,1)} %get-tuple-element.18), calls=%async_computation | async-start | bytes 1048576 | tf_op jit(solution)/shard_map/all_to_all | solution.py:163
  14.7 22.8 %collective-permute-start.1 = (bf16[64,4096]{1,0:T(8,128)(2,1)}, bf16[64,4096]{1,0:T(8,128)(2,1)S(1)}, u32[]{:S(2)}, u32[]{:S(2)}) collective-permute-start(bf16[64,4096]{1,0:T(8,128)(2,1)} %bitcast.15), channel_id=1, source_target_pairs={{0,64},{64,128},{128,192},{192,256},{256,320},{320,384},{384,448},... | collective-permute-start | bytes 1572872 | tf_op jit(solution)/shard_map/ppermute | solution.py:129
  18.7 19.7 %collective-permute-start = (bf16[64,4096]{1,0:T(8,128)(2,1)}, bf16[64,4096]{1,0:T(8,128)(2,1)S(1)}, u32[]{:S(2)}, u32[]{:S(2)}) collective-permute-start(bf16[64,4096]{1,0:T(8,128)(2,1)} %bitcast.16), channel_id=1, source_target_pairs={{0,448},{64,0},{128,64},{192,128},{256,192},{320,256},{384,320},{4... | collective-permute-start | bytes 1572872 | tf_op jit(solution)/shard_map/ppermute | solution.py:127
  37.5 18.4 %copy-start.2 = (bf16[64,4096]{1,0:T(8,128)(2,1)}, bf16[64,4096]{1,0:T(8,128)(2,1)S(1)}, u32[]{:S(2)}) copy-start(bf16[64,4096]{1,0:T(8,128)(2,1)S(1)} %collective-permute-done.1.refs_7_.refs_15_) | copy-start | bytes 1572868
  38.5 0.8 copy-start.3
  38.5 1.0 copy-start.1
  39.4 84.6 %all-to-all-start.2 = ((bf16[64,8,2048]{2,1,0:T(8,128)(2,1)}), bf16[64,8,2048]{2,1,0:T(8,128)(2,1)S(1)}, u32[]{:S(2)}, u32[]{:S(2)}) async-start(bf16[64,8,2048]{2,1,0:T(8,128)(2,1)} %get-tuple-element.24), calls=%async_computation.2 | async-start | bytes 4194304 | tf_op jit(solution)/shard_map/all_to_all | solution.py:190
  50.7 16.4 %collective-permute-start.2 = (bf16[64,4096]{1,0:T(8,128)(2,1)}, bf16[64,4096]{1,0:T(8,128)(2,1)S(1)}, u32[]{:S(2)}, u32[]{:S(2)}) collective-permute-start(bf16[64,4096]{1,0:T(8,128)(2,1)} %copy-done.3), channel_id=1, source_target_pairs={{0,448},{64,0},{128,64},{192,128},{256,192},{320,256},{384,320},{4... | collective-permute-start | bytes 1572872 | tf_op jit(solution)/shard_map/ppermute | solution.py:127
  55.9 16.3 %collective-permute-start.5 = (bf16[64,4096]{1,0:T(8,128)(2,1)S(1)}, bf16[64,4096]{1,0:T(8,128)(2,1)}, u32[]{:S(2)}, u32[]{:S(2)}) collective-permute-start(bf16[64,4096]{1,0:T(8,128)(2,1)S(1)} %collective-permute-done.1.refs_7_.refs_15_), channel_id=1, source_target_pairs={{0,64},{64,128},{128,192},{192,256},{256,320},{320,384},{384,448},... | collective-permute-start | bytes 1572872 | tf_op jit(solution)/shard_map/ppermute | solution.py:129
  67.0 49.7 %copy-start.4 = (bf16[64,4096]{1,0:T(8,128)(2,1)}, bf16[64,4096]{1,0:T(8,128)(2,1)S(1)}, u32[]{:S(2)}) copy-start(bf16[64,4096]{1,0:T(8,128)(2,1)S(1)} %collective-permute-done.2.refs_2_.refs_10_) | copy-start | bytes 1572868
  67.0 15.1 %collective-permute-start.3 = (bf16[64,4096]{1,0:T(8,128)(2,1)S(1)}, bf16[64,4096]{1,0:T(8,128)(2,1)}, u32[]{:S(2)}, u32[]{:S(2)}) collective-permute-start(bf16[64,4096]{1,0:T(8,128)(2,1)S(1)} %collective-permute-done.2.refs_2_.refs_10_), channel_id=1, source_target_pairs={{0,448},{64,0},{128,64},{192,128},{256,192},{320,256},{384,320},{4... | collective-permute-start | bytes 1572872 | tf_op jit(solution)/shard_map/ppermute | solution.py:127
  72.2 44.5 %collective-permute-start.6 = (bf16[64,4096]{1,0:T(8,128)(2,1)}, bf16[64,4096]{1,0:T(8,128)(2,1)S(1)}, u32[]{:S(2)}, u32[]{:S(2)}) collective-permute-start(bf16[64,4096]{1,0:T(8,128)(2,1)} %collective-permute-done.5.refs_6_.refs_14_), channel_id=1, source_target_pairs={{0,64},{64,128},{128,192},{192,256},{256,320},{320,384},{384,448},... | collective-permute-start | bytes 1572872 | tf_op jit(solution)/shard_map/ppermute | solution.py:129
  82.1 34.6 %collective-permute-start.4 = (bf16[64,4096]{1,0:T(8,128)(2,1)}, bf16[64,4096]{1,0:T(8,128)(2,1)}, u32[]{:S(2)}, u32[]{:S(2)}) collective-permute-start(bf16[64,4096]{1,0:T(8,128)(2,1)} %collective-permute-done.3.refs_3_.refs_11_), channel_id=1, source_target_pairs={{0,448},{64,0},{128,64},{192,128},{256,192},{320,256},{384,320},{4... | collective-permute-start | bytes 1572872 | tf_op jit(solution)/shard_map/ppermute | solution.py:127
  116.8 0.8 copy-start.5
  124.0 18.2 %copy-start = (bf16[64,8,2048]{2,1,0:T(8,128)(2,1)}, bf16[64,8,2048]{2,1,0:T(8,128)(2,1)S(1)}, u32[]{:S(2)}) copy-start(bf16[64,8,2048]{2,1,0:T(8,128)(2,1)S(1)} %all-to-all-done.2.rows_ref) | copy-start | bytes 6291460
  124.0 67.8 %all-to-all-start.1 = ((bf16[64,8,2048]{2,1,0:T(8,128)(2,1)}), bf16[64,8,2048]{2,1,0:T(8,128)(2,1)}, u32[]{:S(2)}, u32[]{:S(2)}) async-start(bf16[64,8,2048]{2,1,0:T(8,128)(2,1)} %term.1), calls=%async_computation.1 | async-start | bytes 4194304 | tf_op jit(solution)/shard_map/all_to_all | solution.py:209

commit v3 on v2

--- a/solution.py
+++ b/solution.py
@@ -54,8 +54,8 @@
 
     @pl.when(pl.program_id(0) == 0)
     def _():
-        back_ref[0] = lower.astype(f32).T.astype(bf16)
-        back_ref[1] = upper.astype(f32).T.astype(bf16)
+        back_ref[: lower.shape[1]] = lower.astype(f32).T.astype(bf16)
+        back_ref[lower.shape[1] :] = upper.astype(f32).T.astype(bf16)
 
     sent = dot(lower, low_ref[...], ((1,), (0,))) + dot(upper, high_ref[...], ((1,), (0,)))
     send_ref[...] = sent.astype(bf16).reshape(send_ref.shape)
@@ -66,24 +66,40 @@
     return (blocks + pltpu.roll(blocks, row_limit, 1)).reshape(x.shape)
 
 
-def coef_kernel(grad_ref, up_ref, coef_ref):
+def coef_kernel(grad_ref, up_ref, coef_ref, compact_ref):
     grads = grad_ref[...].reshape(coef_ref.shape[0], grad_ref.shape[2])
     width = grad_ref.shape[2]
     low = dot(grads, up_ref[:, :width], ((1,), (1,)))
     high = dot(grads, up_ref[:, width:], ((1,), (1,)))
     part = jnp.where(half_of(low.shape) == 0, low, high)
-    coef_ref[...] = (adapter_scale * both_halves(part)).astype(bf16)
+    coef = (adapter_scale * both_halves(part)).astype(bf16)
+    coef_ref[...] = coef
+    shape = (coef.shape[0], compact_ref.shape[1])
+    row, column = iota(shape, 0), iota(shape, 1)
+    first = row // group * group + row % row_limit == column // row_limit * group + column % row_limit
+    picked = jnp.where(first & (half_of(shape) == 0), 1.0, 0.0).astype(bf16)
+    compact_ref[...] = dot(coef, picked, ((0,), (0,))).astype(bf16)
 
 
 def term_kernel(place_ref, coef_ref, *refs):
-    sections = coef_ref.shape[0]
-    lows, highs, out_ref = refs[:sections], refs[sections:-1], refs[-1]
-    place = place_ref[0]
-    parts = []
-    for step in range(sections):
-        part = coef_ref[(place + step) % sections]
-        parts.append(jnp.where(place + step < sections, part, jnp.zeros_like(part)))
-    coef = jnp.concatenate(parts, axis=1)
+    sections, rank, columns = coef_ref.shape
+    lows, highs, out_ref, wide_ref = refs[:sections], refs[sections : 2 * sections], refs[-2], refs[-1]
+
+    @pl.when(pl.program_id(0) == 0)
+    def _():
+        place = place_ref[0]
+        parts = []
+        for step in range(sections):
+            part = coef_ref[(place + step) % sections]
+            parts.append(jnp.where(place + step < sections, part, jnp.zeros_like(part)))
+        shape = (columns, wide_ref.shape[0])
+        column, row = iota(shape, 0), iota(shape, 1)
+        same = column == row // group * row_limit + row % row_limit
+        spread = jnp.where(same, 1.0, 0.0).astype(bf16)
+        wide = dot(jnp.concatenate(parts, axis=0), spread, ((1,), (0,)))
+        wide_ref[...] = wide.T.astype(bf16)
+
+    coef = wide_ref[...]
     low = dot(coef, jnp.concatenate([r[...] for r in lows], axis=0), ((1,), (0,)))
     high = dot(coef, jnp.concatenate([r[...] for r in highs], axis=0), ((1,), (0,)))
     out = jnp.where(half_of(low.shape) == 0, low, high)
@@ -114,8 +130,14 @@
 
 
 def unplace_kernel(back_ref, rows_ref, out_ref):
-    rows = rows_ref[...].reshape(back_ref.shape[2], rows_ref.shape[2])
-    out_ref[...] = dot(back_ref[0], rows, ((1,), (0,))).astype(bf16)
+    tok_rows = out_ref.shape[0]
+    block = rows_ref.shape[2]
+    rows = rows_ref[...].reshape(back_ref.shape[1], block)
+    both = dot(back_ref[...], rows, ((1,), (0,))).astype(bf16)
+    start = pl.multiple_of(pl.program_id(0) * block, block)
+    out_ref[:, pl.ds(start, block)] = both[:tok_rows]
+    start = pl.multiple_of(out_ref.shape[1] // 2 + pl.program_id(0) * block, block)
+    out_ref[:, pl.ds(start, block)] = both[tok_rows:]
 
 
 def ring_round(blocks, axis):
@@ -159,7 +181,6 @@
         out_shape=(shape((slots, tok_rows), bf16), shape((owners, group, out_width // 2), bf16)),
         name="place_gradient",
     )(tenant.reshape(1, tok_rows), adapter_owner_index.reshape(1, owners), gradient_list)
-    send_grads, ring_start = lax.optimization_barrier((send_grads, down_factor))
     recv_grads = lax.all_to_all(send_grads, "owner", split_axis=0, concat_axis=0, tiled=True)
 
     send_inputs, back = pl.pallas_call(
@@ -172,23 +193,23 @@
         ],
         out_specs=(
             pl.BlockSpec((owners, group, block), lambda c: (0, 0, c)),
-            pl.BlockSpec((2, tok_rows, slots), lambda c: (0, 0, 0)),
+            pl.BlockSpec((2 * tok_rows, slots), lambda c: (0, 0)),
         ),
-        out_shape=(shape((owners, group, half_width), bf16), shape((2, tok_rows, slots), bf16)),
+        out_shape=(shape((owners, group, half_width), bf16), shape((2 * tok_rows, slots), bf16)),
         name="place_inputs",
     )(placing, inputs, inputs)
 
-    blocks = ring_round({0: ring_start}, "segment")
+    blocks = ring_round(ring_round({0: down_factor}, "segment"), "segment")
     send_inputs, blocks = lax.optimization_barrier((send_inputs, blocks))
 
-    coef = pl.pallas_call(
+    coef, compact = pl.pallas_call(
         coef_kernel,
-        out_shape=shape((slots, rank), bf16),
+        out_shape=(shape((slots, rank), bf16), shape((rank, slots // 2), bf16)),
         name="coef",
     )(recv_grads, up_factor)
 
     recv_inputs = lax.all_to_all(send_inputs, "owner", split_axis=0, concat_axis=0, tiled=True)
-    all_coef = lax.all_gather(coef, "segment")
+    all_coef = lax.all_gather(compact, "segment")
     while len(blocks) < sections:
         blocks = ring_round(blocks, "segment")
     downs = [blocks[step] for step in range(sections)]
@@ -198,12 +219,13 @@
         grid=(steps,),
         in_specs=[
             pl.BlockSpec(memory_space=pltpu.SMEM),
-            pl.BlockSpec((sections, slots, rank), lambda c: (0, 0, 0)),
+            pl.BlockSpec((sections, rank, slots // 2), lambda c: (0, 0, 0)),
         ]
         + [pl.BlockSpec((rank, block), lambda c: (0, c))] * sections
         + [pl.BlockSpec((rank, block), lambda c: (0, c + steps))] * sections,
         out_specs=pl.BlockSpec((owners, group, block), lambda c: (0, 0, c)),
         out_shape=shape((owners, group, half_width), bf16),
+        scratch_shapes=[pltpu.VMEM((slots, sections * rank), bf16)],
         name="term",
     )(place, all_coef, *downs, *downs)
     returned = lax.all_to_all(terms, "owner", split_axis=0, concat_axis=0, tiled=True)
@@ -214,16 +236,14 @@
         name="weight_gradient",
     )(recv_inputs, recv_grads, coef, down_factor)
 
-    back_steps = 2
-    back_block = half_width // back_steps
     passed = pl.pallas_call(
         unplace_kernel,
-        grid=(back_steps, 2),
+        grid=(steps,),
         in_specs=[
-            pl.BlockSpec((1, tok_rows, slots), lambda c, h: (h, 0, 0)),
-            pl.BlockSpec((owners, group, back_block), lambda c, h: (0, 0, c)),
+            pl.BlockSpec((2 * tok_rows, slots), lambda c: (0, 0)),
+            pl.BlockSpec((owners, group, block), lambda c: (0, 0, c)),
         ],
-        out_specs=pl.BlockSpec((tok_rows, back_block), lambda c, h: (0, h * back_steps + c)),
+        out_specs=pl.BlockSpec((tok_rows, width), lambda c: (0, 0)),
         out_shape=shape((tok_rows, width), bf16),
         name="unplace",
     )(back, returned)

time: 198 us -> 185 us (0.934)
  waiting for transfers between devices: 68.4 us -> 60.5 us
  blocking collectives: 27.1 us -> 24.9 us
    ppermute x4, waiting for transfers between devices: 18.1 us -> 10.1 us  [ring_round(): new[step] = lax.ppermute(blocks[step - 1], axis, down)]
    all_gather x1, blocking collectives: 27.1 us -> 24.9 us  [local(): all_coef = lax.all_gather(compact, 'segment')]
  transfers between devices with their start and end apart: 10 -> 10, of which waited for: 5 -> 5; matrix products, arithmetic and copies ran while one was open for 0% -> 0% of each run, Pallas kernels for 9% -> 11%
where the time goes in v3:
time: 185 us; the launch traced here: 184 us
  starting transfers between devices  71.5 us (39%)
  waiting for transfers between devices  60.5 us (33%)
  blocking collectives  24.9 us (13%)
  Pallas kernels  24.6 us (13%)
    all_to_all x1, waiting for transfers between devices, local(): lax.all_to_all(terms, 'owner', split_axis=0, concat_axis=0, tiled=True)  45 us
    all_gather x1, blocking collectives, local(): all_coef = lax.all_gather(compact, 'segment')  24.9 us
    ppermute x4, starting transfers between devices, ring_round(): new[step] = lax.ppermute(blocks[step - 1], axis, down)  23.7 us
    all_to_all x1, starting transfers between devices, local(): lax.all_to_all(terms, 'owner', split_axis=0, concat_axis=0, tiled=True)  17 us
    all_to_all x1, starting transfers between devices, local(): lax.all_to_all(send_grads, 'owner', split_axis=0, concat_axis=0, tiled=True)  11.1 us
    all_to_all x1, starting transfers between devices, local(): lax.all_to_all(send_inputs, 'owner', split_axis=0, concat_axis=0, tiled=T...  11.1 us
    ppermute x4, waiting for transfers between devices, ring_round(): new[step] = lax.ppermute(blocks[step - 1], axis, down)  10.1 us
    ppermute x3, starting transfers between devices, ring_round(): lax.ppermute(blocks[(count - step + 1) % count], axis, up)  8.67 us
  transfers between devices with their start and end apart: 10, of which 5 were waited for; matrix products, arithmetic and copies ran while one was open for 0% of the time, Pallas kernels for 11%

profile of v3, /device:TPU:1, one launch (start us, length us, event | category | flops | bytes accessed | tf_op | source)
XLA Modules:
  0.0 183.9 jit_solution(11067036933135593303)
XLA Ops:
  0.6 4.8 %collective-permute-start.2 = (bf16[64,4096]{1,0:T(8,128)(2,1)}, bf16[64,4096]{1,0:T(8,128)(2,1)S(1)}, u32[]{:S(2)}, u32[]{:S(2)}) collective-permute-start(bf16[64,4096]{1,0:T(8,128)(2,1)} %bitcast.15), channel_id=1, source_target_pairs={{0,64},{64,128},{128,192},{192,256},{256,320},{320,384},{384,448},... | collective-permute-start | bytes 1572872 | tf_op jit(solution)/shard_map/ppermute | solution.py:151
  5.5 8.6 %collective-permute-start = (bf16[64,4096]{1,0:T(8,128)(2,1)}, bf16[64,4096]{1,0:T(8,128)(2,1)S(1)}, u32[]{:S(2)}, u32[]{:S(2)}) collective-permute-start(bf16[64,4096]{1,0:T(8,128)(2,1)} %bitcast.16), channel_id=1, source_target_pairs={{0,448},{64,0},{128,64},{192,128},{256,192},{320,256},{384,320},{4... | collective-permute-start | bytes 1572872 | tf_op jit(solution)/shard_map/ppermute | solution.py:149
  14.1 2.5 %place_gradient.1 = (bf16[512,128]{1,0:T(8,128)(2,1)}, bf16[64,8,512]{2,1,0:T(8,128)(2,1)}) custom-call(s32[1,128]{1,0:T(1,128)} %bitcast.26, s32[1,64]{1,0:T(1,128)} %bitcast.27, bf16[128,1024]{1,0:T(8,128)(2,1)} %bitcast.24), custom_call_target="tpu_custom_call" | custom-call | tf_op jit(solution)/shard_map/place_gradient/pallas_call | solution.py:179
  16.5 11.1 %all-to-all-start = ((bf16[64,8,512]{2,1,0:T(8,128)(2,1)}), bf16[64,8,512]{2,1,0:T(8,128)(2,1)S(1)}, u32[]{:S(2)}, u32[]{:S(2)}) async-start(bf16[64,8,512]{2,1,0:T(8,128)(2,1)} %get-tuple-element.19), calls=%async_computation | async-start | bytes 1048576 | tf_op jit(solution)/shard_map/all_to_all | solution.py:184
  27.6 0.0 collective-permute-done.2.refs_7_.refs_15_
  27.6 0.0 copy-start.2
  27.6 1.9 %collective-permute-start.3 = (bf16[64,4096]{1,0:T(8,128)(2,1)S(1)}, bf16[64,4096]{1,0:T(8,128)(2,1)S(1)}, u32[]{:S(2)}, u32[]{:S(2)}) collective-permute-start(bf16[64,4096]{1,0:T(8,128)(2,1)S(1)} %collective-permute-done.2.refs_7_.refs_15_), channel_id=1, source_target_pairs={{0,64},{64,128},{128,192},{192,256},{256,320},{320,384},{384,448},... | collective-permute-start | bytes 1572872 | tf_op jit(solution)/shard_map/ppermute | solution.py:151
  29.6 0.0 collective-permute-done.refs_1_.refs_9_
  29.6 0.0 copy-start.3
  29.6 4.6 %collective-permute-start.1 = (bf16[64,4096]{1,0:T(8,128)(2,1)S(1)}, bf16[64,4096]{1,0:T(8,128)(2,1)S(1)}, u32[]{:S(2)}, u32[]{:S(2)}) collective-permute-start(bf16[64,4096]{1,0:T(8,128)(2,1)S(1)} %collective-permute-done.refs_1_.refs_9_), channel_id=1, source_target_pairs={{0,448},{64,0},{128,64},{192,128},{256,192},{320,256},{384,320},{4... | collective-permute-start | bytes 1572872 | tf_op jit(solution)/shard_map/ppermute | solution.py:149
  34.2 4.9 %place_inputs.1 = (bf16[64,8,2048]{2,1,0:T(8,128)(2,1)}, bf16[256,512]{1,0:T(8,128)(2,1)}) custom-call(bf16[512,128]{1,0:T(8,128)(2,1)} %get-tuple-element.17.placing_ref, bf16[128,4096]{1,0:T(8,128)(2,1)} %bitcast.20, bf16[128,4096]{1,0:T(8,128)(2,1)} %bitcast.21), custom_call_target="tpu_custom_call" | custom-call | tf_op jit(solution)/shard_map/place_inputs/pallas_call | solution.py:186
  39.1 4.7 %collective-permute-done.3.refs_6_.refs_14_ = bf16[64,4096]{1,0:T(8,128)(2,1)S(1)} collective-permute-done((bf16[64,4096]{1,0:T(8,128)(2,1)S(1)}, bf16[64,4096]{1,0:T(8,128)(2,1)S(1)}, u32[]{:S(2)}, u32[]{:S(2)}) %collective-permute-start.3) | collective-permute-done | bytes 524320 | tf_op jit(solution)/shard_map/ppermute | solution.py:151
  43.8 0.9 collective-permute-done.1.refs_2_.refs_10_
  44.7 0.7 all-to-all-done.grad_ref.grads_ref
  45.3 0.1 copy-done.5
  45.5 0.7 copy-done.1
  46.1 11.1 %all-to-all-start.2 = ((bf16[64,8,2048]{2,1,0:T(8,128)(2,1)}), bf16[64,8,2048]{2,1,0:T(8,128)(2,1)S(1)}, u32[]{:S(2)}, u32[]{:S(2)}) async-start(bf16[64,8,2048]{2,1,0:T(8,128)(2,1)} %get-tuple-element.27), calls=%async_computation.2 | async-start | bytes 4194304 | tf_op jit(solution)/shard_map/all_to_all | solution.py:211
  57.2 5.3 %collective-permute-start.4 = (bf16[64,4096]{1,0:T(8,128)(2,1)}, bf16[64,4096]{1,0:T(8,128)(2,1)S(1)}, u32[]{:S(2)}, u32[]{:S(2)}) collective-permute-start(bf16[64,4096]{1,0:T(8,128)(2,1)} %copy-done.5), channel_id=1, source_target_pairs={{0,448},{64,0},{128,64},{192,128},{256,192},{320,256},{384,320},{4... | collective-permute-start | bytes 1572872 | tf_op jit(solution)/shard_map/ppermute | solution.py:149
  62.5 1.9 %collective-permute-start.6 = (bf16[64,4096]{1,0:T(8,128)(2,1)}, bf16[64,4096]{1,0:T(8,128)(2,1)S(1)}, u32[]{:S(2)}, u32[]{:S(2)}) collective-permute-start(bf16[64,4096]{1,0:T(8,128)(2,1)} %copy-done.4), channel_id=1, source_target_pairs={{0,64},{64,128},{128,192},{192,256},{256,320},{320,384},{384,448},... | collective-permute-start | bytes 1572872 | tf_op jit(solution)/shard_map/ppermute | solution.py:151
  64.4 9.2 %collective-permute-done.4.refs_3_.refs_11_ = bf16[64,4096]{1,0:T(8,128)(2,1)S(1)} collective-permute-done((bf16[64,4096]{1,0:T(8,128)(2,1)}, bf16[64,4096]{1,0:T(8,128)(2,1)S(1)}, u32[]{:S(2)}, u32[]{:S(2)}) %collective-permute-start.4) | collective-permute-done | bytes 524320 | tf_op jit(solution)/shard_map/ppermute | solution.py:149
  73.6 5.2 %collective-permute-start.5 = (bf16[64,4096]{1,0:T(8,128)(2,1)S(1)}, bf16[64,4096]{1,0:T(8,128)(2,1)}, u32[]{:S(2)}, u32[]{:S(2)}) collective-permute-start(bf16[64,4096]{1,0:T(8,128)(2,1)S(1)} %collective-permute-done.4.refs_3_.refs_11_), channel_id=1, source_target_pairs={{0,448},{64,0},{128,64},{192,128},{256,192},{320,256},{384,320},{4... | collective-permute-start | bytes 1572872 | tf_op jit(solution)/shard_map/ppermute | solution.py:149
  78.9 2.3 %coef.1 = (bf16[512,64]{1,0:T(8,128)(2,1)}, bf16[64,256]{1,0:T(8,128)(2,1)}) custom-call(bf16[64,8,512]{2,1,0:T(8,128)(2,1)} %copy-done.1, bf16[64,1024]{1,0:T(8,128)(2,1)} %bitcast.25), custom_call_target="tpu_custom_call" | custom-call | tf_op jit(solution)/shard_map/coef/pallas_call | solution.py:205
  81.2 24.9 %all-gather = bf16[512,256]{1,0:T(8,128)(2,1)} all-gather(bf16[64,256]{1,0:T(8,128)(2,1)} %get-tuple-element.20), channel_id=2, replica_groups=mesh['segment'=8,'owner'=64] {'segment'}, dimensions={0}, use_global_device_ids=true | all-gather | bytes 294912 | tf_op jit(solution)/shard_map/all_gather | solution.py:212
  106.1 0.0 collective-permute-done.6.refs_5_.refs_13_
  106.1 0.0 collective-permute-done.5.refs_4_.refs_12_
  106.1 0.8 copy-done.7
  106.8 6.3 %term.1 = bf16[64,8,2048]{2,1,0:T(8,128)(2,1)} custom-call(s32[1]{0:T(128)} %bitcast.4.place_ref, bf16[8,64,256]{2,1,0:T(8,128)(2,1)} %bitcast.22, bf16[64,4096]{1,0:T(8,128)(2,1)} %bitcast.17, bf16[64,4096]{1,0:T(8,128)(2,1)} %copy-done.3, bf16[64,4096]{1,0:T(8,128)(2,1)} %copy-done.5, bf16[64,4096]{1,0:T(8,128)(2,1)} %copy-done.6, ...), custom_call_target="tpu_custom_call" | custom-call | tf_op jit(solution)/shard_map/term/pallas_call | solution.py:217
  113.2 0.0 all-to-all-done.2.rows_ref
  113.2 17.0 %all-to-all-start.1 = ((bf16[64,8,2048]{2,1,0:T(8,128)(2,1)}), bf16[64,8,2048]{2,1,0:T(8,128)(2,1)}, u32[]{:S(2)}, u32[]{:S(2)}) async-start(bf16[64,8,2048]{2,1,0:T(8,128)(2,1)} %term.1), calls=%async_computation.1 | async-start | bytes 4194304 | tf_op jit(solution)/shard_map/all_to_all | solution.py:231
  130.2 4.5 %weight_gradient.1 = (f32[64,4096]{1,0:T(8,128)}, f32[64,1024]{1,0:T(8,128)}) custom-call(bf16[64,8,2048]{2,1,0:T(8,128)(2,1)} %copy-done, bf16[64,8,512]{2,1,0:T(8,128)(2,1)} %copy-done.1, bf16[512,64]{1,0:T(8,128)(2,1)} %get-tuple-element.28.coef_ref, bf16[64,4096]{1,0:T(8,128)(2,1)} %bitcast.19), custom_call_target="tpu_custom_call" | custom-call | tf_op jit(solution)/shard_map/weight_gradient/pallas_call | solution.py:233
  134.7 45.0 %all-to-all-done.1.rows_ref = bf16[64,8,2048]{2,1,0:T(8,128)(2,1)} async-done(((bf16[64,8,2048]{2,1,0:T(8,128)(2,1)}), bf16[64,8,2048]{2,1,0:T(8,128)(2,1)}, u32[]{:S(2)}, u32[]{:S(2)}) %all-to-all-start.1) | async-done | bytes 2097184 | tf_op jit(solution)/shard_map/all_to_all | solution.py:231
  179.8 4.1 %unplace.1 = bf16[128,4096]{1,0:T(8,128)(2,1)} custom-call(bf16[256,512]{1,0:T(8,128)(2,1)} %get-tuple-element.18.back_ref, bf16[64,8,2048]{2,1,0:T(8,128)(2,1)} %all-to-all-done.1.rows_ref), custom_call_target="tpu_custom_call" | custom-call | tf_op jit(solution)/shard_map/unplace/pallas_call | solution.py:239
  (11 shorter events, 0.0 us)
Async XLA Ops:
  0.6 27.0 %collective-permute-start.2 = (bf16[64,4096]{1,0:T(8,128)(2,1)}, bf16[64,4096]{1,0:T(8,128)(2,1)S(1)}, u32[]{:S(2)}, u32[]{:S(2)}) collective-permute-start(bf16[64,4096]{1,0:T(8,128)(2,1)} %bitcast.15), channel_id=1, source_target_pairs={{0,64},{64,128},{128,192},{192,256},{256,320},{320,384},{384,448},... | collective-permute-start | bytes 1572872 | tf_op jit(solution)/shard_map/ppermute | solution.py:151
  5.5 24.1 %collective-permute-start = (bf16[64,4096]{1,0:T(8,128)(2,1)}, bf16[64,4096]{1,0:T(8,128)(2,1)S(1)}, u32[]{:S(2)}, u32[]{:S(2)}) collective-permute-start(bf16[64,4096]{1,0:T(8,128)(2,1)} %bitcast.16), channel_id=1, source_target_pairs={{0,448},{64,0},{128,64},{192,128},{256,192},{320,256},{384,320},{4... | collective-permute-start | bytes 1572872 | tf_op jit(solution)/shard_map/ppermute | solution.py:149
  16.5 28.8 %all-to-all-start = ((bf16[64,8,512]{2,1,0:T(8,128)(2,1)}), bf16[64,8,512]{2,1,0:T(8,128)(2,1)S(1)}, u32[]{:S(2)}, u32[]{:S(2)}) async-start(bf16[64,8,512]{2,1,0:T(8,128)(2,1)} %get-tuple-element.19), calls=%async_computation | async-start | bytes 1048576 | tf_op jit(solution)/shard_map/all_to_all | solution.py:184
  27.6 17.8 %copy-start.2 = (bf16[64,4096]{1,0:T(8,128)(2,1)}, bf16[64,4096]{1,0:T(8,128)(2,1)S(1)}, u32[]{:S(2)}) copy-start(bf16[64,4096]{1,0:T(8,128)(2,1)S(1)} %collective-permute-done.2.refs_7_.refs_15_) | copy-start | bytes 1572868
  27.6 16.1 %collective-permute-start.3 = (bf16[64,4096]{1,0:T(8,128)(2,1)S(1)}, bf16[64,4096]{1,0:T(8,128)(2,1)S(1)}, u32[]{:S(2)}, u32[]{:S(2)}) collective-permute-start(bf16[64,4096]{1,0:T(8,128)(2,1)S(1)} %collective-permute-done.2.refs_7_.refs_15_), channel_id=1, source_target_pairs={{0,64},{64,128},{128,192},{192,256},{256,320},{320,384},{384,448},... | collective-permute-start | bytes 1572872 | tf_op jit(solution)/shard_map/ppermute | solution.py:151
  29.6 15.8 %copy-start.3 = (bf16[64,4096]{1,0:T(8,128)(2,1)}, bf16[64,4096]{1,0:T(8,128)(2,1)S(1)}, u32[]{:S(2)}) copy-start(bf16[64,4096]{1,0:T(8,128)(2,1)S(1)} %collective-permute-done.refs_1_.refs_9_) | copy-start | bytes 1572868
  29.6 15.1 %collective-permute-start.1 = (bf16[64,4096]{1,0:T(8,128)(2,1)S(1)}, bf16[64,4096]{1,0:T(8,128)(2,1)S(1)}, u32[]{:S(2)}, u32[]{:S(2)}) collective-permute-start(bf16[64,4096]{1,0:T(8,128)(2,1)S(1)} %collective-permute-done.refs_1_.refs_9_), channel_id=1, source_target_pairs={{0,448},{64,0},{128,64},{192,128},{256,192},{320,256},{384,320},{4... | collective-permute-start | bytes 1572872 | tf_op jit(solution)/shard_map/ppermute | solution.py:149
  43.8 1.6 copy-start.4
  44.7 0.8 copy-start.5
  45.3 0.8 copy-start.1
  46.1 67.1 %all-to-all-start.2 = ((bf16[64,8,2048]{2,1,0:T(8,128)(2,1)}), bf16[64,8,2048]{2,1,0:T(8,128)(2,1)S(1)}, u32[]{:S(2)}, u32[]{:S(2)}) async-start(bf16[64,8,2048]{2,1,0:T(8,128)(2,1)} %get-tuple-element.27), calls=%async_computation.2 | async-start | bytes 4194304 | tf_op jit(solution)/shard_map/all_to_all | solution.py:211
  57.2 16.5 %collective-permute-start.4 = (bf16[64,4096]{1,0:T(8,128)(2,1)}, bf16[64,4096]{1,0:T(8,128)(2,1)S(1)}, u32[]{:S(2)}, u32[]{:S(2)}) collective-permute-start(bf16[64,4096]{1,0:T(8,128)(2,1)} %copy-done.5), channel_id=1, source_target_pairs={{0,448},{64,0},{128,64},{192,128},{256,192},{320,256},{384,320},{4... | collective-permute-start | bytes 1572872 | tf_op jit(solution)/shard_map/ppermute | solution.py:149
  62.5 43.5 %collective-permute-start.6 = (bf16[64,4096]{1,0:T(8,128)(2,1)}, bf16[64,4096]{1,0:T(8,128)(2,1)S(1)}, u32[]{:S(2)}, u32[]{:S(2)}) collective-permute-start(bf16[64,4096]{1,0:T(8,128)(2,1)} %copy-done.4), channel_id=1, source_target_pairs={{0,64},{64,128},{128,192},{192,256},{256,320},{320,384},{384,448},... | collective-permute-start | bytes 1572872 | tf_op jit(solution)/shard_map/ppermute | solution.py:151
  73.6 32.4 %copy-start.6 = (bf16[64,4096]{1,0:T(8,128)(2,1)}, bf16[64,4096]{1,0:T(8,128)(2,1)S(1)}, u32[]{:S(2)}) copy-start(bf16[64,4096]{1,0:T(8,128)(2,1)S(1)} %collective-permute-done.4.refs_3_.refs_11_) | copy-start | bytes 1572868
  73.6 32.4 %collective-permute-start.5 = (bf16[64,4096]{1,0:T(8,128)(2,1)S(1)}, bf16[64,4096]{1,0:T(8,128)(2,1)}, u32[]{:S(2)}, u32[]{:S(2)}) collective-permute-start(bf16[64,4096]{1,0:T(8,128)(2,1)S(1)} %collective-permute-done.4.refs_3_.refs_11_), channel_id=1, source_target_pairs={{0,448},{64,0},{128,64},{192,128},{256,192},{320,256},{384,320},{4... | collective-permute-start | bytes 1572872 | tf_op jit(solution)/shard_map/ppermute | solution.py:149
  106.1 0.8 copy-start.7
  113.2 17.0 %copy-start = (bf16[64,8,2048]{2,1,0:T(8,128)(2,1)}, bf16[64,8,2048]{2,1,0:T(8,128)(2,1)S(1)}, u32[]{:S(2)}) copy-start(bf16[64,8,2048]{2,1,0:T(8,128)(2,1)S(1)} %all-to-all-done.2.rows_ref) | copy-start | bytes 6291460
  113.2 66.6 %all-to-all-start.1 = ((bf16[64,8,2048]{2,1,0:T(8,128)(2,1)}), bf16[64,8,2048]{2,1,0:T(8,128)(2,1)}, u32[]{:S(2)}, u32[]{:S(2)}) async-start(bf16[64,8,2048]{2,1,0:T(8,128)(2,1)} %term.1), calls=%async_computation.1 | async-start | bytes 4194304 | tf_op jit(solution)/shard_map/all_to_all | solution.py:231

commit v4 on v3

--- a/solution.py
+++ b/solution.py
@@ -81,17 +81,15 @@
     compact_ref[...] = dot(coef, picked, ((0,), (0,))).astype(bf16)
 
 
-def term_kernel(place_ref, coef_ref, *refs):
+def term_kernel(place_ref, coef_ref, low_ref, high_ref, out_ref, wide_ref):
     sections, rank, columns = coef_ref.shape
-    lows, highs, out_ref, wide_ref = refs[:sections], refs[sections : 2 * sections], refs[-2], refs[-1]
 
     @pl.when(pl.program_id(0) == 0)
     def _():
         place = place_ref[0]
         parts = []
-        for step in range(sections):
-            part = coef_ref[(place + step) % sections]
-            parts.append(jnp.where(place + step < sections, part, jnp.zeros_like(part)))
+        for k in range(sections):
+            parts.append(jnp.where(place <= k, coef_ref[k], jnp.zeros_like(coef_ref[k])))
         shape = (columns, wide_ref.shape[0])
         column, row = iota(shape, 0), iota(shape, 1)
         same = column == row // group * row_limit + row % row_limit
@@ -100,8 +98,8 @@
         wide_ref[...] = wide.T.astype(bf16)
 
     coef = wide_ref[...]
-    low = dot(coef, jnp.concatenate([r[...] for r in lows], axis=0), ((1,), (0,)))
-    high = dot(coef, jnp.concatenate([r[...] for r in highs], axis=0), ((1,), (0,)))
+    low = dot(coef, low_ref[...], ((1,), (0,)))
+    high = dot(coef, high_ref[...], ((1,), (0,)))
     out = jnp.where(half_of(low.shape) == 0, low, high)
     out_ref[...] = out.astype(bf16).reshape(out_ref.shape)
 
@@ -138,18 +136,6 @@
     out_ref[:, pl.ds(start, block)] = both[:tok_rows]
     start = pl.multiple_of(out_ref.shape[1] // 2 + pl.program_id(0) * block, block)
     out_ref[:, pl.ds(start, block)] = both[tok_rows:]
-
-
-def ring_round(blocks, axis):
-    count = lax.axis_size(axis)
-    down = [(i, (i - 1) % count) for i in range(count)]
-    up = [(i, (i + 1) % count) for i in range(count)]
-    step = (len(blocks) + 1) // 2
-    new = dict(blocks)
-    new[step] = lax.ppermute(blocks[step - 1], axis, down)
-    if step < count - step:
-        new[count - step] = lax.ppermute(blocks[(count - step + 1) % count], axis, up)
-    return new
 
 
 def local(
@@ -176,6 +162,8 @@
     block = half_width // steps
     shape = jax.ShapeDtypeStruct
 
+    all_down = lax.all_gather(down_factor, "segment").reshape(sections * rank, width)
+
     placing, send_grads = pl.pallas_call(
         place_gradient_kernel,
         out_shape=(shape((slots, tok_rows), bf16), shape((owners, group, out_width // 2), bf16)),
@@ -199,9 +187,6 @@
         name="place_inputs",
     )(placing, inputs, inputs)
 
-    blocks = ring_round(ring_round({0: down_factor}, "segment"), "segment")
-    send_inputs, blocks = lax.optimization_barrier((send_inputs, blocks))
-
     coef, compact = pl.pallas_call(
         coef_kernel,
         out_shape=(shape((slots, rank), bf16), shape((rank, slots // 2), bf16)),
@@ -210,9 +195,6 @@
 
     recv_inputs = lax.all_to_all(send_inputs, "owner", split_axis=0, concat_axis=0, tiled=True)
     all_coef = lax.all_gather(compact, "segment")
-    while len(blocks) < sections:
-        blocks = ring_round(blocks, "segment")
-    downs = [blocks[step] for step in range(sections)]
 
     terms = pl.pallas_call(
         term_kernel,
@@ -220,14 +202,14 @@
         in_specs=[
             pl.BlockSpec(memory_space=pltpu.SMEM),
             pl.BlockSpec((sections, rank, slots // 2), lambda c: (0, 0, 0)),
-        ]
-        + [pl.BlockSpec((rank, block), lambda c: (0, c))] * sections
-        + [pl.BlockSpec((rank, block), lambda c: (0, c + steps))] * sections,
+            pl.BlockSpec((sections * rank, block), lambda c: (0, c)),
+            pl.BlockSpec((sections * rank, block), lambda c: (0, c + steps)),
+        ],
         out_specs=pl.BlockSpec((owners, group, block), lambda c: (0, 0, c)),
         out_shape=shape((owners, group, half_width), bf16),
         scratch_shapes=[pltpu.VMEM((slots, sections * rank), bf16)],
         name="term",
-    )(place, all_coef, *downs, *downs)
+    )(place, all_coef, all_down, all_down)
     returned = lax.all_to_all(terms, "owner", split_axis=0, concat_axis=0, tiled=True)
 
     grad_down, grad_up = pl.pallas_call(

time: 185 us -> 165 us (0.89)
  starting transfers between devices: 71.5 us -> 24.6 us
  between operations: 0.8 us -> 14.1 us
  waiting for transfers between devices: 60.5 us -> 70.6 us
  blocking collectives: 24.9 us -> 29.1 us
    ppermute x7 -> x0, starting transfers between devices: 32.4 us -> none  [the longest x4 23.7 us: ring_round(): new[step] = lax.ppermute(blocks[step - 1], axis, down)]
    ppermute x7 -> x0, waiting for transfers between devices: 14.8 us -> none  [the longest x4 10.1 us: ring_round(): new[step] = lax.ppermute(blocks[step - 1], axis, down)]
    all_to_all x1, waiting for transfers between devices: 0.67 us -> 12.8 us  [local(): lax.all_to_all(send_grads, 'owner', split_axis=0, concat_axis=0, tiled=True)]
    all_to_all x1, waiting for transfers between devices: 0.01 us -> 12.1 us  [local(): lax.all_to_all(send_inputs, 'owner', split_axis=0, concat_axis=0, tiled=T...]
    all_to_all x1, starting transfers between devices: 17 us -> 7.21 us  [local(): lax.all_to_all(terms, 'owner', split_axis=0, concat_axis=0, tiled=True)]
    all_to_all x1, starting transfers between devices: 11.1 us -> 5.72 us  [local(): lax.all_to_all(send_inputs, 'owner', split_axis=0, concat_axis=0, tiled=T...]
    all_gather x1, blocking collectives: 24.9 us -> 29.1 us  [local(): all_coef = lax.all_gather(compact, 'segment')]
  transfers between devices with their start and end apart: 10 -> 4, of which waited for: 5 -> 3; matrix products, arithmetic and copies ran while one was open for 0% -> 0% of each run, Pallas kernels for 11% -> 12%
where the time goes in v4:
time: 165 us; the launch traced here: 164 us
  waiting for transfers between devices  70.6 us (43%)
  blocking collectives  29.1 us (18%)
  starting transfers between devices  24.6 us (15%)
  Pallas kernels  24.5 us (15%)
  between operations  14.1 us (9%)
    all_to_all x1, waiting for transfers between devices, local(): lax.all_to_all(terms, 'owner', split_axis=0, concat_axis=0, tiled=True)  45 us
    all_gather x1, blocking collectives, local(): all_coef = lax.all_gather(compact, 'segment')  29.1 us
    all_to_all x1, waiting for transfers between devices, local(): lax.all_to_all(send_grads, 'owner', split_axis=0, concat_axis=0, tiled=True)  12.8 us
    all_to_all x1, waiting for transfers between devices, local(): lax.all_to_all(send_inputs, 'owner', split_axis=0, concat_axis=0, tiled=T...  12.1 us
    all_to_all x1, starting transfers between devices, local(): lax.all_to_all(send_grads, 'owner', split_axis=0, concat_axis=0, tiled=True)  11.6 us
    all_to_all x1, starting transfers between devices, local(): lax.all_to_all(terms, 'owner', split_axis=0, concat_axis=0, tiled=True)  7.21 us
    pallas_call x1, Pallas kernels, local(): pl.pallas_call(term_kernel, grid=(steps,), in_specs=[pl.BlockSpec(memory_...  6.17 us
    all_to_all x1, starting transfers between devices, local(): lax.all_to_all(send_inputs, 'owner', split_axis=0, concat_axis=0, tiled=T...  5.72 us
  transfers between devices with their start and end apart: 4, of which 3 were waited for; matrix products, arithmetic and copies ran while one was open for 0% of the time, Pallas kernels for 12%

profile of v4, /device:TPU:1, one launch (start us, length us, event | category | flops | bytes accessed | tf_op | source)
XLA Modules:
  0.0 163.6 jit_solution(9871582610238326309)
XLA Ops:
  7.2 0.0 all-gather.4.cloned.1.call-start
  7.2 0.7 all-gather.4.cloned.1.call-update
  7.9 2.5 %place_gradient.1 = (bf16[512,128]{1,0:T(8,128)(2,1)}, bf16[64,8,512]{2,1,0:T(8,128)(2,1)}) custom-call(s32[1,128]{1,0:T(1,128)} %bitcast.23, s32[1,64]{1,0:T(1,128)} %bitcast.24, bf16[128,1024]{1,0:T(8,128)(2,1)} %bitcast.21), custom_call_target="tpu_custom_call" | custom-call | tf_op jit(solution)/shard_map/place_gradient/pallas_call | solution.py:167
  10.4 11.6 %all-to-all-start = ((bf16[64,8,512]{2,1,0:T(8,128)(2,1)}), bf16[64,8,512]{2,1,0:T(8,128)(2,1)S(1)}, u32[]{:S(2)}, u32[]{:S(2)}) async-start(bf16[64,8,512]{2,1,0:T(8,128)(2,1)} %get-tuple-element.13), calls=%async_computation | async-start | bytes 1048576 | tf_op jit(solution)/shard_map/all_to_all | solution.py:172
  22.0 4.9 %place_inputs.1 = (bf16[64,8,2048]{2,1,0:T(8,128)(2,1)}, bf16[256,512]{1,0:T(8,128)(2,1)}) custom-call(bf16[512,128]{1,0:T(8,128)(2,1)} %get-tuple-element.11.placing_ref, bf16[128,4096]{1,0:T(8,128)(2,1)} %bitcast.15, bf16[128,4096]{1,0:T(8,128)(2,1)} %bitcast.16), custom_call_target="tpu_custom_call" | custom-call | tf_op jit(solution)/shard_map/place_inputs/pallas_call | solution.py:174
  26.9 12.8 %all-to-all-done.grad_ref.grads_ref = bf16[64,8,512]{2,1,0:T(8,128)(2,1)S(1)} async-done(((bf16[64,8,512]{2,1,0:T(8,128)(2,1)}), bf16[64,8,512]{2,1,0:T(8,128)(2,1)S(1)}, u32[]{:S(2)}, u32[]{:S(2)}) %all-to-all-start) | async-done | bytes 524320 | tf_op jit(solution)/shard_map/all_to_all | solution.py:172
  39.7 0.0 copy-start.1
  39.7 0.8 copy-done.1
  40.5 5.7 %all-to-all-start.2 = ((bf16[64,8,2048]{2,1,0:T(8,128)(2,1)}), bf16[64,8,2048]{2,1,0:T(8,128)(2,1)S(1)}, u32[]{:S(2)}, u32[]{:S(2)}) async-start(bf16[64,8,2048]{2,1,0:T(8,128)(2,1)} %get-tuple-element.15), calls=%async_computation.2 | async-start | bytes 4194304 | tf_op jit(solution)/shard_map/all_to_all | solution.py:196
  46.2 2.3 %coef.1 = (bf16[512,64]{1,0:T(8,128)(2,1)}, bf16[64,256]{1,0:T(8,128)(2,1)}) custom-call(bf16[64,8,512]{2,1,0:T(8,128)(2,1)} %copy-done.1, bf16[64,1024]{1,0:T(8,128)(2,1)} %bitcast.22), custom_call_target="tpu_custom_call" | custom-call | tf_op jit(solution)/shard_map/coef/pallas_call | solution.py:190
  48.5 29.1 %all-gather = bf16[512,256]{1,0:T(8,128)(2,1)} all-gather(bf16[64,256]{1,0:T(8,128)(2,1)} %get-tuple-element.14), channel_id=2, replica_groups=mesh['segment'=8,'owner'=64] {'segment'}, dimensions={0}, use_global_device_ids=true | all-gather | bytes 294912 | tf_op jit(solution)/shard_map/all_gather | solution.py:197
  77.7 0.0 all-gather.4.cloned.1.call-done.low_ref.high_ref
  77.7 6.2 %term.1 = bf16[64,8,2048]{2,1,0:T(8,128)(2,1)} custom-call(s32[1]{0:T(128)} %bitcast.4.place_ref, bf16[8,64,256]{2,1,0:T(8,128)(2,1)} %bitcast.19, bf16[512,4096]{1,0:T(8,128)(2,1)} %all-gather.4.cloned.1.call-done.low_ref.high_ref, bf16[512,4096]{1,0:T(8,128)(2,1)} %all-gather.4.cloned.1.call-done.low_ref.high_ref), custom_call_target="tpu_custom_call" | custom-call | tf_op jit(solution)/shard_map/term/pallas_call | solution.py:199
  83.8 12.1 %all-to-all-done.2.rows_ref = bf16[64,8,2048]{2,1,0:T(8,128)(2,1)S(1)} async-done(((bf16[64,8,2048]{2,1,0:T(8,128)(2,1)}), bf16[64,8,2048]{2,1,0:T(8,128)(2,1)S(1)}, u32[]{:S(2)}, u32[]{:S(2)}) %all-to-all-start.2) | async-done | bytes 2097184 | tf_op jit(solution)/shard_map/all_to_all | solution.py:196
  95.9 0.0 copy-start
  95.9 7.2 %all-to-all-start.1 = ((bf16[64,8,2048]{2,1,0:T(8,128)(2,1)}), bf16[64,8,2048]{2,1,0:T(8,128)(2,1)}, u32[]{:S(2)}, u32[]{:S(2)}) async-start(bf16[64,8,2048]{2,1,0:T(8,128)(2,1)} %term.1), calls=%async_computation.1 | async-start | bytes 4194304 | tf_op jit(solution)/shard_map/all_to_all | solution.py:213
  103.1 0.0 copy-done
  103.1 4.5 %weight_gradient.1 = (f32[64,4096]{1,0:T(8,128)}, f32[64,1024]{1,0:T(8,128)}) custom-call(bf16[64,8,2048]{2,1,0:T(8,128)(2,1)} %copy-done, bf16[64,8,512]{2,1,0:T(8,128)(2,1)} %copy-done.1, bf16[512,64]{1,0:T(8,128)(2,1)} %get-tuple-element.16.coef_ref, bf16[64,4096]{1,0:T(8,128)(2,1)} %bitcast.18), custom_call_target="tpu_custom_call" | custom-call | tf_op jit(solution)/shard_map/weight_gradient/pallas_call | solution.py:215
  107.7 45.0 %all-to-all-done.1.rows_ref = bf16[64,8,2048]{2,1,0:T(8,128)(2,1)} async-done(((bf16[64,8,2048]{2,1,0:T(8,128)(2,1)}), bf16[64,8,2048]{2,1,0:T(8,128)(2,1)}, u32[]{:S(2)}, u32[]{:S(2)}) %all-to-all-start.1) | async-done | bytes 2097184 | tf_op jit(solution)/shard_map/all_to_all | solution.py:213
  152.7 4.1 %unplace.1 = bf16[128,4096]{1,0:T(8,128)(2,1)} custom-call(bf16[256,512]{1,0:T(8,128)(2,1)} %get-tuple-element.12.back_ref, bf16[64,8,2048]{2,1,0:T(8,128)(2,1)} %all-to-all-done.1.rows_ref), custom_call_target="tpu_custom_call" | custom-call | tf_op jit(solution)/shard_map/unplace/pallas_call | solution.py:221
Async XLA Ops:
  7.2 70.5 %all-gather.4.cloned.1.call-start = ((), (), s32[]{:S(2)}) async-start(), calls=%async_computation.3 | async-start | bytes 4718592 | tf_op jit(solution)/shard_map/all_gather | solution.py:165
  10.4 29.3 %all-to-all-start = ((bf16[64,8,512]{2,1,0:T(8,128)(2,1)}), bf16[64,8,512]{2,1,0:T(8,128)(2,1)S(1)}, u32[]{:S(2)}, u32[]{:S(2)}) async-start(bf16[64,8,512]{2,1,0:T(8,128)(2,1)} %get-tuple-element.13), calls=%async_computation | async-start | bytes 1048576 | tf_op jit(solution)/shard_map/all_to_all | solution.py:172
  39.7 0.8 copy-start.1
  40.5 55.4 %all-to-all-start.2 = ((bf16[64,8,2048]{2,1,0:T(8,128)(2,1)}), bf16[64,8,2048]{2,1,0:T(8,128)(2,1)S(1)}, u32[]{:S(2)}, u32[]{:S(2)}) async-start(bf16[64,8,2048]{2,1,0:T(8,128)(2,1)} %get-tuple-element.15), calls=%async_computation.2 | async-start | bytes 4194304 | tf_op jit(solution)/shard_map/all_to_all | solution.py:196
  95.9 7.2 %copy-start = (bf16[64,8,2048]{2,1,0:T(8,128)(2,1)}, bf16[64,8,2048]{2,1,0:T(8,128)(2,1)S(1)}, u32[]{:S(2)}) copy-start(bf16[64,8,2048]{2,1,0:T(8,128)(2,1)S(1)} %all-to-all-done.2.rows_ref) | copy-start | bytes 6291460
  95.9 56.8 %all-to-all-start.1 = ((bf16[64,8,2048]{2,1,0:T(8,128)(2,1)}), bf16[64,8,2048]{2,1,0:T(8,128)(2,1)}, u32[]{:S(2)}, u32[]{:S(2)}) async-start(bf16[64,8,2048]{2,1,0:T(8,128)(2,1)} %term.1), calls=%async_computation.1 | async-start | bytes 4194304 | tf_op jit(solution)/shard_map/all_to_all | solution.py:213
Sparse Core Ops, SparseCore 0:
  10.1 65.3 all-gather.3

commit v5 on v4

--- a/solution.py
+++ b/solution.py
@@ -8,6 +8,10 @@
 adapter_scale = 2.0
 row_limit = 4
 group = 2 * row_limit
+banks = 8
+members = 8
+bank_slots = 23
+lines = 2 * bank_slots + 2
 f32 = jnp.float32
 bf16 = jnp.bfloat16
 
@@ -45,20 +49,91 @@
     send_ref[...] = sent.astype(bf16).reshape(send_ref.shape)
 
 
-def place_inputs_kernel(placing_ref, low_ref, high_ref, send_ref, back_ref):
+def place_inputs_kernel(placing_ref, low_ref, high_ref, send_ref):
     placing = placing_ref[...]
     half = half_of(placing.shape)
     zero = jnp.zeros_like(placing)
     lower = jnp.where(half == 0, placing, zero)
     upper = jnp.where(half == 1, placing, zero)
+    sent = dot(lower, low_ref[...], ((1,), (0,))) + dot(upper, high_ref[...], ((1,), (0,)))
+    send_ref[...] = sent.astype(bf16).reshape(send_ref.shape)
+
+
+def place_banks_kernel(tenant_ref, owner_ref, placing_ref, low_ref, high_ref, send_ref, back_ref, pick_ref, code_ref):
+    tok_rows = tenant_ref.shape[1]
+    owners = owner_ref.shape[1]
+    total = banks * lines
+    block = low_ref.shape[1]
+    step = pl.program_id(0)
+
+    @pl.when(step == 0)
+    def _():
+        placing = placing_ref[...].astype(f32)
+        half = half_of(placing.shape)
+        back_ref[:tok_rows] = jnp.where(half == 0, placing, 0.0).T.astype(bf16)
+        back_ref[tok_rows:] = jnp.where(half == 1, placing, 0.0).T.astype(bf16)
+        named = iota((owners, tok_rows), 0) == tenant_ref[...]
+        named_bf16 = named.astype(bf16)
+        before = (iota((tok_rows, tok_rows), 0) < iota((tok_rows, tok_rows), 1)).astype(bf16)
+        in_bank = dot((iota((banks, owners), 0) == owner_ref[...] // members).astype(bf16), named_bf16, ((1,), (0,)))
+        bank_rank = dot(in_bank.astype(bf16), before, ((1,), (0,)))
+        key = in_bank * (bank_rank + 1.0)
+        most = jnp.max(key)
+        slot = jnp.sum(key, axis=0, keepdims=True) - 1.0
+        rank = dot(named_bf16, before, ((1,), (0,)))
+        place = jnp.sum(jnp.where(named, rank, 0.0), axis=0, keepdims=True)
+        member = jnp.broadcast_to((owner_ref[...] % members).astype(f32), (banks, owners)).astype(bf16)
+        member = dot(member, named_bf16, ((1,), (0,)))
+        code = in_bank * (member * row_limit + place + 1.0)
+        line = iota((tok_rows, tok_rows), 0)
+        mine = ((line % bank_slots).astype(f32) == slot) & (line < 2 * bank_slots)
+        codes = dot(code.astype(bf16), mine.astype(bf16), ((1,), (1,)))
+        spread = (iota((total, banks), 0) // lines == iota((total, banks), 1)).astype(bf16)
+        wide_key = dot(spread, key.astype(bf16), ((1,), (0,)))
+        line = iota((total, tok_rows), 0) % lines
+        pick = (wide_key == (line % bank_slots + 1).astype(f32)) & (line < 2 * bank_slots)
+        pick_ref[0] = jnp.where(pick & (line < bank_slots), 1.0, 0.0).astype(bf16)
+        pick_ref[1] = jnp.where(pick & (line >= bank_slots), 1.0, 0.0).astype(bf16)
+        wide_code = dot(spread, codes.astype(bf16), ((1,), (0,)))
+        code_ref[...] = jnp.where(line == lines - 2, wide_code, jnp.where(line == lines - 1, most, 0.0))
+
+    sent = dot(pick_ref[0], low_ref[...], ((1,), (0,))) + dot(pick_ref[1], high_ref[...], ((1,), (0,)))
+    send_ref[...] = sent.astype(bf16).reshape(send_ref.shape)
+
+    @pl.when(step == 0)
+    def _():
+        first = sent[:, :tok_rows] + code_ref[...]
+        send_ref[:, :, :tok_rows] = first.astype(bf16).reshape(banks, lines, tok_rows)
+
+
+def route_kernel(member_ref, rows_ref, *refs):
+    outs, pick_ref, most_ref = refs[:members], refs[members], refs[members + 1]
+    block = rows_ref.shape[2]
+    rows = members * group
 
     @pl.when(pl.program_id(0) == 0)
     def _():
-        back_ref[: lower.shape[1]] = lower.astype(f32).T.astype(bf16)
-        back_ref[lower.shape[1] :] = upper.astype(f32).T.astype(bf16)
-
-    sent = dot(lower, low_ref[...], ((1,), (0,))) + dot(upper, high_ref[...], ((1,), (0,)))
-    send_ref[...] = sent.astype(bf16).reshape(send_ref.shape)
+        x, core = member_ref[0] // 2, member_ref[0] % 2
+        row, line = iota((rows, lines), 0), iota((rows, lines), 1)
+        t = row // group
+        to = (x + t // 2) % 4 * 2 + (core + t) % 2
+        want = (to * row_limit + row % row_limit + 1).astype(f32)
+        same_half = (row // row_limit) % 2 == line // bank_slots
+        most = jnp.zeros((1, 128), f32)
+        for y in range(banks):
+            tail = rows_ref[y, :, :128].astype(f32)
+            codes = tail[lines - 2 : lines - 1, :lines]
+            most = jnp.maximum(most, tail[lines - 1 :, :])
+            pick_ref[y] = jnp.where((want == codes) & same_half, 1.0, 0.0).astype(bf16)
+        most_ref[...] = jnp.broadcast_to(most, most_ref.shape)
+
+    for y in range(banks):
+        part = dot(pick_ref[y], rows_ref[y], ((1,), (0,))).astype(bf16).reshape(members, group, block)
+        for t in range(members):
+            outs[t][y] = part[t]
+    most = jnp.broadcast_to(most_ref[:, :1], (group, block)).astype(bf16)
+    for t in range(members):
+        outs[t][banks] = most
 
 
 def both_halves(x):
@@ -89,7 +164,8 @@
         place = place_ref[0]
         parts = []
         for k in range(sections):
-            parts.append(jnp.where(place <= k, coef_ref[k], jnp.zeros_like(coef_ref[k])))
+            part = coef_ref[jnp.bitwise_xor(place, k)]
+            parts.append(jnp.where(place <= k, part, jnp.zeros_like(part)))
         shape = (columns, wide_ref.shape[0])
         column, row = iota(shape, 0), iota(shape, 1)
         same = column == row // group * row_limit + row % row_limit
@@ -104,15 +180,11 @@
     out_ref[...] = out.astype(bf16).reshape(out_ref.shape)
 
 
-def weight_gradient_kernel(rows_ref, grads_ref, coef_ref, down_ref, grad_down_ref, grad_up_ref):
-    slots = coef_ref.shape[0]
-    rank = coef_ref.shape[1]
-    width = rows_ref.shape[2]
-    out_width = grads_ref.shape[2]
-    rows = rows_ref[...].reshape(slots, width)
-    grads = grads_ref[...].reshape(slots, out_width)
-    half = half_of((slots, rank))
-    coef = coef_ref[...]
+def gradients(rows, grads, coef, down_ref, grad_down_ref, grad_up_ref):
+    rank = coef.shape[1]
+    width = rows.shape[1]
+    out_width = grads.shape[1]
+    half = half_of(coef.shape)
     zero = jnp.zeros_like(coef)
     pair = jnp.concatenate([jnp.where(half == 0, coef, zero), jnp.where(half == 1, coef, zero)], axis=1)
     down = dot(pair, rows, ((0,), (0,)))
@@ -125,6 +197,32 @@
     up = dot(pair, grads, ((0,), (0,)))
     grad_up_ref[:, :out_width] = up[:rank]
     grad_up_ref[:, out_width:] = up[rank:]
+
+
+def weight_gradient_kernel(rows_ref, grads_ref, coef_ref, down_ref, grad_down_ref, grad_up_ref):
+    slots = coef_ref.shape[0]
+    rows = rows_ref[...].reshape(slots, rows_ref.shape[2])
+    grads = grads_ref[...].reshape(slots, grads_ref.shape[2])
+    gradients(rows, grads, coef_ref[...], down_ref, grad_down_ref, grad_up_ref)
+
+
+def bank_gradient_kernel(member_ref, grads_ref, coef_ref, down_ref, *refs):
+    blocks, (grad_down_ref, grad_up_ref, most_ref) = refs[:members], refs[members:]
+    rank = coef_ref.shape[3]
+    out_width = grads_ref.shape[3]
+    width = down_ref.shape[1] // 2
+    x, core = member_ref[0] // 2, member_ref[0] % 2
+    rows, coef, grads = [], [], []
+    most = jnp.zeros((group, 128), f32)
+    for t in range(members):
+        source = (x + 4 - t // 2) % 4 * 2 + (core + t) % 2
+        rows.append(blocks[t][:banks].reshape(banks * group, width))
+        coef.append(coef_ref[:, pl.ds(source, 1)].reshape(banks * group, rank))
+        grads.append(grads_ref[:, pl.ds(source, 1)].reshape(banks * group, out_width))
+        most = jnp.maximum(most, blocks[t][banks, :, :128].astype(f32))
+    most_ref[0] = jnp.max(most).astype(jnp.int32)
+    rows, coef, grads = (jnp.concatenate(part, axis=0) for part in (rows, coef, grads))
+    gradients(rows, grads, coef, down_ref, grad_down_ref, grad_up_ref)
 
 
 def unplace_kernel(back_ref, rows_ref, out_ref):
@@ -164,28 +262,35 @@
 
     all_down = lax.all_gather(down_factor, "segment").reshape(sections * rank, width)
 
+    owner_row = adapter_owner_index.reshape(1, owners)
+    tenant_row = tenant.reshape(1, tok_rows)
+    member = (lax.axis_index("owner") % members).astype(jnp.int32).reshape(1)
+
     placing, send_grads = pl.pallas_call(
         place_gradient_kernel,
         out_shape=(shape((slots, tok_rows), bf16), shape((owners, group, out_width // 2), bf16)),
         name="place_gradient",
-    )(tenant.reshape(1, tok_rows), adapter_owner_index.reshape(1, owners), gradient_list)
+    )(tenant_row, owner_row, gradient_list)
     recv_grads = lax.all_to_all(send_grads, "owner", split_axis=0, concat_axis=0, tiled=True)
 
-    send_inputs, back = pl.pallas_call(
-        place_inputs_kernel,
+    send_banks, back = pl.pallas_call(
+        place_banks_kernel,
         grid=(steps,),
         in_specs=[
+            pl.BlockSpec((1, tok_rows), lambda c: (0, 0)),
+            pl.BlockSpec((1, owners), lambda c: (0, 0)),
             pl.BlockSpec((slots, tok_rows), lambda c: (0, 0)),
             pl.BlockSpec((tok_rows, block), lambda c: (0, c)),
             pl.BlockSpec((tok_rows, block), lambda c: (0, c + steps)),
         ],
         out_specs=(
-            pl.BlockSpec((owners, group, block), lambda c: (0, 0, c)),
+            pl.BlockSpec((banks, lines, block), lambda c: (0, 0, c)),
             pl.BlockSpec((2 * tok_rows, slots), lambda c: (0, 0)),
         ),
-        out_shape=(shape((owners, group, half_width), bf16), shape((2 * tok_rows, slots), bf16)),
-        name="place_inputs",
-    )(placing, inputs, inputs)
+        out_shape=(shape((banks, lines, half_width), bf16), shape((2 * tok_rows, slots), bf16)),
+        scratch_shapes=[pltpu.VMEM((2, banks * lines, tok_rows), bf16), pltpu.VMEM((banks * lines, tok_rows), f32)],
+        name="place_banks",
+    )(tenant_row, owner_row, placing, inputs, inputs)
 
     coef, compact = pl.pallas_call(
         coef_kernel,
@@ -193,8 +298,15 @@
         name="coef",
     )(recv_grads, up_factor)
 
-    recv_inputs = lax.all_to_all(send_inputs, "owner", split_axis=0, concat_axis=0, tiled=True)
-    all_coef = lax.all_gather(compact, "segment")
+    same_member = [[y * members + m for y in range(banks)] for m in range(members)]
+    recv_banks = lax.all_to_all(
+        send_banks, "owner", split_axis=0, concat_axis=0, axis_index_groups=same_member, tiled=True
+    )
+    all_coef = compact[None]
+    while all_coef.shape[0] < sections:
+        apart = all_coef.shape[0]
+        other = lax.ppermute(all_coef, "segment", [(i, i ^ apart) for i in range(sections)])
+        all_coef = jnp.concatenate([all_coef, other], axis=0)
 
     terms = pl.pallas_call(
         term_kernel,
@@ -212,11 +324,71 @@
     )(place, all_coef, all_down, all_down)
     returned = lax.all_to_all(terms, "owner", split_axis=0, concat_axis=0, tiled=True)
 
-    grad_down, grad_up = pl.pallas_call(
-        weight_gradient_kernel,
-        out_shape=(shape((rank, width), f32), shape((rank, out_width), f32)),
-        name="weight_gradient",
-    )(recv_inputs, recv_grads, coef, down_factor)
+    sent_blocks = pl.pallas_call(
+        route_kernel,
+        grid=(steps,),
+        in_specs=[
+            pl.BlockSpec(memory_space=pltpu.SMEM),
+            pl.BlockSpec((banks, lines, block), lambda c: (0, 0, c)),
+        ],
+        out_specs=[pl.BlockSpec((banks + 1, group, block), lambda c: (0, 0, c))] * members,
+        out_shape=[shape((banks + 1, group, half_width), bf16)] * members,
+        scratch_shapes=[pltpu.VMEM((banks, members * group, lines), bf16), pltpu.VMEM((group, 128), f32)],
+        name="route",
+    )(member, recv_banks)
+    got_blocks = [sent_blocks[0]]
+    for t in range(1, members):
+        pairs = []
+        for i in range(owners):
+            y, x, core = i // members, i % members // 2, i % 2
+            pairs.append((i, y * members + (x + t // 2) % 4 * 2 + (core + t) % 2))
+        got_blocks.append(lax.ppermute(sent_blocks[t], "owner", pairs))
+
+    smem = pl.BlockSpec(memory_space=pltpu.SMEM)
+    vmem = pl.BlockSpec(memory_space=pltpu.VMEM)
+    grad_down, grad_up, most = pl.pallas_call(
+        bank_gradient_kernel,
+        in_specs=[smem] + [vmem] * (3 + members),
+        out_specs=(vmem, vmem, smem),
+        out_shape=(shape((rank, width), f32), shape((rank, out_width), f32), shape((1,), jnp.int32)),
+        name="bank_gradient",
+    )(
+        member,
+        recv_grads.reshape(banks, members, group, out_width // 2),
+        coef.reshape(banks, members, group, rank),
+        down_factor,
+        *got_blocks,
+    )
+
+    def direct(grad_down, grad_up, placing, inputs, recv_grads, coef, down_factor):
+        send_inputs = pl.pallas_call(
+            place_inputs_kernel,
+            grid=(steps,),
+            in_specs=[
+                pl.BlockSpec((slots, tok_rows), lambda c: (0, 0)),
+                pl.BlockSpec((tok_rows, block), lambda c: (0, c)),
+                pl.BlockSpec((tok_rows, block), lambda c: (0, c + steps)),
+            ],
+            out_specs=pl.BlockSpec((owners, group, block), lambda c: (0, 0, c)),
+            out_shape=shape((owners, group, half_width), bf16),
+            name="place_inputs",
+        )(placing, inputs, inputs)
+        recv_inputs = lax.all_to_all(send_inputs, "owner", split_axis=0, concat_axis=0, tiled=True)
+        return tuple(
+            pl.pallas_call(
+                weight_gradient_kernel,
+                out_shape=(shape((rank, width), f32), shape((rank, out_width), f32)),
+                name="weight_gradient",
+            )(recv_inputs, recv_grads, coef, down_factor)
+        )
+
+    def kept(grad_down, grad_up, *rest):
+        return grad_down, grad_up
+
+    grad_down, grad_up, most, returned = lax.optimization_barrier((grad_down, grad_up, most, returned))
+    grad_down, grad_up = lax.cond(
+        most[0] > bank_slots, direct, kept, grad_down, grad_up, placing, inputs, recv_grads, coef, down_factor
+    )
 
     passed = pl.pallas_call(
         unplace_kernel,

time: 165 us -> 179 us (1.085)
  starting transfers between devices: 24.6 us -> 71.9 us
  blocking collectives: 29.1 us -> 0 us
  waiting for transfers between devices: 70.6 us -> 57.3 us
  other arithmetic: 0 us -> 3.83 us
  Pallas kernels: 24.5 us -> 27.9 us
    all_to_all x1, waiting for transfers between devices: 45 us -> 0.01 us  [local(): lax.all_to_all(terms, 'owner', split_axis=0, concat_axis=0, tiled=True)]
    ppermute x0 -> x10, waiting for transfers between devices: none -> 43.1 us  [the longest x7 29.7 us: local(): got_blocks.append(lax.ppermute(sent_blocks[t], 'owner', pairs))]
    ppermute x0 -> x10, starting transfers between devices: none -> 42.9 us  [the longest x7 24.4 us: local(): got_blocks.append(lax.ppermute(sent_blocks[t], 'owner', pairs))]
    all_gather x1 -> x0, blocking collectives: 29.1 us -> none  [local(): all_coef = lax.all_gather(compact, 'segment')]
    all_to_all x1, waiting for transfers between devices: 12.1 us -> 0.01 us  [local(): lax.all_to_all(send_banks, 'owner', split_axis=0, concat_axis=0, axis_ind...]
    all_to_all x1, starting transfers between devices: 7.21 us -> 13.8 us  [local(): lax.all_to_all(terms, 'owner', split_axis=0, concat_axis=0, tiled=True)]
    concatenate x0 -> x3, other arithmetic: none -> 3.83 us  [local(): all_coef = jnp.concatenate([all_coef, other], axis=0)]
    pallas_call x2 -> x3, Pallas kernels: 9.48 us -> 13 us  [the longest x1 4.55 us: local(): pl.pallas_call(bank_gradient_kernel, in_specs=[smem] + [vmem] * (3 + memb...]
  transfers between devices with their start and end apart: 4 -> 14, of which waited for: 3 -> 8; matrix products, arithmetic and copies ran while one was open for 0% -> 2% of each run, Pallas kernels for 12% -> 13%
where the time goes in v5:
time: 179 us; the launch traced here: 178 us
  starting transfers between devices  71.9 us (40%)
  waiting for transfers between devices  57.3 us (32%)
  Pallas kernels  27.9 us (16%)
  between operations  14.8 us (8%)
  other arithmetic  3.83 us (2%)
  local copies, waits for them, and re-layouts  1.98 us (1%)
    ppermute x7, waiting for transfers between devices, local(): got_blocks.append(lax.ppermute(sent_blocks[t], 'owner', pairs))  29.7 us
    ppermute x7, starting transfers between devices, local(): got_blocks.append(lax.ppermute(sent_blocks[t], 'owner', pairs))  24.4 us
    ppermute x3, starting transfers between devices, local(): lax.ppermute(all_coef, 'segment', [(i, i ^ apart) for i in range(sections)])  18.6 us
    all_to_all x1, starting transfers between devices, local(): lax.all_to_all(terms, 'owner', split_axis=0, concat_axis=0, tiled=True)  13.8 us
    all_to_all x1, waiting for transfers between devices, local(): lax.all_to_all(send_grads, 'owner', split_axis=0, concat_axis=0, tiled=True)  13.5 us
    ppermute x3, waiting for transfers between devices, local(): lax.ppermute(all_coef, 'segment', [(i, i ^ apart) for i in range(sections)])  13.5 us
    all_to_all x1, starting transfers between devices, local(): lax.all_to_all(send_grads, 'owner', split_axis=0, concat_axis=0, tiled=True)  11.6 us
    pallas_call x1, Pallas kernels, local(): pl.pallas_call(term_kernel, grid=(steps,), in_specs=[pl.BlockSpec(memory_...  6.15 us
  transfers between devices with their start and end apart: 14, of which 8 were waited for; matrix products, arithmetic and copies ran while one was open for 2% of the time, Pallas kernels for 13%

profile of v5, /device:TPU:1, one launch (start us, length us, event | category | flops | bytes accessed | tf_op | source)
XLA Modules:
  0.0 177.7 jit_solution(17163505323479080152)
XLA Ops:
  7.9 2.5 %place_gradient.1 = (bf16[512,128]{1,0:T(8,128)(2,1)S(1)}, bf16[64,8,512]{2,1,0:T(8,128)(2,1)}) custom-call(s32[1,128]{1,0:T(1,128)} %bitcast.34, s32[1,64]{1,0:T(1,128)} %bitcast.36, bf16[128,1024]{1,0:T(8,128)(2,1)} %bitcast.32), custom_call_target="tpu_custom_call" | custom-call | tf_op jit(solution)/shard_map/place_gradient/pallas_call | solution.py:269
  10.4 11.6 %all-to-all-start.1 = ((bf16[64,8,512]{2,1,0:T(8,128)(2,1)}), bf16[64,8,512]{2,1,0:T(8,128)(2,1)S(1)}, u32[]{:S(2)}, u32[]{:S(2)}) async-start(bf16[64,8,512]{2,1,0:T(8,128)(2,1)} %get-tuple-element.61), calls=%async_computation.1 | async-start | bytes 1048576 | tf_op jit(solution)/shard_map/all_to_all | solution.py:274
  22.0 4.2 %place_banks.1 = (bf16[8,48,2048]{2,1,0:T(8,128)(2,1)}, bf16[256,512]{1,0:T(8,128)(2,1)}) custom-call(s32[1,128]{1,0:T(1,128)} %bitcast.35, s32[1,64]{1,0:T(1,128)} %bitcast.37, bf16[512,128]{1,0:T(8,128)(2,1)S(1)} %get-tuple-element.59.placing_ref, bf16[128,4096]{1,0:T(8,128)(2,1)S(1)} %bitcast.19, bf16[128,4096]{1,0:T(8,128)(2,1)S(1)} %bitcast.20), custom_call_target="tpu_custom_call" | custom-call | tf_op jit(solution)/shard_map/place_banks/pallas_call | solution.py:276
  26.2 13.5 %all-to-all-done.1.grad_ref = bf16[64,8,512]{2,1,0:T(8,128)(2,1)S(1)} async-done(((bf16[64,8,512]{2,1,0:T(8,128)(2,1)}), bf16[64,8,512]{2,1,0:T(8,128)(2,1)S(1)}, u32[]{:S(2)}, u32[]{:S(2)}) %all-to-all-start.1) | async-done | bytes 524320 | tf_op jit(solution)/shard_map/all_to_all | solution.py:274
  39.7 3.6 %all-to-all-start.2 = ((bf16[8,48,2048]{2,1,0:T(8,128)(2,1)}), bf16[8,48,2048]{2,1,0:T(8,128)(2,1)S(1)}, u32[]{:S(2)}, u32[]{:S(2)}) async-start(bf16[8,48,2048]{2,1,0:T(8,128)(2,1)} %get-tuple-element.63), calls=%async_computation.2 | async-start | bytes 3145728 | tf_op jit(solution)/shard_map/all_to_all | solution.py:302
  43.3 2.2 %coef.1 = (bf16[512,64]{1,0:T(8,128)(2,1)S(1)}, bf16[64,256]{1,0:T(8,128)(2,1)}) custom-call(bf16[64,8,512]{2,1,0:T(8,128)(2,1)S(1)} %all-to-all-done.1.grad_ref, bf16[64,1024]{1,0:T(8,128)(2,1)} %bitcast.33), custom_call_target="tpu_custom_call" | custom-call | tf_op jit(solution)/shard_map/coef/pallas_call | solution.py:295
  45.5 4.0 %collective-permute-start.7 = (bf16[1,64,256]{2,1,0:T(8,128)(2,1)}, bf16[1,64,256]{2,1,0:T(8,128)(2,1)S(1)}, u32[]{:S(2)}, u32[]{:S(2)}) collective-permute-start(bf16[1,64,256]{2,1,0:T(8,128)(2,1)} %bitcast.28), channel_id=1, source_target_pairs={{0,64},{64,0},{128,192},{192,128},{256,320},{320,256},{384,448},{4... | collective-permute-start | bytes 98312 | tf_op jit(solution)/shard_map/ppermute | solution.py:308
  49.4 2.6 %collective-permute-done.7 = bf16[1,64,256]{2,1,0:T(8,128)(2,1)S(1)} collective-permute-done((bf16[1,64,256]{2,1,0:T(8,128)(2,1)}, bf16[1,64,256]{2,1,0:T(8,128)(2,1)S(1)}, u32[]{:S(2)}, u32[]{:S(2)}) %collective-permute-start.7) | collective-permute-done | bytes 32800 | tf_op jit(solution)/shard_map/ppermute | solution.py:308
  52.8 5.8 %collective-permute-start.8 = (bf16[2,64,256]{2,1,0:T(8,128)(2,1)S(1)}, bf16[2,64,256]{2,1,0:T(8,128)(2,1)S(1)}, u32[]{:S(2)}, u32[]{:S(2)}) collective-permute-start(bf16[2,64,256]{2,1,0:T(8,128)(2,1)S(1)} %pad_maximum_fusion.2), channel_id=1, source_target_pairs={{0,128},{64,192},{128,0},{192,64},{256,384},{320,448},{384,256},{4... | collective-permute-start | bytes 196616 | tf_op jit(solution)/shard_map/ppermute | solution.py:308
  58.6 3.8 %collective-permute-done.8 = bf16[2,64,256]{2,1,0:T(8,128)(2,1)S(1)} collective-permute-done((bf16[2,64,256]{2,1,0:T(8,128)(2,1)S(1)}, bf16[2,64,256]{2,1,0:T(8,128)(2,1)S(1)}, u32[]{:S(2)}, u32[]{:S(2)}) %collective-permute-start.8) | collective-permute-done | bytes 65568 | tf_op jit(solution)/shard_map/ppermute | solution.py:308
  62.4 1.4 pad_maximum_fusion.1
  63.8 8.8 %collective-permute-start.9 = (bf16[4,64,256]{2,1,0:T(8,128)(2,1)}, bf16[4,64,256]{2,1,0:T(8,128)(2,1)}, u32[]{:S(2)}, u32[]{:S(2)}) collective-permute-start(bf16[4,64,256]{2,1,0:T(8,128)(2,1)} %pad_maximum_fusion.1), channel_id=1, source_target_pairs={{0,256},{64,320},{128,384},{192,448},{256,0},{320,64},{384,128},{4... | collective-permute-start | bytes 393224 | tf_op jit(solution)/shard_map/ppermute | solution.py:308
  72.6 7.1 %collective-permute-done.9 = bf16[4,64,256]{2,1,0:T(8,128)(2,1)} collective-permute-done((bf16[4,64,256]{2,1,0:T(8,128)(2,1)}, bf16[4,64,256]{2,1,0:T(8,128)(2,1)}, u32[]{:S(2)}, u32[]{:S(2)}) %collective-permute-start.9) | collective-permute-done | bytes 131104 | tf_op jit(solution)/shard_map/ppermute | solution.py:308
  79.7 1.6 pad_maximum_fusion.coef_ref
  81.4 6.2 %term.1 = bf16[64,8,2048]{2,1,0:T(8,128)(2,1)} custom-call(s32[1]{0:T(128)} %bitcast.10.place_ref, bf16[8,64,256]{2,1,0:T(8,128)(2,1)} %pad_maximum_fusion.coef_ref, bf16[512,4096]{1,0:T(8,128)(2,1)} %all-gather.3.cloned.1.call-done.low_ref.high_ref, bf16[512,4096]{1,0:T(8,128)(2,1)} %all-gather.3.cloned.1.call-done.low_ref.high_ref), custom_call_target="tpu_custom_call" | custom-call | tf_op jit(solution)/shard_map/term/pallas_call | solution.py:311
  87.5 1.2 copy-done.4
  88.7 13.8 %all-to-all-start.3 = ((bf16[64,8,2048]{2,1,0:T(8,128)(2,1)}), bf16[64,8,2048]{2,1,0:T(8,128)(2,1)S(1)}, u32[]{:S(2)}, u32[]{:S(2)}) async-start(bf16[64,8,2048]{2,1,0:T(8,128)(2,1)} %term.1), calls=%async_computation.3 | async-start | bytes 4194304 | tf_op jit(solution)/shard_map/all_to_all | solution.py:325
  102.5 4.3 %route.1 = (bf16[9,8,2048]{2,1,0:T(8,128)(2,1)}, bf16[9,8,2048]{2,1,0:T(8,128)(2,1)}, bf16[9,8,2048]{2,1,0:T(8,128)(2,1)}, bf16[9,8,2048]{2,1,0:T(8,128)(2,1)}, ...) custom-call(s32[1]{0:T(128)} %bitcast.4.member_ref, ...), custom_call_target="tpu_custom_call" | custom-call | tf_op jit(solution)/shard_map/route/pallas_call | solution.py:327
  106.7 2.4 %collective-permute-start = (bf16[9,8,2048]{2,1,0:T(8,128)(2,1)}, bf16[9,8,2048]{2,1,0:T(8,128)(2,1)}, u32[]{:S(2)}, u32[]{:S(2)}) collective-permute-start(bf16[9,8,2048]{2,1,0:T(8,128)(2,1)} %get-tuple-element.65), channel_id=1, source_target_pairs={{0,1},{1,0},{2,3},{3,2},{4,5},{5,4},{6,7},{7,6},{8,9},{9,8},{10,11... | collective-permute-start | bytes 884744 | tf_op jit(solution)/shard_map/ppermute | solution.py:345
  109.1 3.2 %collective-permute-start.1 = (bf16[9,8,2048]{2,1,0:T(8,128)(2,1)}, bf16[9,8,2048]{2,1,0:T(8,128)(2,1)}, u32[]{:S(2)}, u32[]{:S(2)}) collective-permute-start(bf16[9,8,2048]{2,1,0:T(8,128)(2,1)} %get-tuple-element.66), channel_id=1, source_target_pairs={{0,2},{1,3},{2,4},{3,5},{4,6},{5,7},{6,0},{7,1},{8,10},{9,11},{10,... | collective-permute-start | bytes 884744 | tf_op jit(solution)/shard_map/ppermute | solution.py:345
  112.3 3.4 %collective-permute-start.2 = (bf16[9,8,2048]{2,1,0:T(8,128)(2,1)}, bf16[9,8,2048]{2,1,0:T(8,128)(2,1)}, u32[]{:S(2)}, u32[]{:S(2)}) collective-permute-start(bf16[9,8,2048]{2,1,0:T(8,128)(2,1)} %get-tuple-element.67), channel_id=1, source_target_pairs={{0,3},{1,2},{2,5},{3,4},{4,7},{5,6},{6,1},{7,0},{8,11},{9,10},{10,... | collective-permute-start | bytes 884744 | tf_op jit(solution)/shard_map/ppermute | solution.py:345
  115.7 3.2 %collective-permute-start.3 = (bf16[9,8,2048]{2,1,0:T(8,128)(2,1)}, bf16[9,8,2048]{2,1,0:T(8,128)(2,1)}, u32[]{:S(2)}, u32[]{:S(2)}) collective-permute-start(bf16[9,8,2048]{2,1,0:T(8,128)(2,1)} %get-tuple-element.68), channel_id=1, source_target_pairs={{0,4},{1,5},{2,6},{3,7},{4,0},{5,1},{6,2},{7,3},{8,12},{9,13},{10,... | collective-permute-start | bytes 884744 | tf_op jit(solution)/shard_map/ppermute | solution.py:345
  118.9 3.8 %collective-permute-start.4 = (bf16[9,8,2048]{2,1,0:T(8,128)(2,1)}, bf16[9,8,2048]{2,1,0:T(8,128)(2,1)}, u32[]{:S(2)}, u32[]{:S(2)}) collective-permute-start(bf16[9,8,2048]{2,1,0:T(8,128)(2,1)} %get-tuple-element.69), channel_id=1, source_target_pairs={{0,5},{1,4},{2,7},{3,6},{4,1},{5,0},{6,3},{7,2},{8,13},{9,12},{10,... | collective-permute-start | bytes 884744 | tf_op jit(solution)/shard_map/ppermute | solution.py:345
  122.8 3.4 %collective-permute-start.5 = (bf16[9,8,2048]{2,1,0:T(8,128)(2,1)}, bf16[9,8,2048]{2,1,0:T(8,128)(2,1)}, u32[]{:S(2)}, u32[]{:S(2)}) collective-permute-start(bf16[9,8,2048]{2,1,0:T(8,128)(2,1)} %get-tuple-element.70), channel_id=1, source_target_pairs={{0,6},{1,7},{2,0},{3,1},{4,2},{5,3},{6,4},{7,5},{8,14},{9,15},{10,... | collective-permute-start | bytes 884744 | tf_op jit(solution)/shard_map/ppermute | solution.py:345
  126.2 5.0 %collective-permute-start.6 = (bf16[9,8,2048]{2,1,0:T(8,128)(2,1)}, bf16[9,8,2048]{2,1,0:T(8,128)(2,1)}, u32[]{:S(2)}, u32[]{:S(2)}) collective-permute-start(bf16[9,8,2048]{2,1,0:T(8,128)(2,1)} %get-tuple-element.71), channel_id=1, source_target_pairs={{0,7},{1,6},{2,1},{3,0},{4,3},{5,2},{6,5},{7,4},{8,15},{9,14},{10,... | collective-permute-start | bytes 884744 | tf_op jit(solution)/shard_map/ppermute | solution.py:345
  131.2 8.8 %collective-permute-done.2.refs_3_ = bf16[9,8,2048]{2,1,0:T(8,128)(2,1)} collective-permute-done((bf16[9,8,2048]{2,1,0:T(8,128)(2,1)}, bf16[9,8,2048]{2,1,0:T(8,128)(2,1)}, u32[]{:S(2)}, u32[]{:S(2)}) %collective-permute-start.2) | collective-permute-done | bytes 294944 | tf_op jit(solution)/shard_map/ppermute | solution.py:345
  140.0 10.9 %collective-permute-done.3.refs_4_ = bf16[9,8,2048]{2,1,0:T(8,128)(2,1)} collective-permute-done((bf16[9,8,2048]{2,1,0:T(8,128)(2,1)}, bf16[9,8,2048]{2,1,0:T(8,128)(2,1)}, u32[]{:S(2)}, u32[]{:S(2)}) %collective-permute-start.3) | collective-permute-done | bytes 294944 | tf_op jit(solution)/shard_map/ppermute | solution.py:345
  150.8 7.1 %collective-permute-done.4.refs_5_ = bf16[9,8,2048]{2,1,0:T(8,128)(2,1)} collective-permute-done((bf16[9,8,2048]{2,1,0:T(8,128)(2,1)}, bf16[9,8,2048]{2,1,0:T(8,128)(2,1)}, u32[]{:S(2)}, u32[]{:S(2)}) %collective-permute-start.4) | collective-permute-done | bytes 294944 | tf_op jit(solution)/shard_map/ppermute | solution.py:345
  158.0 2.8 %collective-permute-done.6.refs_7_ = bf16[9,8,2048]{2,1,0:T(8,128)(2,1)} collective-permute-done((bf16[9,8,2048]{2,1,0:T(8,128)(2,1)}, bf16[9,8,2048]{2,1,0:T(8,128)(2,1)}, u32[]{:S(2)}, u32[]{:S(2)}) %collective-permute-start.6) | collective-permute-done | bytes 294944 | tf_op jit(solution)/shard_map/ppermute | solution.py:345
  160.8 4.5 %bank_gradient.1 = (f32[64,4096]{1,0:T(8,128)}, f32[64,1024]{1,0:T(8,128)}, s32[1]{0:T(128)}) custom-call(s32[1]{0:T(128)} %bitcast.4.member_ref, bf16[8,8,8,512]{3,2,1,0:T(8,128)(2,1)} %bitcast.22, bf16[8,8,8,64]{3,2,1,0:T(8,128)(2,1)S(1)} %bitcast.27, bf16[64,4096]{1,0:T(8,128)(2,1)} %bitcast.24, bf16[9,8,2048]{2,1,0:T(8,128)(2,1)} %get-tuple-element.64.refs_0_, ...), custom_call_target="tpu_custom_call" | custom-call | tf_op jit(solution)/shard_map/bank_gradient/pallas_call | solution.py:349
  166.0 0.8 copy-done.1
  166.8 4.1 %unplace.1 = bf16[128,4096]{1,0:T(8,128)(2,1)} custom-call(bf16[256,512]{1,0:T(8,128)(2,1)} %get-tuple-element.60.back_ref, bf16[64,8,2048]{2,1,0:T(8,128)(2,1)} %copy-done.1), custom_call_target="tpu_custom_call" | custom-call | tf_op jit(solution)/shard_map/unplace/pallas_call | solution.py:393
  (16 shorter events, 1.5 us)
Async XLA Ops:
  7.2 14.8 %copy-start = (bf16[1,128,4096]{2,1,0:T(8,128)(2,1)S(1)}, bf16[1,128,4096]{2,1,0:T(8,128)(2,1)}, u32[]{:S(2)}) copy-start(bf16[1,128,4096]{2,1,0:T(8,128)(2,1)} %param.8) | copy-start | bytes 3145732
  7.2 74.2 %all-gather.3.cloned.1.call-start = ((), (), s32[]{:S(2)}) async-start(), calls=%async_computation.4 | async-start | bytes 4718592 | tf_op jit(solution)/shard_map/all_gather | solution.py:263
  10.4 29.3 %all-to-all-start.1 = ((bf16[64,8,512]{2,1,0:T(8,128)(2,1)}), bf16[64,8,512]{2,1,0:T(8,128)(2,1)S(1)}, u32[]{:S(2)}, u32[]{:S(2)}) async-start(bf16[64,8,512]{2,1,0:T(8,128)(2,1)} %get-tuple-element.61), calls=%async_computation.1 | async-start | bytes 1048576 | tf_op jit(solution)/shard_map/all_to_all | solution.py:274
  39.7 24.1 %copy-start.2 = (bf16[64,8,512]{2,1,0:T(8,128)(2,1)}, bf16[64,8,512]{2,1,0:T(8,128)(2,1)S(1)}, u32[]{:S(2)}) copy-start(bf16[64,8,512]{2,1,0:T(8,128)(2,1)S(1)} %all-to-all-done.1.grad_ref) | copy-start | bytes 1572868
  39.7 47.8 %all-to-all-start.2 = ((bf16[8,48,2048]{2,1,0:T(8,128)(2,1)}), bf16[8,48,2048]{2,1,0:T(8,128)(2,1)S(1)}, u32[]{:S(2)}, u32[]{:S(2)}) async-start(bf16[8,48,2048]{2,1,0:T(8,128)(2,1)} %get-tuple-element.63), calls=%async_computation.2 | async-start | bytes 3145728 | tf_op jit(solution)/shard_map/all_to_all | solution.py:302
  45.5 6.6 %collective-permute-start.7 = (bf16[1,64,256]{2,1,0:T(8,128)(2,1)}, bf16[1,64,256]{2,1,0:T(8,128)(2,1)S(1)}, u32[]{:S(2)}, u32[]{:S(2)}) collective-permute-start(bf16[1,64,256]{2,1,0:T(8,128)(2,1)} %bitcast.28), channel_id=1, source_target_pairs={{0,64},{64,0},{128,192},{192,128},{256,320},{320,256},{384,448},{4... | collective-permute-start | bytes 98312 | tf_op jit(solution)/shard_map/ppermute | solution.py:308
  52.8 9.6 %collective-permute-start.8 = (bf16[2,64,256]{2,1,0:T(8,128)(2,1)S(1)}, bf16[2,64,256]{2,1,0:T(8,128)(2,1)S(1)}, u32[]{:S(2)}, u32[]{:S(2)}) collective-permute-start(bf16[2,64,256]{2,1,0:T(8,128)(2,1)S(1)} %pad_maximum_fusion.2), channel_id=1, source_target_pairs={{0,128},{64,192},{128,0},{192,64},{256,384},{320,448},{384,256},{4... | collective-permute-start | bytes 196616 | tf_op jit(solution)/shard_map/ppermute | solution.py:308
  63.8 15.9 %collective-permute-start.9 = (bf16[4,64,256]{2,1,0:T(8,128)(2,1)}, bf16[4,64,256]{2,1,0:T(8,128)(2,1)}, u32[]{:S(2)}, u32[]{:S(2)}) collective-permute-start(bf16[4,64,256]{2,1,0:T(8,128)(2,1)} %pad_maximum_fusion.1), channel_id=1, source_target_pairs={{0,256},{64,320},{128,384},{192,448},{256,0},{320,64},{384,128},{4... | collective-permute-start | bytes 393224 | tf_op jit(solution)/shard_map/ppermute | solution.py:308
  87.5 1.2 copy-start.4
  88.7 76.7 %all-to-all-start.3 = ((bf16[64,8,2048]{2,1,0:T(8,128)(2,1)}), bf16[64,8,2048]{2,1,0:T(8,128)(2,1)S(1)}, u32[]{:S(2)}, u32[]{:S(2)}) async-start(bf16[64,8,2048]{2,1,0:T(8,128)(2,1)} %term.1), calls=%async_computation.3 | async-start | bytes 4194304 | tf_op jit(solution)/shard_map/all_to_all | solution.py:325
  106.7 16.0 %collective-permute-start = (bf16[9,8,2048]{2,1,0:T(8,128)(2,1)}, bf16[9,8,2048]{2,1,0:T(8,128)(2,1)}, u32[]{:S(2)}, u32[]{:S(2)}) collective-permute-start(bf16[9,8,2048]{2,1,0:T(8,128)(2,1)} %get-tuple-element.65), channel_id=1, source_target_pairs={{0,1},{1,0},{2,3},{3,2},{4,5},{5,4},{6,7},{7,6},{8,9},{9,8},{10,11... | collective-permute-start | bytes 884744 | tf_op jit(solution)/shard_map/ppermute | solution.py:345
  109.1 17.1 %collective-permute-start.1 = (bf16[9,8,2048]{2,1,0:T(8,128)(2,1)}, bf16[9,8,2048]{2,1,0:T(8,128)(2,1)}, u32[]{:S(2)}, u32[]{:S(2)}) collective-permute-start(bf16[9,8,2048]{2,1,0:T(8,128)(2,1)} %get-tuple-element.66), channel_id=1, source_target_pairs={{0,2},{1,3},{2,4},{3,5},{4,6},{5,7},{6,0},{7,1},{8,10},{9,11},{10,... | collective-permute-start | bytes 884744 | tf_op jit(solution)/shard_map/ppermute | solution.py:345
  112.3 27.7 %collective-permute-start.2 = (bf16[9,8,2048]{2,1,0:T(8,128)(2,1)}, bf16[9,8,2048]{2,1,0:T(8,128)(2,1)}, u32[]{:S(2)}, u32[]{:S(2)}) collective-permute-start(bf16[9,8,2048]{2,1,0:T(8,128)(2,1)} %get-tuple-element.67), channel_id=1, source_target_pairs={{0,3},{1,2},{2,5},{3,4},{4,7},{5,6},{6,1},{7,0},{8,11},{9,10},{10,... | collective-permute-start | bytes 884744 | tf_op jit(solution)/shard_map/ppermute | solution.py:345
  115.7 35.1 %collective-permute-start.3 = (bf16[9,8,2048]{2,1,0:T(8,128)(2,1)}, bf16[9,8,2048]{2,1,0:T(8,128)(2,1)}, u32[]{:S(2)}, u32[]{:S(2)}) collective-permute-start(bf16[9,8,2048]{2,1,0:T(8,128)(2,1)} %get-tuple-element.68), channel_id=1, source_target_pairs={{0,4},{1,5},{2,6},{3,7},{4,0},{5,1},{6,2},{7,3},{8,12},{9,13},{10,... | collective-permute-start | bytes 884744 | tf_op jit(solution)/shard_map/ppermute | solution.py:345
  118.9 39.1 %collective-permute-start.4 = (bf16[9,8,2048]{2,1,0:T(8,128)(2,1)}, bf16[9,8,2048]{2,1,0:T(8,128)(2,1)}, u32[]{:S(2)}, u32[]{:S(2)}) collective-permute-start(bf16[9,8,2048]{2,1,0:T(8,128)(2,1)} %get-tuple-element.69), channel_id=1, source_target_pairs={{0,5},{1,4},{2,7},{3,6},{4,1},{5,0},{6,3},{7,2},{8,13},{9,12},{10,... | collective-permute-start | bytes 884744 | tf_op jit(solution)/shard_map/ppermute | solution.py:345
  122.8 35.2 %collective-permute-start.5 = (bf16[9,8,2048]{2,1,0:T(8,128)(2,1)}, bf16[9,8,2048]{2,1,0:T(8,128)(2,1)}, u32[]{:S(2)}, u32[]{:S(2)}) collective-permute-start(bf16[9,8,2048]{2,1,0:T(8,128)(2,1)} %get-tuple-element.70), channel_id=1, source_target_pairs={{0,6},{1,7},{2,0},{3,1},{4,2},{5,3},{6,4},{7,5},{8,14},{9,15},{10,... | collective-permute-start | bytes 884744 | tf_op jit(solution)/shard_map/ppermute | solution.py:345
  126.2 34.6 %collective-permute-start.6 = (bf16[9,8,2048]{2,1,0:T(8,128)(2,1)}, bf16[9,8,2048]{2,1,0:T(8,128)(2,1)}, u32[]{:S(2)}, u32[]{:S(2)}) collective-permute-start(bf16[9,8,2048]{2,1,0:T(8,128)(2,1)} %get-tuple-element.71), channel_id=1, source_target_pairs={{0,7},{1,6},{2,1},{3,0},{4,3},{5,2},{6,5},{7,4},{8,15},{9,14},{10,... | collective-permute-start | bytes 884744 | tf_op jit(solution)/shard_map/ppermute | solution.py:345
  165.4 1.4 copy-start.1
Sparse Core Ops, SparseCore 0:
  10.1 63.9 all-gather.2

commit v6 on v4

--- a/solution.py
+++ b/solution.py
@@ -8,6 +8,7 @@
 adapter_scale = 2.0
 row_limit = 4
 group = 2 * row_limit
+pieces = 2
 f32 = jnp.float32
 bf16 = jnp.bfloat16
 
@@ -24,7 +25,9 @@
     return (iota(shape, 0) // row_limit) % 2
 
 
-def place_gradient_kernel(tenant_ref, owner_ref, grad_ref, placing_ref, send_ref):
+def place_gradient_kernel(tenant_ref, owner_ref, grad_hbm, placing_ref, send_hbm, grad_ref, send_ref, sems):
+    read = pltpu.make_async_copy(grad_hbm, grad_ref, sems.at[0])
+    read.start()
     tok_rows = tenant_ref.shape[1]
     owners = owner_ref.shape[1]
     slots = owners * group
@@ -41,8 +44,19 @@
     width = grad_ref.shape[1] // 2
     lower = jnp.where(placing & (half == 0), 1.0, 0.0).astype(bf16)
     upper = jnp.where(placing & (half == 1), 1.0, 0.0).astype(bf16)
-    sent = dot(lower, grad_ref[:, :width], ((1,), (0,))) + dot(upper, grad_ref[:, width:], ((1,), (0,)))
-    send_ref[...] = sent.astype(bf16).reshape(send_ref.shape)
+    read.wait()
+    low, high = grad_ref[:, :width], grad_ref[:, width:]
+    part, count = slots // pieces, owners // pieces
+    writes = []
+    for p in range(pieces):
+        rows = slice(p * part, (p + 1) * part)
+        sent = dot(lower[rows], low, ((1,), (0,))) + dot(upper[rows], high, ((1,), (0,)))
+        here = pl.ds(p * count, count)
+        send_ref[here] = sent.astype(bf16).reshape(count, group, width)
+        writes.append(pltpu.make_async_copy(send_ref.at[here], send_hbm.at[here], sems.at[1 + p]))
+        writes[-1].start()
+    for write in writes:
+        write.wait()
 
 
 def place_inputs_kernel(placing_ref, low_ref, high_ref, send_ref, back_ref):
@@ -127,15 +141,27 @@
     grad_up_ref[:, out_width:] = up[rank:]
 
 
-def unplace_kernel(back_ref, rows_ref, out_ref):
-    tok_rows = out_ref.shape[0]
+def unplace_kernel(back_ref, rows_ref, out_hbm, out_ref, sems):
+    steps = out_ref.shape[0]
+    tok_rows = out_hbm.shape[0]
     block = rows_ref.shape[2]
+    step = pl.program_id(0)
+
+    def write(c, h):
+        start = pl.multiple_of((h * steps + c) * block, block)
+        here = out_hbm.at[:, pl.ds(start, block)]
+        return pltpu.make_async_copy(out_ref.at[c, pl.ds(h * tok_rows, tok_rows)], here, sems.at[c, h])
+
     rows = rows_ref[...].reshape(back_ref.shape[1], block)
-    both = dot(back_ref[...], rows, ((1,), (0,))).astype(bf16)
-    start = pl.multiple_of(pl.program_id(0) * block, block)
-    out_ref[:, pl.ds(start, block)] = both[:tok_rows]
-    start = pl.multiple_of(out_ref.shape[1] // 2 + pl.program_id(0) * block, block)
-    out_ref[:, pl.ds(start, block)] = both[tok_rows:]
+    out_ref[step] = dot(back_ref[...], rows, ((1,), (0,))).astype(bf16)
+    write(step, 0).start()
+    write(step, 1).start()
+
+    @pl.when(step == steps - 1)
+    def _():
+        for c in range(steps):
+            write(c, 0).wait()
+            write(c, 1).wait()
 
 
 def local(
@@ -162,11 +188,21 @@
     block = half_width // steps
     shape = jax.ShapeDtypeStruct
 
+    vmem = pl.BlockSpec(memory_space=pltpu.VMEM)
+    anywhere = pl.BlockSpec(memory_space=pl.ANY)
+
     all_down = lax.all_gather(down_factor, "segment").reshape(sections * rank, width)
 
     placing, send_grads = pl.pallas_call(
         place_gradient_kernel,
+        in_specs=[vmem, vmem, anywhere],
+        out_specs=(vmem, anywhere),
         out_shape=(shape((slots, tok_rows), bf16), shape((owners, group, out_width // 2), bf16)),
+        scratch_shapes=[
+            pltpu.VMEM((tok_rows, out_width), bf16),
+            pltpu.VMEM((owners, group, out_width // 2), bf16),
+            pltpu.SemaphoreType.DMA((1 + pieces,)),
+        ],
         name="place_gradient",
     )(tenant.reshape(1, tok_rows), adapter_owner_index.reshape(1, owners), gradient_list)
     recv_grads = lax.all_to_all(send_grads, "owner", split_axis=0, concat_axis=0, tiled=True)
@@ -225,8 +261,9 @@
             pl.BlockSpec((2 * tok_rows, slots), lambda c: (0, 0)),
             pl.BlockSpec((owners, group, block), lambda c: (0, 0, c)),
         ],
-        out_specs=pl.BlockSpec((tok_rows, width), lambda c: (0, 0)),
+        out_specs=anywhere,
         out_shape=shape((tok_rows, width), bf16),
+        scratch_shapes=[pltpu.VMEM((steps, 2 * tok_rows, block), bf16), pltpu.SemaphoreType.DMA((steps, 2))],
         name="unplace",
     )(back, returned)
 

time: 165 us -> 166 us (level)
  transfers between devices with their start and end apart: 4 -> 4, of which waited for: 3 -> 3; matrix products, arithmetic and copies ran while one was open for 0% -> 0% of each run, Pallas kernels for 12% -> 13%
where the time goes in v6:
time: 166 us; the launch traced here: 165 us
  waiting for transfers between devices  70.4 us (42%)
  blocking collectives  29.3 us (18%)
  Pallas kernels  25.4 us (15%)
  starting transfers between devices  24.6 us (15%)
  between operations  14.1 us (8%)
    all_to_all x1, waiting for transfers between devices, local(): lax.all_to_all(terms, 'owner', split_axis=0, concat_axis=0, tiled=True)  45.1 us
    all_gather x1, blocking collectives, local(): all_coef = lax.all_gather(compact, 'segment')  29.3 us
    all_to_all x1, waiting for transfers between devices, local(): lax.all_to_all(send_grads, 'owner', split_axis=0, concat_axis=0, tiled=True)  12.8 us
    all_to_all x1, waiting for transfers between devices, local(): lax.all_to_all(send_inputs, 'owner', split_axis=0, concat_axis=0, tiled=T...  11.9 us
    all_to_all x1, starting transfers between devices, local(): lax.all_to_all(send_grads, 'owner', split_axis=0, concat_axis=0, tiled=True)  11.6 us
    all_to_all x1, starting transfers between devices, local(): lax.all_to_all(terms, 'owner', split_axis=0, concat_axis=0, tiled=True)  7.21 us
    pallas_call x1, Pallas kernels, local(): pl.pallas_call(term_kernel, grid=(steps,), in_specs=[pl.BlockSpec(memory_...  6.18 us
    all_to_all x1, starting transfers between devices, local(): lax.all_to_all(send_inputs, 'owner', split_axis=0, concat_axis=0, tiled=T...  5.72 us
  transfers between devices with their start and end apart: 4, of which 3 were waited for; matrix products, arithmetic and copies ran while one was open for 0% of the time, Pallas kernels for 13%

profile of v6, /device:TPU:1, one launch (start us, length us, event | category | flops | bytes accessed | tf_op | source)
XLA Modules:
  0.0 164.6 jit_solution(16539883767776366707)
XLA Ops:
  7.2 0.0 all-gather.4.cloned.1.call-start
  7.2 0.7 all-gather.4.cloned.1.call-update
  7.9 3.4 %place_gradient.1 = (bf16[512,128]{1,0:T(8,128)(2,1)}, bf16[64,8,512]{2,1,0:T(8,128)(2,1)}) custom-call(s32[1,128]{1,0:T(1,128)} %bitcast.23, s32[1,64]{1,0:T(1,128)} %bitcast.24, bf16[128,1024]{1,0:T(8,128)(2,1)} %bitcast.21), custom_call_target="tpu_custom_call" | custom-call | tf_op jit(solution)/shard_map/place_gradient/pallas_call | solution.py:196
  11.3 11.6 %all-to-all-start = ((bf16[64,8,512]{2,1,0:T(8,128)(2,1)}), bf16[64,8,512]{2,1,0:T(8,128)(2,1)S(1)}, u32[]{:S(2)}, u32[]{:S(2)}) async-start(bf16[64,8,512]{2,1,0:T(8,128)(2,1)} %get-tuple-element.13), calls=%async_computation | async-start | bytes 1048576 | tf_op jit(solution)/shard_map/all_to_all | solution.py:208
  23.0 5.0 %place_inputs.1 = (bf16[64,8,2048]{2,1,0:T(8,128)(2,1)}, bf16[256,512]{1,0:T(8,128)(2,1)}) custom-call(bf16[512,128]{1,0:T(8,128)(2,1)} %get-tuple-element.11.placing_ref, bf16[128,4096]{1,0:T(8,128)(2,1)} %bitcast.15, bf16[128,4096]{1,0:T(8,128)(2,1)} %bitcast.16), custom_call_target="tpu_custom_call" | custom-call | tf_op jit(solution)/shard_map/place_inputs/pallas_call | solution.py:210
  27.9 12.8 %all-to-all-done.grad_ref.grads_ref = bf16[64,8,512]{2,1,0:T(8,128)(2,1)S(1)} async-done(((bf16[64,8,512]{2,1,0:T(8,128)(2,1)}), bf16[64,8,512]{2,1,0:T(8,128)(2,1)S(1)}, u32[]{:S(2)}, u32[]{:S(2)}) %all-to-all-start) | async-done | bytes 524320 | tf_op jit(solution)/shard_map/all_to_all | solution.py:208
  40.7 0.0 copy-start.1
  40.7 0.8 copy-done.1
  41.5 5.7 %all-to-all-start.2 = ((bf16[64,8,2048]{2,1,0:T(8,128)(2,1)}), bf16[64,8,2048]{2,1,0:T(8,128)(2,1)S(1)}, u32[]{:S(2)}, u32[]{:S(2)}) async-start(bf16[64,8,2048]{2,1,0:T(8,128)(2,1)} %get-tuple-element.15), calls=%async_computation.2 | async-start | bytes 4194304 | tf_op jit(solution)/shard_map/all_to_all | solution.py:232
  47.2 2.3 %coef.1 = (bf16[512,64]{1,0:T(8,128)(2,1)}, bf16[64,256]{1,0:T(8,128)(2,1)}) custom-call(bf16[64,8,512]{2,1,0:T(8,128)(2,1)} %copy-done.1, bf16[64,1024]{1,0:T(8,128)(2,1)} %bitcast.22), custom_call_target="tpu_custom_call" | custom-call | tf_op jit(solution)/shard_map/coef/pallas_call | solution.py:226
  49.5 29.3 %all-gather = bf16[512,256]{1,0:T(8,128)(2,1)} all-gather(bf16[64,256]{1,0:T(8,128)(2,1)} %get-tuple-element.14), channel_id=2, replica_groups=mesh['segment'=8,'owner'=64] {'segment'}, dimensions={0}, use_global_device_ids=true | all-gather | bytes 294912 | tf_op jit(solution)/shard_map/all_gather | solution.py:233
  78.9 0.0 all-gather.4.cloned.1.call-done.low_ref.high_ref
  78.9 6.2 %term.1 = bf16[64,8,2048]{2,1,0:T(8,128)(2,1)} custom-call(s32[1]{0:T(128)} %bitcast.4.place_ref, bf16[8,64,256]{2,1,0:T(8,128)(2,1)} %bitcast.19, bf16[512,4096]{1,0:T(8,128)(2,1)} %all-gather.4.cloned.1.call-done.low_ref.high_ref, bf16[512,4096]{1,0:T(8,128)(2,1)} %all-gather.4.cloned.1.call-done.low_ref.high_ref), custom_call_target="tpu_custom_call" | custom-call | tf_op jit(solution)/shard_map/term/pallas_call | solution.py:235
  85.0 11.9 %all-to-all-done.2.rows_ref = bf16[64,8,2048]{2,1,0:T(8,128)(2,1)S(1)} async-done(((bf16[64,8,2048]{2,1,0:T(8,128)(2,1)}), bf16[64,8,2048]{2,1,0:T(8,128)(2,1)S(1)}, u32[]{:S(2)}, u32[]{:S(2)}) %all-to-all-start.2) | async-done | bytes 2097184 | tf_op jit(solution)/shard_map/all_to_all | solution.py:232
  96.9 0.0 copy-start
  96.9 7.2 %all-to-all-start.1 = ((bf16[64,8,2048]{2,1,0:T(8,128)(2,1)}), bf16[64,8,2048]{2,1,0:T(8,128)(2,1)}, u32[]{:S(2)}, u32[]{:S(2)}) async-start(bf16[64,8,2048]{2,1,0:T(8,128)(2,1)} %term.1), calls=%async_computation.1 | async-start | bytes 4194304 | tf_op jit(solution)/shard_map/all_to_all | solution.py:249
  104.1 0.0 copy-done
  104.1 4.5 %weight_gradient.1 = (f32[64,4096]{1,0:T(8,128)}, f32[64,1024]{1,0:T(8,128)}) custom-call(bf16[64,8,2048]{2,1,0:T(8,128)(2,1)} %copy-done, bf16[64,8,512]{2,1,0:T(8,128)(2,1)} %copy-done.1, bf16[512,64]{1,0:T(8,128)(2,1)} %get-tuple-element.16.coef_ref, bf16[64,4096]{1,0:T(8,128)(2,1)} %bitcast.18), custom_call_target="tpu_custom_call" | custom-call | tf_op jit(solution)/shard_map/weight_gradient/pallas_call | solution.py:251
  108.6 45.1 %all-to-all-done.1.rows_ref = bf16[64,8,2048]{2,1,0:T(8,128)(2,1)} async-done(((bf16[64,8,2048]{2,1,0:T(8,128)(2,1)}), bf16[64,8,2048]{2,1,0:T(8,128)(2,1)}, u32[]{:S(2)}, u32[]{:S(2)}) %all-to-all-start.1) | async-done | bytes 2097184 | tf_op jit(solution)/shard_map/all_to_all | solution.py:249
  153.7 4.0 %unplace.1 = bf16[128,4096]{1,0:T(8,128)(2,1)} custom-call(bf16[256,512]{1,0:T(8,128)(2,1)} %get-tuple-element.12.back_ref, bf16[64,8,2048]{2,1,0:T(8,128)(2,1)} %all-to-all-done.1.rows_ref), custom_call_target="tpu_custom_call" | custom-call | tf_op jit(solution)/shard_map/unplace/pallas_call | solution.py:257
Async XLA Ops:
  7.2 71.7 %all-gather.4.cloned.1.call-start = ((), (), s32[]{:S(2)}) async-start(), calls=%async_computation.3 | async-start | bytes 4718592 | tf_op jit(solution)/shard_map/all_gather | solution.py:194
  11.3 29.4 %all-to-all-start = ((bf16[64,8,512]{2,1,0:T(8,128)(2,1)}), bf16[64,8,512]{2,1,0:T(8,128)(2,1)S(1)}, u32[]{:S(2)}, u32[]{:S(2)}) async-start(bf16[64,8,512]{2,1,0:T(8,128)(2,1)} %get-tuple-element.13), calls=%async_computation | async-start | bytes 1048576 | tf_op jit(solution)/shard_map/all_to_all | solution.py:208
  40.7 0.8 copy-start.1
  41.5 55.4 %all-to-all-start.2 = ((bf16[64,8,2048]{2,1,0:T(8,128)(2,1)}), bf16[64,8,2048]{2,1,0:T(8,128)(2,1)S(1)}, u32[]{:S(2)}, u32[]{:S(2)}) async-start(bf16[64,8,2048]{2,1,0:T(8,128)(2,1)} %get-tuple-element.15), calls=%async_computation.2 | async-start | bytes 4194304 | tf_op jit(solution)/shard_map/all_to_all | solution.py:232
  96.9 7.2 %copy-start = (bf16[64,8,2048]{2,1,0:T(8,128)(2,1)}, bf16[64,8,2048]{2,1,0:T(8,128)(2,1)S(1)}, u32[]{:S(2)}) copy-start(bf16[64,8,2048]{2,1,0:T(8,128)(2,1)S(1)} %all-to-all-done.2.rows_ref) | copy-start | bytes 6291460
  96.9 56.8 %all-to-all-start.1 = ((bf16[64,8,2048]{2,1,0:T(8,128)(2,1)}), bf16[64,8,2048]{2,1,0:T(8,128)(2,1)}, u32[]{:S(2)}, u32[]{:S(2)}) async-start(bf16[64,8,2048]{2,1,0:T(8,128)(2,1)} %term.1), calls=%async_computation.1 | async-start | bytes 4194304 | tf_op jit(solution)/shard_map/all_to_all | solution.py:249
Sparse Core Ops, SparseCore 0:
  10.1 65.3 all-gather.3

commit v7 on v5

--- a/solution.py
+++ b/solution.py
@@ -10,7 +10,8 @@
 group = 2 * row_limit
 banks = 8
 members = 8
-bank_slots = 23
+bank_slots = 7
+straight = 2
 lines = 2 * bank_slots + 2
 f32 = jnp.float32
 bf16 = jnp.bfloat16
@@ -75,16 +76,17 @@
         named = iota((owners, tok_rows), 0) == tenant_ref[...]
         named_bf16 = named.astype(bf16)
         before = (iota((tok_rows, tok_rows), 0) < iota((tok_rows, tok_rows), 1)).astype(bf16)
-        in_bank = dot((iota((banks, owners), 0) == owner_ref[...] // members).astype(bf16), named_bf16, ((1,), (0,)))
+        rank = dot(named_bf16, before, ((1,), (0,)))
+        late = (named & (rank >= straight)).astype(bf16)
+        in_bank = dot((iota((banks, owners), 0) == owner_ref[...] // members).astype(bf16), late, ((1,), (0,)))
         bank_rank = dot(in_bank.astype(bf16), before, ((1,), (0,)))
         key = in_bank * (bank_rank + 1.0)
         most = jnp.max(key)
         slot = jnp.sum(key, axis=0, keepdims=True) - 1.0
-        rank = dot(named_bf16, before, ((1,), (0,)))
         place = jnp.sum(jnp.where(named, rank, 0.0), axis=0, keepdims=True)
         member = jnp.broadcast_to((owner_ref[...] % members).astype(f32), (banks, owners)).astype(bf16)
         member = dot(member, named_bf16, ((1,), (0,)))
-        code = in_bank * (member * row_limit + place + 1.0)
+        code = in_bank * (member * straight + place - straight + 1.0)
         line = iota((tok_rows, tok_rows), 0)
         mine = ((line % bank_slots).astype(f32) == slot) & (line < 2 * bank_slots)
         codes = dot(code.astype(bf16), mine.astype(bf16), ((1,), (1,)))
@@ -106,9 +108,26 @@
         send_ref[:, :, :tok_rows] = first.astype(bf16).reshape(banks, lines, tok_rows)
 
 
-def route_kernel(member_ref, rows_ref, *refs):
+def place_straight_kernel(placing_ref, *refs):
+    quarters, send_ref, pick_ref = refs[:4], refs[4], refs[5]
+
+    @pl.when(pl.program_id(0) == 0)
+    def _():
+        placing = placing_ref[...].astype(f32).reshape(-1, group, placing_ref.shape[1])
+        line = iota(placing.shape, 1)
+        first = jnp.where(line % row_limit < straight, placing, pltpu.roll(placing, straight, 1))
+        for q in range(4):
+            pick_ref[q] = jnp.where(line // straight == q, first, 0.0).astype(bf16).reshape(placing_ref.shape)
+
+    sent = dot(pick_ref[0], quarters[0][...], ((1,), (0,)))
+    for q in range(1, 4):
+        sent = sent + dot(pick_ref[q], quarters[q][...], ((1,), (0,)))
+    send_ref[...] = sent.astype(bf16).reshape(send_ref.shape)
+
+
+def route_kernel(member_ref, low_ref, high_ref, *refs):
     outs, pick_ref, most_ref = refs[:members], refs[members], refs[members + 1]
-    block = rows_ref.shape[2]
+    block = low_ref.shape[2]
     rows = members * group
 
     @pl.when(pl.program_id(0) == 0)
@@ -117,18 +136,21 @@
         row, line = iota((rows, lines), 0), iota((rows, lines), 1)
         t = row // group
         to = (x + t // 2) % 4 * 2 + (core + t) % 2
-        want = (to * row_limit + row % row_limit + 1).astype(f32)
-        same_half = (row // row_limit) % 2 == line // bank_slots
+        want = (to * straight + row % straight + 1).astype(f32)
+        same_half = row % group // row_limit == line // bank_slots
         most = jnp.zeros((1, 128), f32)
         for y in range(banks):
-            tail = rows_ref[y, :, :128].astype(f32)
+            tail = low_ref[y, :, :128].astype(f32)
             codes = tail[lines - 2 : lines - 1, :lines]
             most = jnp.maximum(most, tail[lines - 1 :, :])
             pick_ref[y] = jnp.where((want == codes) & same_half, 1.0, 0.0).astype(bf16)
         most_ref[...] = jnp.broadcast_to(most, most_ref.shape)
 
     for y in range(banks):
-        part = dot(pick_ref[y], rows_ref[y], ((1,), (0,))).astype(bf16).reshape(members, group, block)
+        low = dot(pick_ref[y], low_ref[y], ((1,), (0,)))
+        high = dot(pick_ref[y], high_ref[y], ((1,), (0,)))
+        odd = iota(low.shape, 0) // straight % 2 == 1
+        part = jnp.where(odd, high, low).astype(bf16).reshape(members, group, block)
         for t in range(members):
             outs[t][y] = part[t]
     most = jnp.broadcast_to(most_ref[:, :1], (group, block)).astype(bf16)
@@ -164,8 +186,7 @@
         place = place_ref[0]
         parts = []
         for k in range(sections):
-            part = coef_ref[jnp.bitwise_xor(place, k)]
-            parts.append(jnp.where(place <= k, part, jnp.zeros_like(part)))
+            parts.append(jnp.where(place <= k, coef_ref[k], jnp.zeros_like(coef_ref[k])))
         shape = (columns, wide_ref.shape[0])
         column, row = iota(shape, 0), iota(shape, 1)
         same = column == row // group * row_limit + row % row_limit
@@ -206,23 +227,64 @@
     gradients(rows, grads, coef_ref[...], down_ref, grad_down_ref, grad_up_ref)
 
 
-def bank_gradient_kernel(member_ref, grads_ref, coef_ref, down_ref, *refs):
+def add_gradients(rows, grads, coef, lines_of, down_ref, grad_down_ref, grad_up_ref):
+    rank = coef.shape[1]
+    width = rows.shape[1]
+    out_width = grads.shape[1]
+    line = iota(coef.shape, 0) % group
+    zero = jnp.zeros_like(coef)
+    parts = jnp.concatenate([jnp.where(line // straight == q, coef, zero) for q in range(4)], axis=1)
+    down = dot(parts, rows, ((0,), (0,)))
+    proj = jnp.zeros(coef.shape, f32)
+    for q in range(4):
+        here = slice(q * width, (q + 1) * width)
+        grad_down_ref[:, here] += down[q * rank : (q + 1) * rank]
+        proj = jnp.where(line // straight == q, dot(rows, down_ref[:, here], ((1,), (1,))), proj)
+    proj = proj.reshape(-1, group, rank)
+    proj = proj + pltpu.roll(proj, 4, 1)
+    proj = (proj + pltpu.roll(proj, 2, 1)).reshape(coef.shape).astype(bf16)
+    own = lines_of(line)
+    half = line // row_limit
+    pair = [jnp.where(own & (half == h), proj, zero) for h in range(2)]
+    up = dot(jnp.concatenate(pair, axis=1), grads, ((0,), (0,)))
+    grad_up_ref[:, :out_width] += up[:rank]
+    grad_up_ref[:, out_width:] += up[rank:]
+
+
+def bank_gradient_kernel(member_ref, rows_ref, grads_ref, coef_ref, down_ref, *refs):
     blocks, (grad_down_ref, grad_up_ref, most_ref) = refs[:members], refs[members:]
     rank = coef_ref.shape[3]
     out_width = grads_ref.shape[3]
-    width = down_ref.shape[1] // 2
+    width = rows_ref.shape[2]
+    slots = banks * members * group
+    grad_down_ref[...] = jnp.zeros_like(grad_down_ref)
+    grad_up_ref[...] = jnp.zeros_like(grad_up_ref)
+
+    coef = coef_ref[...].reshape(banks * members, group, rank).astype(f32)
+    first = iota(coef.shape, 1) % row_limit < straight
+    coef = jnp.where(first, coef, pltpu.roll(coef, straight, 1)).reshape(slots, rank).astype(bf16)
+    rows = rows_ref[...].reshape(slots, width)
+    grads = grads_ref[...].reshape(slots, out_width)
+    add_gradients(
+        rows, grads, coef, lambda line: line % row_limit < straight, down_ref, grad_down_ref, grad_up_ref
+    )
+
     x, core = member_ref[0] // 2, member_ref[0] % 2
     rows, coef, grads = [], [], []
     most = jnp.zeros((group, 128), f32)
     for t in range(members):
         source = (x + 4 - t // 2) % 4 * 2 + (core + t) % 2
         rows.append(blocks[t][:banks].reshape(banks * group, width))
-        coef.append(coef_ref[:, pl.ds(source, 1)].reshape(banks * group, rank))
+        coef.append(coef_ref[:, pl.ds(source, 1)].reshape(banks, group, rank).astype(f32))
         grads.append(grads_ref[:, pl.ds(source, 1)].reshape(banks * group, out_width))
         most = jnp.maximum(most, blocks[t][banks, :, :128].astype(f32))
     most_ref[0] = jnp.max(most).astype(jnp.int32)
     rows, coef, grads = (jnp.concatenate(part, axis=0) for part in (rows, coef, grads))
-    gradients(rows, grads, coef, down_ref, grad_down_ref, grad_up_ref)
+    last = iota(coef.shape, 1) % row_limit >= straight
+    coef = jnp.where(last, coef, pltpu.roll(coef, group - straight, 1)).reshape(slots, rank).astype(bf16)
+    add_gradients(
+        rows, grads, coef, lambda line: line % row_limit >= straight, down_ref, grad_down_ref, grad_up_ref
+    )
 
 
 def unplace_kernel(back_ref, rows_ref, out_ref):
@@ -302,11 +364,24 @@
     recv_banks = lax.all_to_all(
         send_banks, "owner", split_axis=0, concat_axis=0, axis_index_groups=same_member, tiled=True
     )
-    all_coef = compact[None]
-    while all_coef.shape[0] < sections:
-        apart = all_coef.shape[0]
-        other = lax.ppermute(all_coef, "segment", [(i, i ^ apart) for i in range(sections)])
-        all_coef = jnp.concatenate([all_coef, other], axis=0)
+    quarter = width // 4
+    quarter_steps = 2
+    quarter_block = quarter // quarter_steps
+    send_straight = pl.pallas_call(
+        place_straight_kernel,
+        grid=(quarter_steps,),
+        in_specs=[pl.BlockSpec((slots, tok_rows), lambda c: (0, 0))]
+        + [
+            pl.BlockSpec((tok_rows, quarter_block), lambda c, q=q: (0, q * quarter_steps + c)) for q in range(4)
+        ],
+        out_specs=pl.BlockSpec((owners, group, quarter_block), lambda c: (0, 0, c)),
+        out_shape=shape((owners, group, quarter), bf16),
+        scratch_shapes=[pltpu.VMEM((4, slots, tok_rows), bf16)],
+        name="place_straight",
+    )(placing, inputs, inputs, inputs, inputs)
+    send_straight, recv_banks, compact = lax.optimization_barrier((send_straight, recv_banks, compact))
+    recv_straight = lax.all_to_all(send_straight, "owner", split_axis=0, concat_axis=0, tiled=True)
+    all_coef = lax.all_gather(compact, "segment")
 
     terms = pl.pallas_call(
         term_kernel,
@@ -326,16 +401,17 @@
 
     sent_blocks = pl.pallas_call(
         route_kernel,
-        grid=(steps,),
+        grid=(quarter_steps,),
         in_specs=[
             pl.BlockSpec(memory_space=pltpu.SMEM),
-            pl.BlockSpec((banks, lines, block), lambda c: (0, 0, c)),
+            pl.BlockSpec((banks, lines, quarter_block), lambda c: (0, 0, c)),
+            pl.BlockSpec((banks, lines, quarter_block), lambda c: (0, 0, quarter_steps + c)),
         ],
-        out_specs=[pl.BlockSpec((banks + 1, group, block), lambda c: (0, 0, c))] * members,
-        out_shape=[shape((banks + 1, group, half_width), bf16)] * members,
+        out_specs=[pl.BlockSpec((banks + 1, group, quarter_block), lambda c: (0, 0, c))] * members,
+        out_shape=[shape((banks + 1, group, quarter), bf16)] * members,
         scratch_shapes=[pltpu.VMEM((banks, members * group, lines), bf16), pltpu.VMEM((group, 128), f32)],
         name="route",
-    )(member, recv_banks)
+    )(member, recv_banks, recv_banks)
     got_blocks = [sent_blocks[0]]
     for t in range(1, members):
         pairs = []
@@ -348,12 +424,13 @@
     vmem = pl.BlockSpec(memory_space=pltpu.VMEM)
     grad_down, grad_up, most = pl.pallas_call(
         bank_gradient_kernel,
-        in_specs=[smem] + [vmem] * (3 + members),
+        in_specs=[smem] + [vmem] * (4 + members),
         out_specs=(vmem, vmem, smem),
         out_shape=(shape((rank, width), f32), shape((rank, out_width), f32), shape((1,), jnp.int32)),
         name="bank_gradient",
     )(
         member,
+        recv_straight,
         recv_grads.reshape(banks, members, group, out_width // 2),
         coef.reshape(banks, members, group, rank),
         down_factor,

time: 179 us -> 180 us (level)
  blocking collectives: 0 us -> 28.3 us
  starting transfers between devices: 71.9 us -> 56.7 us
  waiting for transfers between devices: 57.3 us -> 47 us
  other arithmetic: 3.83 us -> 0 us
  Pallas kernels: 27.9 us -> 29.9 us
    all_gather x0 -> x1, blocking collectives: none -> 28.3 us  [local(): all_coef = lax.all_gather(compact, 'segment')]
    ppermute x3 -> x0, starting transfers between devices: 18.6 us -> none  [local(): lax.ppermute(all_coef, 'segment', [(i, i ^ apart) for i in range(sections)])]
    ppermute x3 -> x0, waiting for transfers between devices: 13.5 us -> none  [local(): lax.ppermute(all_coef, 'segment', [(i, i ^ apart) for i in range(sections)])]
    all_to_all x1, waiting for transfers between devices: 0.01 us -> 13.4 us  [local(): lax.all_to_all(send_banks, 'owner', split_axis=0, concat_axis=0, axis_ind...]
    ppermute x7, waiting for transfers between devices: 29.7 us -> 16.5 us  [local(): got_blocks.append(lax.ppermute(sent_blocks[t], 'owner', pairs))]
    all_to_all x0 -> x1, starting transfers between devices: none -> 4.59 us  [local(): lax.all_to_all(send_straight, 'owner', split_axis=0, concat_axis=0, tiled...]
    concatenate x3 -> x0, other arithmetic: 3.83 us -> none  [local(): all_coef = jnp.concatenate([all_coef, other], axis=0)]
    pallas_call x2 -> x3, Pallas kernels: 8.81 us -> 11.6 us  [the longest x1 6.39 us: local(): pl.pallas_call(bank_gradient_kernel, in_specs=[smem] + [vmem] * (4 + memb...]
  transfers between devices with their start and end apart: 14 -> 12, of which waited for: 8 -> 6; matrix products, arithmetic and copies ran while one was open for 2% -> 0% of each run, Pallas kernels for 13% -> 14%
where the time goes in v7:
time: 180 us; the launch traced here: 178 us
  starting transfers between devices  56.7 us (32%)
  waiting for transfers between devices  47 us (26%)
  Pallas kernels  29.9 us (17%)
  blocking collectives  28.3 us (16%)
  between operations  14.8 us (8%)
    all_gather x1, blocking collectives, local(): all_coef = lax.all_gather(compact, 'segment')  28.3 us
    ppermute x7, starting transfers between devices, local(): got_blocks.append(lax.ppermute(sent_blocks[t], 'owner', pairs))  21.7 us
    ppermute x7, waiting for transfers between devices, local(): got_blocks.append(lax.ppermute(sent_blocks[t], 'owner', pairs))  16.5 us
    all_to_all x1, starting transfers between devices, local(): lax.all_to_all(terms, 'owner', split_axis=0, concat_axis=0, tiled=True)  15.2 us
    all_to_all x1, waiting for transfers between devices, local(): lax.all_to_all(send_grads, 'owner', split_axis=0, concat_axis=0, tiled=True)  14.2 us
    all_to_all x1, waiting for transfers between devices, local(): lax.all_to_all(send_banks, 'owner', split_axis=0, concat_axis=0, axis_ind...  13.4 us
    all_to_all x1, starting transfers between devices, local(): lax.all_to_all(send_grads, 'owner', split_axis=0, concat_axis=0, tiled=True)  11.6 us
    pallas_call x1, Pallas kernels, local(): pl.pallas_call(bank_gradient_kernel, in_specs=[smem] + [vmem] * (4 + memb...  6.39 us
  transfers between devices with their start and end apart: 12, of which 6 were waited for; matrix products, arithmetic and copies ran while one was open for 0% of the time, Pallas kernels for 14%

profile of v7, /device:TPU:1, one launch (start us, length us, event | category | flops | bytes accessed | tf_op | source)
XLA Modules:
  0.0 178.5 jit_solution(14211640915559644349)
XLA Ops:
  7.2 0.0 all-gather.4.cloned.1.call-start
  7.2 0.7 all-gather.4.cloned.1.call-update
  7.9 2.5 %place_gradient.1 = (bf16[512,128]{1,0:T(8,128)(2,1)S(1)}, bf16[64,8,512]{2,1,0:T(8,128)(2,1)}) custom-call(s32[1,128]{1,0:T(1,128)} %bitcast.35, s32[1,64]{1,0:T(1,128)} %bitcast.37, bf16[128,1024]{1,0:T(8,128)(2,1)} %bitcast.33), custom_call_target="tpu_custom_call" | custom-call | tf_op jit(solution)/shard_map/place_gradient/pallas_call | solution.py:331
  10.4 11.6 %all-to-all-start.2 = ((bf16[64,8,512]{2,1,0:T(8,128)(2,1)}), bf16[64,8,512]{2,1,0:T(8,128)(2,1)S(1)}, u32[]{:S(2)}, u32[]{:S(2)}) async-start(bf16[64,8,512]{2,1,0:T(8,128)(2,1)} %get-tuple-element.65), calls=%async_computation.2 | async-start | bytes 1048576 | tf_op jit(solution)/shard_map/all_to_all | solution.py:336
  22.0 3.5 %place_banks.1 = (bf16[8,16,2048]{2,1,0:T(8,128)(2,1)}, bf16[256,512]{1,0:T(8,128)(2,1)}) custom-call(s32[1,128]{1,0:T(1,128)} %bitcast.36, s32[1,64]{1,0:T(1,128)} %bitcast.38, bf16[512,128]{1,0:T(8,128)(2,1)S(1)} %get-tuple-element.62.placing_ref, bf16[128,4096]{1,0:T(8,128)(2,1)S(1)} %bitcast.19, bf16[128,4096]{1,0:T(8,128)(2,1)S(1)} %bitcast.20), custom_call_target="tpu_custom_call" | custom-call | tf_op jit(solution)/shard_map/place_banks/pallas_call | solution.py:338
  25.5 14.2 %all-to-all-done.2.grad_ref = bf16[64,8,512]{2,1,0:T(8,128)(2,1)S(1)} async-done(((bf16[64,8,512]{2,1,0:T(8,128)(2,1)}), bf16[64,8,512]{2,1,0:T(8,128)(2,1)S(1)}, u32[]{:S(2)}, u32[]{:S(2)}) %all-to-all-start.2) | async-done | bytes 524320 | tf_op jit(solution)/shard_map/all_to_all | solution.py:336
  39.7 3.5 %all-to-all-start.1 = ((bf16[8,16,2048]{2,1,0:T(8,128)(2,1)}), bf16[8,16,2048]{2,1,0:T(8,128)(2,1)S(1)}, u32[]{:S(2)}, u32[]{:S(2)}) async-start(bf16[8,16,2048]{2,1,0:T(8,128)(2,1)} %get-tuple-element.64), calls=%async_computation.1 | async-start | bytes 1048576 | tf_op jit(solution)/shard_map/all_to_all | solution.py:364
  43.2 2.4 %place_straight.1 = bf16[64,8,1024]{2,1,0:T(8,128)(2,1)} custom-call(bf16[512,128]{1,0:T(8,128)(2,1)S(1)} %get-tuple-element.62.placing_ref, bf16[128,4096]{1,0:T(8,128)(2,1)S(1)} %bitcast.21, bf16[128,4096]{1,0:T(8,128)(2,1)S(1)} %bitcast.22, bf16[128,4096]{1,0:T(8,128)(2,1)S(1)} %bitcast.23, bf16[128,4096]{1,0:T(8,128)(2,1)S(1)} %bitcast.24), custom_call_target="tpu_custom_call" | custom-call | tf_op jit(solution)/shard_map/place_straight/pallas_call | solution.py:370
  45.7 2.2 %coef.1 = (bf16[512,64]{1,0:T(8,128)(2,1)S(1)}, bf16[64,256]{1,0:T(8,128)(2,1)}) custom-call(bf16[64,8,512]{2,1,0:T(8,128)(2,1)S(1)} %all-to-all-done.2.grad_ref, bf16[64,1024]{1,0:T(8,128)(2,1)} %bitcast.34), custom_call_target="tpu_custom_call" | custom-call | tf_op jit(solution)/shard_map/coef/pallas_call | solution.py:357
  47.8 13.4 %all-to-all-done.1.low_ref.high_ref = bf16[8,16,2048]{2,1,0:T(8,128)(2,1)S(1)} async-done(((bf16[8,16,2048]{2,1,0:T(8,128)(2,1)}), bf16[8,16,2048]{2,1,0:T(8,128)(2,1)S(1)}, u32[]{:S(2)}, u32[]{:S(2)}) %all-to-all-start.1) | async-done | bytes 524320 | tf_op jit(solution)/shard_map/all_to_all | solution.py:364
  61.2 4.6 %all-to-all-start.3 = ((bf16[64,8,1024]{2,1,0:T(8,128)(2,1)}), bf16[64,8,1024]{2,1,0:T(8,128)(2,1)S(1)}, u32[]{:S(2)}, u32[]{:S(2)}) async-start(bf16[64,8,1024]{2,1,0:T(8,128)(2,1)} %place_straight.1), calls=%async_computation.3 | async-start | bytes 2097152 | tf_op jit(solution)/shard_map/all_to_all | solution.py:383
  65.8 28.3 %all-gather = bf16[512,256]{1,0:T(8,128)(2,1)} all-gather(bf16[64,256]{1,0:T(8,128)(2,1)S(1)} %copy-done.8), channel_id=2, replica_groups=mesh['segment'=8,'owner'=64] {'segment'}, dimensions={0}, use_global_device_ids=true | all-gather | bytes 294912 | tf_op jit(solution)/shard_map/all_gather | solution.py:384
  94.1 6.2 %term.1 = bf16[64,8,2048]{2,1,0:T(8,128)(2,1)} custom-call(s32[1]{0:T(128)} %bitcast.10.place_ref, bf16[8,64,256]{2,1,0:T(8,128)(2,1)} %bitcast.30, bf16[512,4096]{1,0:T(8,128)(2,1)} %all-gather.4.cloned.1.call-done.low_ref.high_ref, bf16[512,4096]{1,0:T(8,128)(2,1)} %all-gather.4.cloned.1.call-done.low_ref.high_ref), custom_call_target="tpu_custom_call" | custom-call | tf_op jit(solution)/shard_map/term/pallas_call | solution.py:386
  100.3 0.0 copy-start.6
  100.3 1.0 copy-done.6
  101.2 15.2 %all-to-all-start.4 = ((bf16[64,8,2048]{2,1,0:T(8,128)(2,1)}), bf16[64,8,2048]{2,1,0:T(8,128)(2,1)S(1)}, u32[]{:S(2)}, u32[]{:S(2)}) async-start(bf16[64,8,2048]{2,1,0:T(8,128)(2,1)} %term.1), calls=%async_computation.4 | async-start | bytes 4194304 | tf_op jit(solution)/shard_map/all_to_all | solution.py:400
  116.5 2.8 %route.1 = (bf16[9,8,1024]{2,1,0:T(8,128)(2,1)}, bf16[9,8,1024]{2,1,0:T(8,128)(2,1)}, bf16[9,8,1024]{2,1,0:T(8,128)(2,1)}, bf16[9,8,1024]{2,1,0:T(8,128)(2,1)}, ...) custom-call(s32[1]{0:T(128)} %bitcast.4.member_ref, ...), custom_call_target="tpu_custom_call" | custom-call | tf_op jit(solution)/shard_map/route/pallas_call | solution.py:402
  119.3 2.4 %collective-permute-start = (bf16[9,8,1024]{2,1,0:T(8,128)(2,1)}, bf16[9,8,1024]{2,1,0:T(8,128)(2,1)S(1)}, u32[]{:S(2)}, u32[]{:S(2)}) collective-permute-start(bf16[9,8,1024]{2,1,0:T(8,128)(2,1)} %get-tuple-element.71), channel_id=1, source_target_pairs={{0,1},{1,0},{2,3},{3,2},{4,5},{5,4},{6,7},{7,6},{8,9},{9,8},{10,11... | collective-permute-start | bytes 442376 | tf_op jit(solution)/shard_map/ppermute | solution.py:421
  121.6 3.2 %collective-permute-start.1 = (bf16[9,8,1024]{2,1,0:T(8,128)(2,1)}, bf16[9,8,1024]{2,1,0:T(8,128)(2,1)}, u32[]{:S(2)}, u32[]{:S(2)}) collective-permute-start(bf16[9,8,1024]{2,1,0:T(8,128)(2,1)} %get-tuple-element.72), channel_id=1, source_target_pairs={{0,2},{1,3},{2,4},{3,5},{4,6},{5,7},{6,0},{7,1},{8,10},{9,11},{10,... | collective-permute-start | bytes 442376 | tf_op jit(solution)/shard_map/ppermute | solution.py:421
  124.8 3.4 %collective-permute-start.2 = (bf16[9,8,1024]{2,1,0:T(8,128)(2,1)}, bf16[9,8,1024]{2,1,0:T(8,128)(2,1)}, u32[]{:S(2)}, u32[]{:S(2)}) collective-permute-start(bf16[9,8,1024]{2,1,0:T(8,128)(2,1)} %get-tuple-element.73), channel_id=1, source_target_pairs={{0,3},{1,2},{2,5},{3,4},{4,7},{5,6},{6,1},{7,0},{8,11},{9,10},{10,... | collective-permute-start | bytes 442376 | tf_op jit(solution)/shard_map/ppermute | solution.py:421
  128.2 3.2 %collective-permute-start.3 = (bf16[9,8,1024]{2,1,0:T(8,128)(2,1)}, bf16[9,8,1024]{2,1,0:T(8,128)(2,1)}, u32[]{:S(2)}, u32[]{:S(2)}) collective-permute-start(bf16[9,8,1024]{2,1,0:T(8,128)(2,1)} %get-tuple-element.74), channel_id=1, source_target_pairs={{0,4},{1,5},{2,6},{3,7},{4,0},{5,1},{6,2},{7,3},{8,12},{9,13},{10,... | collective-permute-start | bytes 442376 | tf_op jit(solution)/shard_map/ppermute | solution.py:421
  131.4 3.8 %collective-permute-start.4 = (bf16[9,8,1024]{2,1,0:T(8,128)(2,1)}, bf16[9,8,1024]{2,1,0:T(8,128)(2,1)}, u32[]{:S(2)}, u32[]{:S(2)}) collective-permute-start(bf16[9,8,1024]{2,1,0:T(8,128)(2,1)} %get-tuple-element.75), channel_id=1, source_target_pairs={{0,5},{1,4},{2,7},{3,6},{4,1},{5,0},{6,3},{7,2},{8,13},{9,12},{10,... | collective-permute-start | bytes 442376 | tf_op jit(solution)/shard_map/ppermute | solution.py:421
  135.3 3.4 %collective-permute-start.5 = (bf16[9,8,1024]{2,1,0:T(8,128)(2,1)}, bf16[9,8,1024]{2,1,0:T(8,128)(2,1)}, u32[]{:S(2)}, u32[]{:S(2)}) collective-permute-start(bf16[9,8,1024]{2,1,0:T(8,128)(2,1)} %get-tuple-element.76), channel_id=1, source_target_pairs={{0,6},{1,7},{2,0},{3,1},{4,2},{5,3},{6,4},{7,5},{8,14},{9,15},{10,... | collective-permute-start | bytes 442376 | tf_op jit(solution)/shard_map/ppermute | solution.py:421
  138.7 0.0 collective-permute-done.1.refs_2_
  138.7 2.3 %collective-permute-start.6 = (bf16[9,8,1024]{2,1,0:T(8,128)(2,1)}, bf16[9,8,1024]{2,1,0:T(8,128)(2,1)}, u32[]{:S(2)}, u32[]{:S(2)}) collective-permute-start(bf16[9,8,1024]{2,1,0:T(8,128)(2,1)} %get-tuple-element.77), channel_id=1, source_target_pairs={{0,7},{1,6},{2,1},{3,0},{4,3},{5,2},{6,5},{7,4},{8,15},{9,14},{10,... | collective-permute-start | bytes 442376 | tf_op jit(solution)/shard_map/ppermute | solution.py:421
  141.1 4.7 %collective-permute-done.3.refs_4_ = bf16[9,8,1024]{2,1,0:T(8,128)(2,1)} collective-permute-done((bf16[9,8,1024]{2,1,0:T(8,128)(2,1)}, bf16[9,8,1024]{2,1,0:T(8,128)(2,1)}, u32[]{:S(2)}, u32[]{:S(2)}) %collective-permute-start.3) | collective-permute-done | bytes 147488 | tf_op jit(solution)/shard_map/ppermute | solution.py:421
  145.8 7.2 %collective-permute-done.4.refs_5_ = bf16[9,8,1024]{2,1,0:T(8,128)(2,1)} collective-permute-done((bf16[9,8,1024]{2,1,0:T(8,128)(2,1)}, bf16[9,8,1024]{2,1,0:T(8,128)(2,1)}, u32[]{:S(2)}, u32[]{:S(2)}) %collective-permute-start.4) | collective-permute-done | bytes 147488 | tf_op jit(solution)/shard_map/ppermute | solution.py:421
  153.0 4.6 %collective-permute-done.6.refs_7_ = bf16[9,8,1024]{2,1,0:T(8,128)(2,1)} collective-permute-done((bf16[9,8,1024]{2,1,0:T(8,128)(2,1)}, bf16[9,8,1024]{2,1,0:T(8,128)(2,1)}, u32[]{:S(2)}, u32[]{:S(2)}) %collective-permute-start.6) | collective-permute-done | bytes 147488 | tf_op jit(solution)/shard_map/ppermute | solution.py:421
  157.5 6.4 %bank_gradient.1 = (f32[64,4096]{1,0:T(8,128)}, f32[64,1024]{1,0:T(8,128)}, s32[1]{0:T(128)}) custom-call(s32[1]{0:T(128)} %bitcast.4.member_ref, bf16[64,8,1024]{2,1,0:T(8,128)(2,1)} %copy-done.6, bf16[8,8,8,512]{3,2,1,0:T(8,128)(2,1)} %bitcast.26, bf16[8,8,8,64]{3,2,1,0:T(8,128)(2,1)S(1)} %bitcast.32, bf16[64,4096]{1,0:T(8,128)(2,1)} %bitcast.28, ...), custom_call_target="tpu_custom_call" | custom-call | tf_op jit(solution)/shard_map/bank_gradient/pallas_call | solution.py:425
  163.9 2.2 %all-to-all-done.4.rows_ref = bf16[64,8,2048]{2,1,0:T(8,128)(2,1)S(1)} async-done(((bf16[64,8,2048]{2,1,0:T(8,128)(2,1)}), bf16[64,8,2048]{2,1,0:T(8,128)(2,1)S(1)}, u32[]{:S(2)}, u32[]{:S(2)}) %all-to-all-start.4) | async-done | bytes 2097184 | tf_op jit(solution)/shard_map/all_to_all | solution.py:400
  166.8 0.7 copy-done.1
  167.5 4.1 %unplace.1 = bf16[128,4096]{1,0:T(8,128)(2,1)} custom-call(bf16[256,512]{1,0:T(8,128)(2,1)} %get-tuple-element.63.back_ref, bf16[64,8,2048]{2,1,0:T(8,128)(2,1)} %copy-done.1), custom_call_target="tpu_custom_call" | custom-call | tf_op jit(solution)/shard_map/unplace/pallas_call | solution.py:470
  (17 shorter events, 0.0 us)
Async XLA Ops:
  7.2 14.8 %copy-start = (bf16[1,128,4096]{2,1,0:T(8,128)(2,1)S(1)}, bf16[1,128,4096]{2,1,0:T(8,128)(2,1)}, u32[]{:S(2)}) copy-start(bf16[1,128,4096]{2,1,0:T(8,128)(2,1)} %param.8) | copy-start | bytes 3145732
  7.2 86.9 %all-gather.4.cloned.1.call-start = ((), (), s32[]{:S(2)}) async-start(), calls=%async_computation.5 | async-start | bytes 4718592 | tf_op jit(solution)/shard_map/all_gather | solution.py:325
  10.4 29.3 %all-to-all-start.2 = ((bf16[64,8,512]{2,1,0:T(8,128)(2,1)}), bf16[64,8,512]{2,1,0:T(8,128)(2,1)S(1)}, u32[]{:S(2)}, u32[]{:S(2)}) async-start(bf16[64,8,512]{2,1,0:T(8,128)(2,1)} %get-tuple-element.65), calls=%async_computation.2 | async-start | bytes 1048576 | tf_op jit(solution)/shard_map/all_to_all | solution.py:336
  39.7 6.0 %copy-start.2 = (bf16[64,8,512]{2,1,0:T(8,128)(2,1)}, bf16[64,8,512]{2,1,0:T(8,128)(2,1)S(1)}, u32[]{:S(2)}) copy-start(bf16[64,8,512]{2,1,0:T(8,128)(2,1)S(1)} %all-to-all-done.2.grad_ref) | copy-start | bytes 1572868
  39.7 21.5 %all-to-all-start.1 = ((bf16[8,16,2048]{2,1,0:T(8,128)(2,1)}), bf16[8,16,2048]{2,1,0:T(8,128)(2,1)S(1)}, u32[]{:S(2)}, u32[]{:S(2)}) async-start(bf16[8,16,2048]{2,1,0:T(8,128)(2,1)} %get-tuple-element.64), calls=%async_computation.1 | async-start | bytes 1048576 | tf_op jit(solution)/shard_map/all_to_all | solution.py:364
  47.8 18.0 %copy-start.8 = (bf16[64,256]{1,0:T(8,128)(2,1)S(1)}, bf16[64,256]{1,0:T(8,128)(2,1)}, u32[]{:S(2)}) copy-start(bf16[64,256]{1,0:T(8,128)(2,1)} %get-tuple-element.81) | copy-start | bytes 98308
  61.2 39.1 %copy-start.5 = (bf16[8,16,2048]{2,1,0:T(8,128)(2,1)}, bf16[8,16,2048]{2,1,0:T(8,128)(2,1)S(1)}, u32[]{:S(2)}) copy-start(bf16[8,16,2048]{2,1,0:T(8,128)(2,1)S(1)} %all-to-all-done.1.low_ref.high_ref) | copy-start | bytes 1572868
  61.2 39.1 %all-to-all-start.3 = ((bf16[64,8,1024]{2,1,0:T(8,128)(2,1)}), bf16[64,8,1024]{2,1,0:T(8,128)(2,1)S(1)}, u32[]{:S(2)}, u32[]{:S(2)}) async-start(bf16[64,8,1024]{2,1,0:T(8,128)(2,1)} %place_straight.1), calls=%async_computation.3 | async-start | bytes 2097152 | tf_op jit(solution)/shard_map/all_to_all | solution.py:383
  100.3 1.0 copy-start.6
  101.2 64.9 %all-to-all-start.4 = ((bf16[64,8,2048]{2,1,0:T(8,128)(2,1)}), bf16[64,8,2048]{2,1,0:T(8,128)(2,1)S(1)}, u32[]{:S(2)}, u32[]{:S(2)}) async-start(bf16[64,8,2048]{2,1,0:T(8,128)(2,1)} %term.1), calls=%async_computation.4 | async-start | bytes 4194304 | tf_op jit(solution)/shard_map/all_to_all | solution.py:400
  119.3 16.0 %collective-permute-start = (bf16[9,8,1024]{2,1,0:T(8,128)(2,1)}, bf16[9,8,1024]{2,1,0:T(8,128)(2,1)S(1)}, u32[]{:S(2)}, u32[]{:S(2)}) collective-permute-start(bf16[9,8,1024]{2,1,0:T(8,128)(2,1)} %get-tuple-element.71), channel_id=1, source_target_pairs={{0,1},{1,0},{2,3},{3,2},{4,5},{5,4},{6,7},{7,6},{8,9},{9,8},{10,11... | collective-permute-start | bytes 442376 | tf_op jit(solution)/shard_map/ppermute | solution.py:421
  121.6 17.1 %collective-permute-start.1 = (bf16[9,8,1024]{2,1,0:T(8,128)(2,1)}, bf16[9,8,1024]{2,1,0:T(8,128)(2,1)}, u32[]{:S(2)}, u32[]{:S(2)}) collective-permute-start(bf16[9,8,1024]{2,1,0:T(8,128)(2,1)} %get-tuple-element.72), channel_id=1, source_target_pairs={{0,2},{1,3},{2,4},{3,5},{4,6},{5,7},{6,0},{7,1},{8,10},{9,11},{10,... | collective-permute-start | bytes 442376 | tf_op jit(solution)/shard_map/ppermute | solution.py:421
  124.8 16.2 %collective-permute-start.2 = (bf16[9,8,1024]{2,1,0:T(8,128)(2,1)}, bf16[9,8,1024]{2,1,0:T(8,128)(2,1)}, u32[]{:S(2)}, u32[]{:S(2)}) collective-permute-start(bf16[9,8,1024]{2,1,0:T(8,128)(2,1)} %get-tuple-element.73), channel_id=1, source_target_pairs={{0,3},{1,2},{2,5},{3,4},{4,7},{5,6},{6,1},{7,0},{8,11},{9,10},{10,... | collective-permute-start | bytes 442376 | tf_op jit(solution)/shard_map/ppermute | solution.py:421
  128.2 17.5 %collective-permute-start.3 = (bf16[9,8,1024]{2,1,0:T(8,128)(2,1)}, bf16[9,8,1024]{2,1,0:T(8,128)(2,1)}, u32[]{:S(2)}, u32[]{:S(2)}) collective-permute-start(bf16[9,8,1024]{2,1,0:T(8,128)(2,1)} %get-tuple-element.74), channel_id=1, source_target_pairs={{0,4},{1,5},{2,6},{3,7},{4,0},{5,1},{6,2},{7,3},{8,12},{9,13},{10,... | collective-permute-start | bytes 442376 | tf_op jit(solution)/shard_map/ppermute | solution.py:421
  131.4 21.5 %collective-permute-start.4 = (bf16[9,8,1024]{2,1,0:T(8,128)(2,1)}, bf16[9,8,1024]{2,1,0:T(8,128)(2,1)}, u32[]{:S(2)}, u32[]{:S(2)}) collective-permute-start(bf16[9,8,1024]{2,1,0:T(8,128)(2,1)} %get-tuple-element.75), channel_id=1, source_target_pairs={{0,5},{1,4},{2,7},{3,6},{4,1},{5,0},{6,3},{7,2},{8,13},{9,12},{10,... | collective-permute-start | bytes 442376 | tf_op jit(solution)/shard_map/ppermute | solution.py:421
  135.3 22.2 %copy-start.7 = (bf16[9,8,1024]{2,1,0:T(8,128)(2,1)}, bf16[9,8,1024]{2,1,0:T(8,128)(2,1)S(1)}, u32[]{:S(2)}) copy-start(bf16[9,8,1024]{2,1,0:T(8,128)(2,1)S(1)} %collective-permute-done.refs_1_) | copy-start | bytes 442372
  135.3 17.7 %collective-permute-start.5 = (bf16[9,8,1024]{2,1,0:T(8,128)(2,1)}, bf16[9,8,1024]{2,1,0:T(8,128)(2,1)}, u32[]{:S(2)}, u32[]{:S(2)}) collective-permute-start(bf16[9,8,1024]{2,1,0:T(8,128)(2,1)} %get-tuple-element.76), channel_id=1, source_target_pairs={{0,6},{1,7},{2,0},{3,1},{4,2},{5,3},{6,4},{7,5},{8,14},{9,15},{10,... | collective-permute-start | bytes 442376 | tf_op jit(solution)/shard_map/ppermute | solution.py:421
  138.7 18.8 %collective-permute-start.6 = (bf16[9,8,1024]{2,1,0:T(8,128)(2,1)}, bf16[9,8,1024]{2,1,0:T(8,128)(2,1)}, u32[]{:S(2)}, u32[]{:S(2)}) collective-permute-start(bf16[9,8,1024]{2,1,0:T(8,128)(2,1)} %get-tuple-element.77), channel_id=1, source_target_pairs={{0,7},{1,6},{2,1},{3,0},{4,3},{5,2},{6,5},{7,4},{8,15},{9,14},{10,... | collective-permute-start | bytes 442376 | tf_op jit(solution)/shard_map/ppermute | solution.py:421
  166.2 1.4 copy-start.1
Sparse Core Ops, SparseCore 0:
  10.1 63.7 all-gather.3

commit v8 on v4

--- a/solution.py
+++ b/solution.py
@@ -72,7 +72,7 @@
     low = dot(grads, up_ref[:, :width], ((1,), (1,)))
     high = dot(grads, up_ref[:, width:], ((1,), (1,)))
     part = jnp.where(half_of(low.shape) == 0, low, high)
-    coef = (adapter_scale * both_halves(part)).astype(bf16)
+    coef = both_halves(part).astype(bf16)
     coef_ref[...] = coef
     shape = (coef.shape[0], compact_ref.shape[1])
     row, column = iota(shape, 0), iota(shape, 1)
@@ -191,7 +191,7 @@
         coef_kernel,
         out_shape=(shape((slots, rank), bf16), shape((rank, slots // 2), bf16)),
         name="coef",
-    )(recv_grads, up_factor)
+    )(recv_grads * jnp.asarray(adapter_scale, bf16), up_factor)
 
     recv_inputs = lax.all_to_all(send_inputs, "owner", split_axis=0, concat_axis=0, tiled=True)
     all_coef = lax.all_gather(compact, "segment")

time: 165 us -> 164 us (level)
  transfers between devices with their start and end apart: 4 -> 4, of which waited for: 3 -> 3; matrix products, arithmetic and copies ran while one was open for 0% -> 1% of each run, Pallas kernels for 12% -> 13%
where the time goes in v8:
time: 164 us; the launch traced here: 163 us
  waiting for transfers between devices  69.5 us (42%)
  blocking collectives  29.3 us (18%)
  starting transfers between devices  24.6 us (15%)
  Pallas kernels  24.5 us (15%)
  between operations  14.1 us (9%)
    all_to_all x1, waiting for transfers between devices, local(): lax.all_to_all(terms, 'owner', split_axis=0, concat_axis=0, tiled=True)  45 us
    all_gather x1, blocking collectives, local(): all_coef = lax.all_gather(compact, 'segment')  29.3 us
    all_to_all x1, waiting for transfers between devices, local(): lax.all_to_all(send_grads, 'owner', split_axis=0, concat_axis=0, tiled=True)  12.7 us
    all_to_all x1, starting transfers between devices, local(): lax.all_to_all(send_grads, 'owner', split_axis=0, concat_axis=0, tiled=True)  11.6 us
    all_to_all x1, waiting for transfers between devices, local(): lax.all_to_all(send_inputs, 'owner', split_axis=0, concat_axis=0, tiled=T...  11 us
    all_to_all x1, starting transfers between devices, local(): lax.all_to_all(terms, 'owner', split_axis=0, concat_axis=0, tiled=True)  7.21 us
    pallas_call x1, Pallas kernels, local(): pl.pallas_call(term_kernel, grid=(steps,), in_specs=[pl.BlockSpec(memory_...  6.19 us
    all_to_all x1, starting transfers between devices, local(): lax.all_to_all(send_inputs, 'owner', split_axis=0, concat_axis=0, tiled=T...  5.72 us
  transfers between devices with their start and end apart: 4, of which 3 were waited for; matrix products, arithmetic and copies ran while one was open for 1% of the time, Pallas kernels for 13%

profile of v8, /device:TPU:1, one launch (start us, length us, event | category | flops | bytes accessed | tf_op | source)
XLA Modules:
  0.0 162.9 jit_solution(970249911402475204)
XLA Ops:
  7.2 0.0 all-gather.4.cloned.1.call-start
  7.2 0.7 all-gather.4.cloned.1.call-update
  7.9 2.5 %place_gradient.1 = (bf16[512,128]{1,0:T(8,128)(2,1)}, bf16[64,8,512]{2,1,0:T(8,128)(2,1)}) custom-call(s32[1,128]{1,0:T(1,128)} %bitcast.23, s32[1,64]{1,0:T(1,128)} %bitcast.24, bf16[128,1024]{1,0:T(8,128)(2,1)} %bitcast.21), custom_call_target="tpu_custom_call" | custom-call | tf_op jit(solution)/shard_map/place_gradient/pallas_call | solution.py:167
  10.4 11.6 %all-to-all-start = ((bf16[64,8,512]{2,1,0:T(8,128)(2,1)}), bf16[64,8,512]{2,1,0:T(8,128)(2,1)S(1)}, u32[]{:S(2)}, u32[]{:S(2)}) async-start(bf16[64,8,512]{2,1,0:T(8,128)(2,1)} %get-tuple-element.13), calls=%async_computation | async-start | bytes 1048576 | tf_op jit(solution)/shard_map/all_to_all | solution.py:172
  22.0 5.0 %place_inputs.1 = (bf16[64,8,2048]{2,1,0:T(8,128)(2,1)}, bf16[256,512]{1,0:T(8,128)(2,1)}) custom-call(bf16[512,128]{1,0:T(8,128)(2,1)} %get-tuple-element.11.placing_ref, bf16[128,4096]{1,0:T(8,128)(2,1)} %bitcast.15, bf16[128,4096]{1,0:T(8,128)(2,1)} %bitcast.16), custom_call_target="tpu_custom_call" | custom-call | tf_op jit(solution)/shard_map/place_inputs/pallas_call | solution.py:174
  27.0 12.7 %all-to-all-done.grads_ref = bf16[64,8,512]{2,1,0:T(8,128)(2,1)S(1)} async-done(((bf16[64,8,512]{2,1,0:T(8,128)(2,1)}), bf16[64,8,512]{2,1,0:T(8,128)(2,1)S(1)}, u32[]{:S(2)}, u32[]{:S(2)}) %all-to-all-start) | async-done | bytes 524320 | tf_op jit(solution)/shard_map/all_to_all | solution.py:172
  39.7 0.0 copy-start.1
  39.7 5.7 %all-to-all-start.2 = ((bf16[64,8,2048]{2,1,0:T(8,128)(2,1)}), bf16[64,8,2048]{2,1,0:T(8,128)(2,1)S(1)}, u32[]{:S(2)}, u32[]{:S(2)}) async-start(bf16[64,8,2048]{2,1,0:T(8,128)(2,1)} %get-tuple-element.15), calls=%async_computation.2 | async-start | bytes 4194304 | tf_op jit(solution)/shard_map/all_to_all | solution.py:196
  45.4 0.0 copy-done.1
  45.4 0.8 broadcast_multiply_fusion.grad_ref
  46.3 2.3 %coef.1 = (bf16[512,64]{1,0:T(8,128)(2,1)}, bf16[64,256]{1,0:T(8,128)(2,1)}) custom-call(bf16[64,8,512]{2,1,0:T(8,128)(2,1)} %broadcast_multiply_fusion.grad_ref, bf16[64,1024]{1,0:T(8,128)(2,1)} %bitcast.22), custom_call_target="tpu_custom_call" | custom-call | tf_op jit(solution)/shard_map/coef/pallas_call | solution.py:190
  48.6 29.3 %all-gather = bf16[512,256]{1,0:T(8,128)(2,1)} all-gather(bf16[64,256]{1,0:T(8,128)(2,1)} %get-tuple-element.14), channel_id=2, replica_groups=mesh['segment'=8,'owner'=64] {'segment'}, dimensions={0}, use_global_device_ids=true | all-gather | bytes 294912 | tf_op jit(solution)/shard_map/all_gather | solution.py:197
  77.9 0.0 all-gather.4.cloned.1.call-done.low_ref.high_ref
  77.9 6.2 %term.1 = bf16[64,8,2048]{2,1,0:T(8,128)(2,1)} custom-call(s32[1]{0:T(128)} %bitcast.4.place_ref, bf16[8,64,256]{2,1,0:T(8,128)(2,1)} %bitcast.19, bf16[512,4096]{1,0:T(8,128)(2,1)} %all-gather.4.cloned.1.call-done.low_ref.high_ref, bf16[512,4096]{1,0:T(8,128)(2,1)} %all-gather.4.cloned.1.call-done.low_ref.high_ref), custom_call_target="tpu_custom_call" | custom-call | tf_op jit(solution)/shard_map/term/pallas_call | solution.py:199
  84.1 11.0 %all-to-all-done.2.rows_ref = bf16[64,8,2048]{2,1,0:T(8,128)(2,1)S(1)} async-done(((bf16[64,8,2048]{2,1,0:T(8,128)(2,1)}), bf16[64,8,2048]{2,1,0:T(8,128)(2,1)S(1)}, u32[]{:S(2)}, u32[]{:S(2)}) %all-to-all-start.2) | async-done | bytes 2097184 | tf_op jit(solution)/shard_map/all_to_all | solution.py:196
  95.1 0.0 copy-start
  95.1 7.2 %all-to-all-start.1 = ((bf16[64,8,2048]{2,1,0:T(8,128)(2,1)}), bf16[64,8,2048]{2,1,0:T(8,128)(2,1)}, u32[]{:S(2)}, u32[]{:S(2)}) async-start(bf16[64,8,2048]{2,1,0:T(8,128)(2,1)} %term.1), calls=%async_computation.1 | async-start | bytes 4194304 | tf_op jit(solution)/shard_map/all_to_all | solution.py:213
  102.3 0.0 copy-done
  102.3 4.5 %weight_gradient.1 = (f32[64,4096]{1,0:T(8,128)}, f32[64,1024]{1,0:T(8,128)}) custom-call(bf16[64,8,2048]{2,1,0:T(8,128)(2,1)} %copy-done, bf16[64,8,512]{2,1,0:T(8,128)(2,1)} %copy-done.1, bf16[512,64]{1,0:T(8,128)(2,1)} %get-tuple-element.16.coef_ref, bf16[64,4096]{1,0:T(8,128)(2,1)} %bitcast.18), custom_call_target="tpu_custom_call" | custom-call | tf_op jit(solution)/shard_map/weight_gradient/pallas_call | solution.py:215
  106.9 45.0 %all-to-all-done.1.rows_ref = bf16[64,8,2048]{2,1,0:T(8,128)(2,1)} async-done(((bf16[64,8,2048]{2,1,0:T(8,128)(2,1)}), bf16[64,8,2048]{2,1,0:T(8,128)(2,1)}, u32[]{:S(2)}, u32[]{:S(2)}) %all-to-all-start.1) | async-done | bytes 2097184 | tf_op jit(solution)/shard_map/all_to_all | solution.py:213
  151.9 4.1 %unplace.1 = bf16[128,4096]{1,0:T(8,128)(2,1)} custom-call(bf16[256,512]{1,0:T(8,128)(2,1)} %get-tuple-element.12.back_ref, bf16[64,8,2048]{2,1,0:T(8,128)(2,1)} %all-to-all-done.1.rows_ref), custom_call_target="tpu_custom_call" | custom-call | tf_op jit(solution)/shard_map/unplace/pallas_call | solution.py:221
Async XLA Ops:
  7.2 70.7 %all-gather.4.cloned.1.call-start = ((), (), s32[]{:S(2)}) async-start(), calls=%async_computation.3 | async-start | bytes 4718592 | tf_op jit(solution)/shard_map/all_gather | solution.py:165
  10.4 29.3 %all-to-all-start = ((bf16[64,8,512]{2,1,0:T(8,128)(2,1)}), bf16[64,8,512]{2,1,0:T(8,128)(2,1)S(1)}, u32[]{:S(2)}, u32[]{:S(2)}) async-start(bf16[64,8,512]{2,1,0:T(8,128)(2,1)} %get-tuple-element.13), calls=%async_computation | async-start | bytes 1048576 | tf_op jit(solution)/shard_map/all_to_all | solution.py:172
  39.7 5.7 %copy-start.1 = (bf16[64,8,512]{2,1,0:T(8,128)(2,1)}, bf16[64,8,512]{2,1,0:T(8,128)(2,1)S(1)}, u32[]{:S(2)}) copy-start(bf16[64,8,512]{2,1,0:T(8,128)(2,1)S(1)} %all-to-all-done.grads_ref) | copy-start | bytes 1572868
  39.7 55.4 %all-to-all-start.2 = ((bf16[64,8,2048]{2,1,0:T(8,128)(2,1)}), bf16[64,8,2048]{2,1,0:T(8,128)(2,1)S(1)}, u32[]{:S(2)}, u32[]{:S(2)}) async-start(bf16[64,8,2048]{2,1,0:T(8,128)(2,1)} %get-tuple-element.15), calls=%async_computation.2 | async-start | bytes 4194304 | tf_op jit(solution)/shard_map/all_to_all | solution.py:196
  95.1 7.2 %copy-start = (bf16[64,8,2048]{2,1,0:T(8,128)(2,1)}, bf16[64,8,2048]{2,1,0:T(8,128)(2,1)S(1)}, u32[]{:S(2)}) copy-start(bf16[64,8,2048]{2,1,0:T(8,128)(2,1)S(1)} %all-to-all-done.2.rows_ref) | copy-start | bytes 6291460
  95.1 56.8 %all-to-all-start.1 = ((bf16[64,8,2048]{2,1,0:T(8,128)(2,1)}), bf16[64,8,2048]{2,1,0:T(8,128)(2,1)}, u32[]{:S(2)}, u32[]{:S(2)}) async-start(bf16[64,8,2048]{2,1,0:T(8,128)(2,1)} %term.1), calls=%async_computation.1 | async-start | bytes 4194304 | tf_op jit(solution)/shard_map/all_to_all | solution.py:213
Sparse Core Ops, SparseCore 0:
  10.1 65.3 all-gather.3

commit v9 on v4

--- a/solution.py
+++ b/solution.py
@@ -27,21 +27,22 @@
 def place_gradient_kernel(tenant_ref, owner_ref, grad_ref, placing_ref, send_ref):
     tok_rows = tenant_ref.shape[1]
     owners = owner_ref.shape[1]
-    slots = owners * group
+    width = grad_ref.shape[1] // 2
     named = iota((owners, tok_rows), 0) == tenant_ref[...]
     before = (iota((tok_rows, tok_rows), 0) < iota((tok_rows, tok_rows), 1)).astype(bf16)
     rank = dot(named.astype(bf16), before, ((1,), (0,)))
     key = jnp.where(named, rank + 1.0, 0.0).astype(bf16)
-    held = (iota((slots, owners), 0) // group == owner_ref[...]).astype(bf16)
-    wide_key = dot(held, key, ((1,), (0,)))
-    index = (iota((slots, tok_rows), 0) % row_limit + 1).astype(f32)
-    placing = wide_key == index
-    placing_ref[...] = placing.astype(bf16)
-    half = half_of((slots, tok_rows))
-    width = grad_ref.shape[1] // 2
-    lower = jnp.where(placing & (half == 0), 1.0, 0.0).astype(bf16)
-    upper = jnp.where(placing & (half == 1), 1.0, 0.0).astype(bf16)
-    sent = dot(lower, grad_ref[:, :width], ((1,), (0,))) + dot(upper, grad_ref[:, width:], ((1,), (0,)))
+    held = (iota((owners, owners), 0) == owner_ref[...]).astype(bf16)
+    key = dot(held, key, ((1,), (0,)))
+    blocks = (owners, group, tok_rows)
+    line = iota(blocks, 1)
+    placing = jnp.broadcast_to(key[:, None, :], blocks) == (line % row_limit + 1).astype(f32)
+    rows = (owners * group, tok_rows)
+    placing_ref[...] = jnp.where(placing, 1.0, 0.0).reshape(rows).astype(bf16)
+    lower = jnp.where(placing & (line < row_limit), 1.0, 0.0).reshape(rows).astype(bf16)
+    upper = jnp.where(placing & (line >= row_limit), 1.0, 0.0).reshape(rows).astype(bf16)
+    grads = jnp.concatenate([grad_ref[:, :width], grad_ref[:, width:]], axis=0)
+    sent = dot(jnp.concatenate([lower, upper], axis=1), grads, ((1,), (0,)))
     send_ref[...] = sent.astype(bf16).reshape(send_ref.shape)
 
 
@@ -127,15 +128,31 @@
     grad_up_ref[:, out_width:] = up[rank:]
 
 
-def unplace_kernel(back_ref, rows_ref, out_ref):
-    tok_rows = out_ref.shape[0]
+def unplace_kernel(back_ref, rows_ref, out_hbm, out_ref, sems):
+    steps = out_ref.shape[0]
+    tok_rows = out_hbm.shape[0]
     block = rows_ref.shape[2]
+    step = pl.program_id(0)
+
+    def write(c, h):
+        start = pl.multiple_of((h * steps + c) * block, block)
+        here = out_hbm.at[:, pl.ds(start, block)]
+        return pltpu.make_async_copy(out_ref.at[c, pl.ds(h * tok_rows, tok_rows)], here, sems.at[c, h])
+
     rows = rows_ref[...].reshape(back_ref.shape[1], block)
-    both = dot(back_ref[...], rows, ((1,), (0,))).astype(bf16)
-    start = pl.multiple_of(pl.program_id(0) * block, block)
-    out_ref[:, pl.ds(start, block)] = both[:tok_rows]
-    start = pl.multiple_of(out_ref.shape[1] // 2 + pl.program_id(0) * block, block)
-    out_ref[:, pl.ds(start, block)] = both[tok_rows:]
+    out_ref[step] = dot(back_ref[...], rows, ((1,), (0,))).astype(bf16)
+    write(step, 0).start()
+    write(step, 1).start()
+
+    @pl.when(step == steps - 1)
+    def _():
+        for c in range(steps):
+            write(c, 0).wait()
+            write(c, 1).wait()
+
+
+def exchange(blocks):
+    return lax.all_to_all(blocks, "owner", split_axis=0, concat_axis=0, tiled=True)
 
 
 def local(
@@ -161,6 +178,7 @@
     steps = 4
     block = half_width // steps
     shape = jax.ShapeDtypeStruct
+    vmem = pl.BlockSpec(memory_space=pltpu.VMEM)
 
     all_down = lax.all_gather(down_factor, "segment").reshape(sections * rank, width)
 
@@ -169,7 +187,7 @@
         out_shape=(shape((slots, tok_rows), bf16), shape((owners, group, out_width // 2), bf16)),
         name="place_gradient",
     )(tenant.reshape(1, tok_rows), adapter_owner_index.reshape(1, owners), gradient_list)
-    recv_grads = lax.all_to_all(send_grads, "owner", split_axis=0, concat_axis=0, tiled=True)
+    recv_grads = pltpu.with_memory_space_constraint(exchange(send_grads), pltpu.VMEM)
 
     send_inputs, back = pl.pallas_call(
         place_inputs_kernel,
@@ -189,11 +207,12 @@
 
     coef, compact = pl.pallas_call(
         coef_kernel,
+        in_specs=[vmem, vmem],
         out_shape=(shape((slots, rank), bf16), shape((rank, slots // 2), bf16)),
         name="coef",
     )(recv_grads, up_factor)
 
-    recv_inputs = lax.all_to_all(send_inputs, "owner", split_axis=0, concat_axis=0, tiled=True)
+    recv_inputs = pltpu.with_memory_space_constraint(exchange(send_inputs), pltpu.VMEM)
     all_coef = lax.all_gather(compact, "segment")
 
     terms = pl.pallas_call(
@@ -210,23 +229,30 @@
         scratch_shapes=[pltpu.VMEM((slots, sections * rank), bf16)],
         name="term",
     )(place, all_coef, all_down, all_down)
-    returned = lax.all_to_all(terms, "owner", split_axis=0, concat_axis=0, tiled=True)
+    returned = exchange(terms)
 
     grad_down, grad_up = pl.pallas_call(
         weight_gradient_kernel,
+        in_specs=[vmem, vmem, vmem, vmem],
         out_shape=(shape((rank, width), f32), shape((rank, out_width), f32)),
         name="weight_gradient",
     )(recv_inputs, recv_grads, coef, down_factor)
 
+    back_steps = 2
+    back_block = half_width // back_steps
     passed = pl.pallas_call(
         unplace_kernel,
-        grid=(steps,),
+        grid=(back_steps,),
         in_specs=[
             pl.BlockSpec((2 * tok_rows, slots), lambda c: (0, 0)),
-            pl.BlockSpec((owners, group, block), lambda c: (0, 0, c)),
-        ],
-        out_specs=pl.BlockSpec((tok_rows, width), lambda c: (0, 0)),
+            pl.BlockSpec((owners, group, back_block), lambda c: (0, 0, c)),
+        ],
+        out_specs=pl.BlockSpec(memory_space=pl.ANY),
         out_shape=shape((tok_rows, width), bf16),
+        scratch_shapes=[
+            pltpu.VMEM((back_steps, 2 * tok_rows, back_block), bf16),
+            pltpu.SemaphoreType.DMA((back_steps, 2)),
+        ],
         name="unplace",
     )(back, returned)
 

time: 165 us -> 163 us (0.988)
  Pallas kernels: 24.5 us -> 22.5 us
    pallas_call x3, Pallas kernels: 10.9 us -> 9.07 us  [the longest x1 3.93 us: local(): pl.pallas_call(weight_gradient_kernel, in_specs=[vmem, vmem, vmem, vmem],...]
where the time goes in v9:
time: 163 us; the launch traced here: 162 us
  waiting for transfers between devices  70.8 us (43%)
  blocking collectives  29.6 us (18%)
  starting transfers between devices  24.6 us (15%)
  Pallas kernels  22.5 us (14%)
  between operations  14.1 us (9%)
    all_to_all x3, waiting for transfers between devices, exchange(): lax.all_to_all(blocks, 'owner', split_axis=0, concat_axis=0, tiled=True)  70.2 us
    all_gather x1, blocking collectives, local(): all_coef = lax.all_gather(compact, 'segment')  29.6 us
    all_to_all x3, starting transfers between devices, exchange(): lax.all_to_all(blocks, 'owner', split_axis=0, concat_axis=0, tiled=True)  24.6 us
    pallas_call x1, Pallas kernels, local(): pl.pallas_call(term_kernel, grid=(steps,), in_specs=[pl.BlockSpec(memory_...  6.18 us
    pallas_call x1, Pallas kernels, local(): pl.pallas_call(place_inputs_kernel, grid=(steps,), in_specs=[pl.BlockSpec...  4.97 us
    pallas_call x1, Pallas kernels, local(): pl.pallas_call(weight_gradient_kernel, in_specs=[vmem, vmem, vmem, vmem],...  3.93 us
  transfers between devices with their start and end apart: 4, of which 3 were waited for; matrix products, arithmetic and copies ran while one was open for 0% of the time, Pallas kernels for 12%

profile of v9, /device:TPU:1, one launch (start us, length us, event | category | flops | bytes accessed | tf_op | source)
XLA Modules:
  0.0 161.6 jit_solution(15190422790447000373)
XLA Ops:
  7.2 0.0 all-gather.4.cloned.1.call-start
  7.2 0.7 all-gather.4.cloned.1.call-update
  7.9 2.3 %place_gradient.1 = (bf16[512,128]{1,0:T(8,128)(2,1)}, bf16[64,8,512]{2,1,0:T(8,128)(2,1)}) custom-call(s32[1,128]{1,0:T(1,128)} %bitcast.23, s32[1,64]{1,0:T(1,128)} %bitcast.24, bf16[128,1024]{1,0:T(8,128)(2,1)} %bitcast.21), custom_call_target="tpu_custom_call" | custom-call | tf_op jit(solution)/shard_map/place_gradient/pallas_call | solution.py:185
  10.2 11.6 %all-to-all-start = ((bf16[64,8,512]{2,1,0:T(8,128)(2,1)}), bf16[64,8,512]{2,1,0:T(8,128)(2,1)S(1)}, u32[]{:S(2)}, u32[]{:S(2)}) async-start(bf16[64,8,512]{2,1,0:T(8,128)(2,1)} %get-tuple-element.13), calls=%async_computation | async-start | bytes 1048576 | tf_op jit(solution)/shard_map/all_to_all | solution.py:155
  21.8 5.0 %place_inputs.1 = (bf16[64,8,2048]{2,1,0:T(8,128)(2,1)}, bf16[256,512]{1,0:T(8,128)(2,1)}) custom-call(bf16[512,128]{1,0:T(8,128)(2,1)} %get-tuple-element.11.placing_ref, bf16[128,4096]{1,0:T(8,128)(2,1)} %bitcast.15, bf16[128,4096]{1,0:T(8,128)(2,1)} %bitcast.16), custom_call_target="tpu_custom_call" | custom-call | tf_op jit(solution)/shard_map/place_inputs/pallas_call | solution.py:192
  26.8 12.8 %all-to-all-done.grad_ref.grads_ref = bf16[64,8,512]{2,1,0:T(8,128)(2,1)S(1)} async-done(((bf16[64,8,512]{2,1,0:T(8,128)(2,1)}), bf16[64,8,512]{2,1,0:T(8,128)(2,1)S(1)}, u32[]{:S(2)}, u32[]{:S(2)}) %all-to-all-start) | async-done | bytes 524320 | tf_op jit(solution)/shard_map/all_to_all | solution.py:155
  39.6 5.7 %all-to-all-start.2 = ((bf16[64,8,2048]{2,1,0:T(8,128)(2,1)}), bf16[64,8,2048]{2,1,0:T(8,128)(2,1)S(1)}, u32[]{:S(2)}, u32[]{:S(2)}) async-start(bf16[64,8,2048]{2,1,0:T(8,128)(2,1)} %get-tuple-element.15), calls=%async_computation.2 | async-start | bytes 4194304 | tf_op jit(solution)/shard_map/all_to_all | solution.py:155
  45.3 2.2 %coef.1 = (bf16[512,64]{1,0:T(8,128)(2,1)}, bf16[64,256]{1,0:T(8,128)(2,1)}) custom-call(bf16[64,8,512]{2,1,0:T(8,128)(2,1)S(1)} %all-to-all-done.grad_ref.grads_ref, bf16[64,1024]{1,0:T(8,128)(2,1)} %bitcast.22), custom_call_target="tpu_custom_call" | custom-call | tf_op jit(solution)/shard_map/coef/pallas_call | solution.py:208
  47.4 29.6 %all-gather = bf16[512,256]{1,0:T(8,128)(2,1)} all-gather(bf16[64,256]{1,0:T(8,128)(2,1)} %get-tuple-element.14), channel_id=2, replica_groups=mesh['segment'=8,'owner'=64] {'segment'}, dimensions={0}, use_global_device_ids=true | all-gather | bytes 294912 | tf_op jit(solution)/shard_map/all_gather | solution.py:216
  77.0 0.0 all-gather.4.cloned.1.call-done.low_ref.high_ref
  77.0 6.2 %term.1 = bf16[64,8,2048]{2,1,0:T(8,128)(2,1)} custom-call(s32[1]{0:T(128)} %bitcast.4.place_ref, bf16[8,64,256]{2,1,0:T(8,128)(2,1)} %bitcast.19, bf16[512,4096]{1,0:T(8,128)(2,1)} %all-gather.4.cloned.1.call-done.low_ref.high_ref, bf16[512,4096]{1,0:T(8,128)(2,1)} %all-gather.4.cloned.1.call-done.low_ref.high_ref), custom_call_target="tpu_custom_call" | custom-call | tf_op jit(solution)/shard_map/term/pallas_call | solution.py:218
  83.2 11.8 %all-to-all-done.2.rows_ref = bf16[64,8,2048]{2,1,0:T(8,128)(2,1)S(1)} async-done(((bf16[64,8,2048]{2,1,0:T(8,128)(2,1)}), bf16[64,8,2048]{2,1,0:T(8,128)(2,1)S(1)}, u32[]{:S(2)}, u32[]{:S(2)}) %all-to-all-start.2) | async-done | bytes 2097184 | tf_op jit(solution)/shard_map/all_to_all | solution.py:155
  95.0 7.2 %all-to-all-start.1 = ((bf16[64,8,2048]{2,1,0:T(8,128)(2,1)}), bf16[64,8,2048]{2,1,0:T(8,128)(2,1)}, u32[]{:S(2)}, u32[]{:S(2)}) async-start(bf16[64,8,2048]{2,1,0:T(8,128)(2,1)} %term.1), calls=%async_computation.1 | async-start | bytes 4194304 | tf_op jit(solution)/shard_map/all_to_all | solution.py:155
  102.2 3.9 %weight_gradient.1 = (f32[64,4096]{1,0:T(8,128)}, f32[64,1024]{1,0:T(8,128)}) custom-call(bf16[64,8,2048]{2,1,0:T(8,128)(2,1)S(1)} %all-to-all-done.2.rows_ref, bf16[64,8,512]{2,1,0:T(8,128)(2,1)S(1)} %all-to-all-done.grad_ref.grads_ref, bf16[512,64]{1,0:T(8,128)(2,1)} %get-tuple-element.16.coef_ref, bf16[64,4096]{1,0:T(8,128)(2,1)} %bitcast.18), custom_call_target="tpu_custom_call" | custom-call | tf_op jit(solution)/shard_map/weight_gradient/pallas_call | solution.py:234
  106.1 45.7 %all-to-all-done.1.rows_ref = bf16[64,8,2048]{2,1,0:T(8,128)(2,1)} async-done(((bf16[64,8,2048]{2,1,0:T(8,128)(2,1)}), bf16[64,8,2048]{2,1,0:T(8,128)(2,1)}, u32[]{:S(2)}, u32[]{:S(2)}) %all-to-all-start.1) | async-done | bytes 2097184 | tf_op jit(solution)/shard_map/all_to_all | solution.py:155
  151.8 3.0 %unplace.1 = bf16[128,4096]{1,0:T(8,128)(2,1)} custom-call(bf16[256,512]{1,0:T(8,128)(2,1)} %get-tuple-element.12.back_ref, bf16[64,8,2048]{2,1,0:T(8,128)(2,1)} %all-to-all-done.1.rows_ref), custom_call_target="tpu_custom_call" | custom-call | tf_op jit(solution)/shard_map/unplace/pallas_call | solution.py:243
Async XLA Ops:
  7.2 69.9 %all-gather.4.cloned.1.call-start = ((), (), s32[]{:S(2)}) async-start(), calls=%async_computation.3 | async-start | bytes 4718592 | tf_op jit(solution)/shard_map/all_gather | solution.py:183
  10.2 29.3 %all-to-all-start = ((bf16[64,8,512]{2,1,0:T(8,128)(2,1)}), bf16[64,8,512]{2,1,0:T(8,128)(2,1)S(1)}, u32[]{:S(2)}, u32[]{:S(2)}) async-start(bf16[64,8,512]{2,1,0:T(8,128)(2,1)} %get-tuple-element.13), calls=%async_computation | async-start | bytes 1048576 | tf_op jit(solution)/shard_map/all_to_all | solution.py:155
  39.6 55.4 %all-to-all-start.2 = ((bf16[64,8,2048]{2,1,0:T(8,128)(2,1)}), bf16[64,8,2048]{2,1,0:T(8,128)(2,1)S(1)}, u32[]{:S(2)}, u32[]{:S(2)}) async-start(bf16[64,8,2048]{2,1,0:T(8,128)(2,1)} %get-tuple-element.15), calls=%async_computation.2 | async-start | bytes 4194304 | tf_op jit(solution)/shard_map/all_to_all | solution.py:155
  95.0 56.8 %all-to-all-start.1 = ((bf16[64,8,2048]{2,1,0:T(8,128)(2,1)}), bf16[64,8,2048]{2,1,0:T(8,128)(2,1)}, u32[]{:S(2)}, u32[]{:S(2)}) async-start(bf16[64,8,2048]{2,1,0:T(8,128)(2,1)} %term.1), calls=%async_computation.1 | async-start | bytes 4194304 | tf_op jit(solution)/shard_map/all_to_all | solution.py:155
Sparse Core Ops, SparseCore 0:
  10.1 65.6 all-gather.3

commit v10 on v9

--- a/solution.py
+++ b/solution.py
@@ -73,17 +73,20 @@
     low = dot(grads, up_ref[:, :width], ((1,), (1,)))
     high = dot(grads, up_ref[:, width:], ((1,), (1,)))
     part = jnp.where(half_of(low.shape) == 0, low, high)
-    coef = (adapter_scale * both_halves(part)).astype(bf16)
+    exact = adapter_scale * both_halves(part)
+    coef = exact.astype(bf16)
+    rest = (exact - coef.astype(f32)).astype(bf16)
     coef_ref[...] = coef
     shape = (coef.shape[0], compact_ref.shape[1])
     row, column = iota(shape, 0), iota(shape, 1)
     first = row // group * group + row % row_limit == column // row_limit * group + column % row_limit
     picked = jnp.where(first & (half_of(shape) == 0), 1.0, 0.0).astype(bf16)
-    compact_ref[...] = dot(coef, picked, ((0,), (0,))).astype(bf16)
+    compact_ref[...] = dot(jnp.concatenate([coef, rest], axis=1), picked, ((0,), (0,))).astype(bf16)
 
 
 def term_kernel(place_ref, coef_ref, low_ref, high_ref, out_ref, wide_ref):
     sections, rank, columns = coef_ref.shape
+    rank = rank // 2
 
     @pl.when(pl.program_id(0) == 0)
     def _():
@@ -91,16 +94,18 @@
         parts = []
         for k in range(sections):
             parts.append(jnp.where(place <= k, coef_ref[k], jnp.zeros_like(coef_ref[k])))
-        shape = (columns, wide_ref.shape[0])
+        shape = (columns, wide_ref.shape[1])
         column, row = iota(shape, 0), iota(shape, 1)
         same = column == row // group * row_limit + row % row_limit
         spread = jnp.where(same, 1.0, 0.0).astype(bf16)
-        wide = dot(jnp.concatenate(parts, axis=0), spread, ((1,), (0,)))
-        wide_ref[...] = wide.T.astype(bf16)
-
-    coef = wide_ref[...]
-    low = dot(coef, low_ref[...], ((1,), (0,)))
-    high = dot(coef, high_ref[...], ((1,), (0,)))
+        for level in range(2):
+            here = slice(level * rank, (level + 1) * rank)
+            wide = dot(jnp.concatenate([part[here] for part in parts], axis=0), spread, ((1,), (0,)))
+            wide_ref[level] = wide.T.astype(bf16)
+
+    coef, rest = wide_ref[0], wide_ref[1]
+    low = dot(coef, low_ref[...], ((1,), (0,))) + dot(rest, low_ref[...], ((1,), (0,)))
+    high = dot(coef, high_ref[...], ((1,), (0,))) + dot(rest, high_ref[...], ((1,), (0,)))
     out = jnp.where(half_of(low.shape) == 0, low, high)
     out_ref[...] = out.astype(bf16).reshape(out_ref.shape)
 
@@ -208,7 +213,7 @@
     coef, compact = pl.pallas_call(
         coef_kernel,
         in_specs=[vmem, vmem],
-        out_shape=(shape((slots, rank), bf16), shape((rank, slots // 2), bf16)),
+        out_shape=(shape((slots, rank), bf16), shape((2 * rank, slots // 2), bf16)),
         name="coef",
     )(recv_grads, up_factor)
 
@@ -220,13 +225,13 @@
         grid=(steps,),
         in_specs=[
             pl.BlockSpec(memory_space=pltpu.SMEM),
-            pl.BlockSpec((sections, rank, slots // 2), lambda c: (0, 0, 0)),
+            pl.BlockSpec((sections, 2 * rank, slots // 2), lambda c: (0, 0, 0)),
             pl.BlockSpec((sections * rank, block), lambda c: (0, c)),
             pl.BlockSpec((sections * rank, block), lambda c: (0, c + steps)),
         ],
         out_specs=pl.BlockSpec((owners, group, block), lambda c: (0, 0, c)),
         out_shape=shape((owners, group, half_width), bf16),
-        scratch_shapes=[pltpu.VMEM((slots, sections * rank), bf16)],
+        scratch_shapes=[pltpu.VMEM((2, slots, sections * rank), bf16)],
         name="term",
     )(place, all_coef, all_down, all_down)
     returned = exchange(terms)

time: 163 us -> 163 us (level)
  waiting for transfers between devices: 70.8 us -> 67.3 us
  Pallas kernels: 22.5 us -> 24.5 us
    all_to_all x3, waiting for transfers between devices: 70.2 us -> 66.6 us  [exchange(): lax.all_to_all(blocks, 'owner', split_axis=0, concat_axis=0, tiled=True)]
    pallas_call x1, Pallas kernels: 6.18 us -> 8 us  [local(): pl.pallas_call(term_kernel, grid=(steps,), in_specs=[pl.BlockSpec(memory_...]
  transfers between devices with their start and end apart: 4 -> 4, of which waited for: 3 -> 3; matrix products, arithmetic and copies ran while one was open for 0% -> 0% of each run, Pallas kernels for 12% -> 13%
where the time goes in v10:
time: 163 us; the launch traced here: 162 us
  waiting for transfers between devices  67.3 us (41%)
  blocking collectives  31.2 us (19%)
  starting transfers between devices  24.6 us (15%)
  Pallas kernels  24.5 us (15%)
  between operations  14.1 us (9%)
    all_to_all x3, waiting for transfers between devices, exchange(): lax.all_to_all(blocks, 'owner', split_axis=0, concat_axis=0, tiled=True)  66.6 us
    all_gather x1, blocking collectives, local(): all_coef = lax.all_gather(compact, 'segment')  31.2 us
    all_to_all x3, starting transfers between devices, exchange(): lax.all_to_all(blocks, 'owner', split_axis=0, concat_axis=0, tiled=True)  24.6 us
    pallas_call x1, Pallas kernels, local(): pl.pallas_call(term_kernel, grid=(steps,), in_specs=[pl.BlockSpec(memory_...  8 us
    pallas_call x1, Pallas kernels, local(): pl.pallas_call(place_inputs_kernel, grid=(steps,), in_specs=[pl.BlockSpec...  4.97 us
    pallas_call x1, Pallas kernels, local(): pl.pallas_call(weight_gradient_kernel, in_specs=[vmem, vmem, vmem, vmem],...  3.93 us
  transfers between devices with their start and end apart: 4, of which 3 were waited for; matrix products, arithmetic and copies ran while one was open for 0% of the time, Pallas kernels for 13%

profile of v10, /device:TPU:1, one launch (start us, length us, event | category | flops | bytes accessed | tf_op | source)
XLA Modules:
  0.0 161.6 jit_solution(11223758180464560810)
XLA Ops:
  7.2 0.0 all-gather.4.cloned.1.call-start
  7.2 0.7 all-gather.4.cloned.1.call-update
  7.9 2.3 %place_gradient.1 = (bf16[512,128]{1,0:T(8,128)(2,1)}, bf16[64,8,512]{2,1,0:T(8,128)(2,1)}) custom-call(s32[1,128]{1,0:T(1,128)} %bitcast.23, s32[1,64]{1,0:T(1,128)} %bitcast.24, bf16[128,1024]{1,0:T(8,128)(2,1)} %bitcast.21), custom_call_target="tpu_custom_call" | custom-call | tf_op jit(solution)/shard_map/place_gradient/pallas_call | solution.py:190
  10.2 11.6 %all-to-all-start = ((bf16[64,8,512]{2,1,0:T(8,128)(2,1)}), bf16[64,8,512]{2,1,0:T(8,128)(2,1)S(1)}, u32[]{:S(2)}, u32[]{:S(2)}) async-start(bf16[64,8,512]{2,1,0:T(8,128)(2,1)} %get-tuple-element.13), calls=%async_computation | async-start | bytes 1048576 | tf_op jit(solution)/shard_map/all_to_all | solution.py:160
  21.8 5.0 %place_inputs.1 = (bf16[64,8,2048]{2,1,0:T(8,128)(2,1)}, bf16[256,512]{1,0:T(8,128)(2,1)}) custom-call(bf16[512,128]{1,0:T(8,128)(2,1)} %get-tuple-element.11.placing_ref, bf16[128,4096]{1,0:T(8,128)(2,1)} %bitcast.15, bf16[128,4096]{1,0:T(8,128)(2,1)} %bitcast.16), custom_call_target="tpu_custom_call" | custom-call | tf_op jit(solution)/shard_map/place_inputs/pallas_call | solution.py:197
  26.8 12.8 %all-to-all-done.grad_ref.grads_ref = bf16[64,8,512]{2,1,0:T(8,128)(2,1)S(1)} async-done(((bf16[64,8,512]{2,1,0:T(8,128)(2,1)}), bf16[64,8,512]{2,1,0:T(8,128)(2,1)S(1)}, u32[]{:S(2)}, u32[]{:S(2)}) %all-to-all-start) | async-done | bytes 524320 | tf_op jit(solution)/shard_map/all_to_all | solution.py:160
  39.6 5.7 %all-to-all-start.2 = ((bf16[64,8,2048]{2,1,0:T(8,128)(2,1)}), bf16[64,8,2048]{2,1,0:T(8,128)(2,1)S(1)}, u32[]{:S(2)}, u32[]{:S(2)}) async-start(bf16[64,8,2048]{2,1,0:T(8,128)(2,1)} %get-tuple-element.15), calls=%async_computation.2 | async-start | bytes 4194304 | tf_op jit(solution)/shard_map/all_to_all | solution.py:160
  45.3 2.3 %coef.1 = (bf16[512,64]{1,0:T(8,128)(2,1)}, bf16[128,256]{1,0:T(8,128)(2,1)}) custom-call(bf16[64,8,512]{2,1,0:T(8,128)(2,1)S(1)} %all-to-all-done.grad_ref.grads_ref, bf16[64,1024]{1,0:T(8,128)(2,1)} %bitcast.22), custom_call_target="tpu_custom_call" | custom-call | tf_op jit(solution)/shard_map/coef/pallas_call | solution.py:213
  47.6 31.2 %all-gather = bf16[1024,256]{1,0:T(8,128)(2,1)} all-gather(bf16[128,256]{1,0:T(8,128)(2,1)} %get-tuple-element.14), channel_id=2, replica_groups=mesh['segment'=8,'owner'=64] {'segment'}, dimensions={0}, use_global_device_ids=true | all-gather | bytes 589824 | tf_op jit(solution)/shard_map/all_gather | solution.py:221
  78.8 0.0 all-gather.4.cloned.1.call-done.low_ref.high_ref
  78.8 8.0 %term.1 = bf16[64,8,2048]{2,1,0:T(8,128)(2,1)} custom-call(s32[1]{0:T(128)} %bitcast.4.place_ref, bf16[8,128,256]{2,1,0:T(8,128)(2,1)} %bitcast.19, bf16[512,4096]{1,0:T(8,128)(2,1)} %all-gather.4.cloned.1.call-done.low_ref.high_ref, bf16[512,4096]{1,0:T(8,128)(2,1)} %all-gather.4.cloned.1.call-done.low_ref.high_ref), custom_call_target="tpu_custom_call" | custom-call | tf_op jit(solution)/shard_map/term/pallas_call | solution.py:223
  86.8 8.2 %all-to-all-done.2.rows_ref = bf16[64,8,2048]{2,1,0:T(8,128)(2,1)S(1)} async-done(((bf16[64,8,2048]{2,1,0:T(8,128)(2,1)}), bf16[64,8,2048]{2,1,0:T(8,128)(2,1)S(1)}, u32[]{:S(2)}, u32[]{:S(2)}) %all-to-all-start.2) | async-done | bytes 2097184 | tf_op jit(solution)/shard_map/all_to_all | solution.py:160
  95.0 7.2 %all-to-all-start.1 = ((bf16[64,8,2048]{2,1,0:T(8,128)(2,1)}), bf16[64,8,2048]{2,1,0:T(8,128)(2,1)}, u32[]{:S(2)}, u32[]{:S(2)}) async-start(bf16[64,8,2048]{2,1,0:T(8,128)(2,1)} %term.1), calls=%async_computation.1 | async-start | bytes 4194304 | tf_op jit(solution)/shard_map/all_to_all | solution.py:160
  102.2 3.9 %weight_gradient.1 = (f32[64,4096]{1,0:T(8,128)}, f32[64,1024]{1,0:T(8,128)}) custom-call(bf16[64,8,2048]{2,1,0:T(8,128)(2,1)S(1)} %all-to-all-done.2.rows_ref, bf16[64,8,512]{2,1,0:T(8,128)(2,1)S(1)} %all-to-all-done.grad_ref.grads_ref, bf16[512,64]{1,0:T(8,128)(2,1)} %get-tuple-element.16.coef_ref, bf16[64,4096]{1,0:T(8,128)(2,1)} %bitcast.18), custom_call_target="tpu_custom_call" | custom-call | tf_op jit(solution)/shard_map/weight_gradient/pallas_call | solution.py:239
  106.1 45.7 %all-to-all-done.1.rows_ref = bf16[64,8,2048]{2,1,0:T(8,128)(2,1)} async-done(((bf16[64,8,2048]{2,1,0:T(8,128)(2,1)}), bf16[64,8,2048]{2,1,0:T(8,128)(2,1)}, u32[]{:S(2)}, u32[]{:S(2)}) %all-to-all-start.1) | async-done | bytes 2097184 | tf_op jit(solution)/shard_map/all_to_all | solution.py:160
  151.8 3.0 %unplace.1 = bf16[128,4096]{1,0:T(8,128)(2,1)} custom-call(bf16[256,512]{1,0:T(8,128)(2,1)} %get-tuple-element.12.back_ref, bf16[64,8,2048]{2,1,0:T(8,128)(2,1)} %all-to-all-done.1.rows_ref), custom_call_target="tpu_custom_call" | custom-call | tf_op jit(solution)/shard_map/unplace/pallas_call | solution.py:248
Async XLA Ops:
  7.2 71.6 %all-gather.4.cloned.1.call-start = ((), (), s32[]{:S(2)}) async-start(), calls=%async_computation.3 | async-start | bytes 4718592 | tf_op jit(solution)/shard_map/all_gather | solution.py:188
  10.2 29.3 %all-to-all-start = ((bf16[64,8,512]{2,1,0:T(8,128)(2,1)}), bf16[64,8,512]{2,1,0:T(8,128)(2,1)S(1)}, u32[]{:S(2)}, u32[]{:S(2)}) async-start(bf16[64,8,512]{2,1,0:T(8,128)(2,1)} %get-tuple-element.13), calls=%async_computation | async-start | bytes 1048576 | tf_op jit(solution)/shard_map/all_to_all | solution.py:160
  39.6 55.4 %all-to-all-start.2 = ((bf16[64,8,2048]{2,1,0:T(8,128)(2,1)}), bf16[64,8,2048]{2,1,0:T(8,128)(2,1)S(1)}, u32[]{:S(2)}, u32[]{:S(2)}) async-start(bf16[64,8,2048]{2,1,0:T(8,128)(2,1)} %get-tuple-element.15), calls=%async_computation.2 | async-start | bytes 4194304 | tf_op jit(solution)/shard_map/all_to_all | solution.py:160
  95.0 56.8 %all-to-all-start.1 = ((bf16[64,8,2048]{2,1,0:T(8,128)(2,1)}), bf16[64,8,2048]{2,1,0:T(8,128)(2,1)}, u32[]{:S(2)}, u32[]{:S(2)}) async-start(bf16[64,8,2048]{2,1,0:T(8,128)(2,1)} %term.1), calls=%async_computation.1 | async-start | bytes 4194304 | tf_op jit(solution)/shard_map/all_to_all | solution.py:160
Sparse Core Ops, SparseCore 0:
  10.1 67.5 all-gather.3
